TPU v7x, 32 devices: a whole 2x2x4 slice. The times are simulated.
32 devices in a mesh: dp: 4 (over z), ctx: 8 (over y, x, core).
Axes of the slice: x: 2, y: 2, z: 4, core: 2. Of those that a mesh axis runs over, the one named last changes fastest.
Arguments:
- tokens: float32 [16, 2048, 768], P('dp', 'ctx'), may hold values from -6 to 6
- cotangent: float32 [16, 2048, 768], P('dp', 'ctx'), may hold values from -6 to 6
- lengths: int32 [16], replicated, may hold values from 1024 to 2048, as said below
- w_query: bfloat16 [768, 768], P(('dp', 'ctx')), may hold values from -0.21875 to 0.21875
- w_key: bfloat16 [768, 768], P(('dp', 'ctx')), may hold values from -0.21875 to 0.21875
- w_value: bfloat16 [768, 768], P(('dp', 'ctx')), may hold values from -0.21875 to 0.21875
- w_attn_out: bfloat16 [768, 768], P(('dp', 'ctx')), may hold values from -6 to 6
- w_up: bfloat16 [768, 3072], P(('dp', 'ctx')), may hold values from -0.21875 to 0.21875
- b_up: bfloat16 [3072], P(('dp', 'ctx')), may hold values from -4 to 4
- w_down: bfloat16 [3072, 768], P(('dp', 'ctx')), may hold values from -0.109375 to 0.109375
- vectors: bfloat16 [8, 768], P(None, ('dp', 'ctx')), may hold values from -0.6 to 1.4
Outputs:
- output: float32 [16, 2048, 768], P('dp', 'ctx')
- d_tokens: float32 [16, 2048, 768], P('dp', 'ctx')
- d_w_query: float32 [768, 768], P(('dp', 'ctx'))
- d_w_key: float32 [768, 768], P(('dp', 'ctx'))
- d_w_value: float32 [768, 768], P(('dp', 'ctx'))
- d_w_attn_out: float32 [768, 768], P(('dp', 'ctx'))
- d_w_up: float32 [768, 3072], P(('dp', 'ctx'))
- d_b_up: float32 [3072], P(('dp', 'ctx'))
- d_w_down: float32 [3072, 768], P(('dp', 'ctx'))
- d_vectors: float32 [8, 768], P(None, ('dp', 'ctx'))
Inputs may be any that keep to these rules, and one draw needn't show every extreme that they name: `lengths`: each sequence fills 2048 / 2 to 2048 of its 2048 slots; among the 4 sequences of every index of dp one has length 2048.
All inputs are finite; a program needn't handle non-finite values.
Results may differ from a plain program's by a relative error of at most 0.018.
The roundings to bfloat16 on the way count: a program that leaves them out, or rounds other values in their place, can miss the bound.
Values may be sent and summed in bfloat16 or wider, within the bound.
A program may use at most 320 MiB of HBM per device.

v0:
```python
import jax
import jax.numpy as jnp
from jax import lax
from jax.sharding import PartitionSpec as P

HEADS = 12
HEAD_DIM = 64


epsilon = 1e-12
floor_score = -1e30


def stored_position(row_ids, rows_dev, ctx_count):
    device = row_ids // rows_dev
    offset = row_ids % rows_dev
    half_rows = rows_dev // 2
    return jnp.where(
        offset < half_rows,
        device * half_rows + offset,
        (2 * ctx_count - 1 - device) * half_rows + offset - half_rows,
    )


def normalize(hidden, scale_row, shift_row):
    centred = hidden - jnp.mean(hidden, axis=-1, keepdims=True)
    inverse = lax.rsqrt(jnp.mean(centred * centred, axis=-1, keepdims=True) + epsilon)
    standard = centred * inverse
    return (standard * scale_row + shift_row, standard, inverse)


def normalize_back(gradient, standard, inverse, scale_row):
    scaled = gradient * scale_row
    centred = scaled - jnp.mean(scaled, axis=-1, keepdims=True)
    return (centred - standard * jnp.mean(scaled * standard, axis=-1, keepdims=True)) * inverse


def blockwise(update, carried, portion, block_rows, along):
    total_rows = portion.shape[along]

    def inner_step(block_index, running):
        sliced = lax.dynamic_slice_in_dim(portion, block_index * block_rows, block_rows, along)
        return update(running, sliced, block_index * block_rows)

    return lax.fori_loop(0, total_rows // block_rows, inner_step, carried)


def matmul(left_side, right_side):
    return jnp.dot(left_side, right_side, preferred_element_type=jnp.float32)


def matmul_left(left_side, right_side):
    return lax.dot_general(
        left_side, right_side, (((0,), (0,)), ((), ())), preferred_element_type=jnp.float32
    )


def matmul_right(left_side, right_side):
    return lax.dot_general(
        left_side, right_side, (((1,), (1,)), ((), ())), preferred_element_type=jnp.float32
    )


def on_device(
    tokens, cotangent, lengths, w_query, w_key, w_value, w_attn_out, w_up, b_up, w_down, vectors
):
    seq_count, rows_dev, model_width = tokens.shape
    row_count = seq_count * rows_dev
    ctx_count = lax.axis_size("ctx")
    data_count = lax.axis_size("dp")
    data_index = lax.axis_index("dp")
    ctx_index = lax.axis_index("ctx")
    head_count = HEADS
    head_size = HEAD_DIM
    factor = head_size ** (-0.5)
    seq_slots = jnp.arange(seq_count, dtype=jnp.int32)
    per_group = seq_count // data_count
    grouped = lengths.reshape(data_count, seq_count)
    sort_keys = grouped * seq_count + seq_slots[None, :]
    ranking = jnp.sum(sort_keys[:, None, :] < sort_keys[:, :, None], axis=2)
    own_rank = lax.dynamic_index_in_dim(ranking, data_index, 0, keepdims=False)
    destination = (
        data_index + own_rank // per_group
    ) % data_count * per_group + own_rank % per_group
    sender_order = jnp.sum(
        jnp.where(destination[None, :] == seq_slots[:, None], seq_slots[None, :], 0), axis=1
    )
    arrived = (
        lax.all_to_all(
            jnp.take(tokens, sender_order, axis=0), "dp", split_axis=0, concat_axis=0, tiled=True
        ),
        lax.all_to_all(
            jnp.take(cotangent, sender_order, axis=0), "dp", split_axis=0, concat_axis=0, tiled=True
        ),
    )
    residual = arrived[0]
    upstream = arrived[1]
    anchor = seq_slots // per_group
    wanted = (data_index - anchor) % data_count * per_group + seq_slots % per_group
    seq_len = jnp.sum(
        jnp.where(
            jnp.take(ranking, anchor, axis=0) == wanted[:, None],
            jnp.take(grouped, anchor, axis=0),
            0,
        ),
        axis=1,
    )
    gathered = (
        lax.all_gather(w_query, ("dp", "ctx"), axis=0, tiled=True),
        lax.all_gather(w_key, ("dp", "ctx"), axis=0, tiled=True),
        lax.all_gather(w_value, ("dp", "ctx"), axis=0, tiled=True),
        lax.all_gather(w_attn_out, ("dp", "ctx"), axis=0, tiled=True),
        lax.all_gather(w_up, ("dp", "ctx"), axis=0, tiled=True),
        lax.all_gather(b_up, ("dp", "ctx"), axis=0, tiled=True),
        lax.all_gather(w_down, ("dp", "ctx"), axis=0, tiled=True),
        lax.all_gather(vectors, ("dp", "ctx"), axis=1, tiled=True),
    )
    full_query, full_key, full_value, full_attn, full_up, full_bias_up, full_down, full_vectors = (
        gathered
    )
    vector_rows = full_vectors.astype(jnp.float32)

    def key_counted(first_row, span_rows):
        positions = stored_position(
            first_row + jnp.arange(span_rows, dtype=jnp.int32), rows_dev, ctx_count
        )
        return (positions[None, :] < seq_len[:, None])[:, None, None, :]

    flat_in = residual.reshape(row_count, model_width)
    low_in = flat_in.astype(jnp.bfloat16)
    queries = (matmul(low_in, full_query) + vector_rows[0]).astype(jnp.bfloat16)
    key_rows = matmul(low_in, full_key)
    value_rows = matmul(low_in, full_value) + vector_rows[1]
    keys_values = (
        jnp.stack([key_rows, value_rows])
        .astype(jnp.bfloat16)
        .reshape(2, seq_count, rows_dev, model_width)
    )
    query_heads = queries.reshape(seq_count, rows_dev, head_count, head_size)

    def attend_block(running, portion, first_row):
        running_max, running_sum, summed = running
        span_rows = portion.shape[2]
        key_heads = portion[0].reshape(seq_count, span_rows, head_count, head_size)
        value_heads = portion[1].reshape(seq_count, span_rows, head_count, head_size)
        counted = key_counted(first_row, span_rows)
        scores = (
            jnp.einsum(
                "sqhd,skhd->shqk", query_heads, key_heads, preferred_element_type=jnp.float32
            )
            * factor
        )
        scores = jnp.where(counted, scores, floor_score)
        newest = jnp.maximum(running_max, jnp.max(scores, axis=-1))
        weights = jnp.where(counted, jnp.exp(scores - newest[..., None]), 0.0)
        rescale = jnp.exp(running_max - newest)
        running_sum = running_sum * rescale + jnp.sum(weights, axis=-1)
        added = jnp.einsum(
            "shqk,skhd->sqhd",
            weights.astype(jnp.bfloat16),
            value_heads,
            preferred_element_type=jnp.float32,
        )
        summed = summed * jnp.transpose(rescale, (0, 2, 1))[..., None] + added
        return (newest, running_sum, summed)

    start_state = (
        jnp.full((seq_count, head_count, rows_dev), floor_score, jnp.float32),
        jnp.zeros((seq_count, head_count, rows_dev), jnp.float32),
        jnp.zeros((seq_count, rows_dev, head_count, head_size), jnp.float32),
    )
    running_max, running_sum, summed = blockwise(
        attend_block,
        start_state,
        lax.all_gather(keys_values, "ctx", axis=2, tiled=True),
        rows_dev,
        2,
    )
    mixed_heads = summed / jnp.transpose(running_sum, (0, 2, 1))[..., None]
    log_total = running_max + jnp.log(running_sum)
    low_mixed = mixed_heads.reshape(row_count, model_width).astype(jnp.bfloat16)
    attention = matmul(low_mixed, full_attn) + vector_rows[2]
    normed_one, standard_one, inverse_one = normalize(
        flat_in + attention, vector_rows[6], vector_rows[4]
    )
    low_first = normed_one.astype(jnp.bfloat16)
    inner = matmul(low_first, full_up) + full_bias_up.astype(jnp.float32)
    active = jax.nn.gelu(inner, approximate=False).astype(jnp.bfloat16)
    branch = matmul(active, full_down) + vector_rows[3]
    result, standard_two, inverse_two = normalize(
        normed_one + branch, vector_rows[7], vector_rows[5]
    )
    result = result.reshape(seq_count, rows_dev, model_width)
    output = jnp.take(
        lax.all_to_all(result, "dp", split_axis=0, concat_axis=0, tiled=True), destination, axis=0
    )
    back_set = (
        lax.all_gather(w_query, ("dp", "ctx"), axis=0, tiled=True),
        lax.all_gather(w_key, ("dp", "ctx"), axis=0, tiled=True),
        lax.all_gather(w_value, ("dp", "ctx"), axis=0, tiled=True),
        lax.all_gather(w_attn_out, ("dp", "ctx"), axis=0, tiled=True),
        lax.all_gather(w_up, ("dp", "ctx"), axis=0, tiled=True),
        lax.all_gather(b_up, ("dp", "ctx"), axis=0, tiled=True),
        lax.all_gather(w_down, ("dp", "ctx"), axis=0, tiled=True),
        lax.all_gather(vectors, ("dp", "ctx"), axis=1, tiled=True),
    )
    full_query, full_key, full_value, full_attn, full_up, full_bias_up, full_down, full_vectors = (
        back_set
    )
    vector_rows = full_vectors.astype(jnp.float32)
    upstream_flat = upstream.reshape(row_count, model_width)
    d_gain_two = jnp.sum(upstream_flat * standard_two, axis=0)
    d_shift_two = jnp.sum(upstream_flat, axis=0)
    grad_second = normalize_back(upstream_flat, standard_two, inverse_two, vector_rows[7])
    low_branch = grad_second.astype(jnp.bfloat16)
    d_bias_down = jnp.sum(low_branch.astype(jnp.float32), axis=0)
    d_down = matmul_left(active, low_branch)
    d_active = matmul_right(low_branch, full_down)
    gelu_back = jax.vjp(lambda values_in: jax.nn.gelu(values_in, approximate=False), inner)[1]
    low_inner = gelu_back(d_active)[0].astype(jnp.bfloat16)
    d_bias_up = jnp.sum(low_inner.astype(jnp.float32), axis=0)
    d_up = matmul_left(low_first, low_inner)
    ffn_grads = (
        lax.psum_scatter(d_up, ("dp", "ctx"), scatter_dimension=0, tiled=True),
        lax.psum_scatter(d_bias_up, ("dp", "ctx"), scatter_dimension=0, tiled=True),
        lax.psum_scatter(d_down, ("dp", "ctx"), scatter_dimension=0, tiled=True),
    )
    grad_first = grad_second + matmul_right(low_inner, full_up)
    d_gain_one = jnp.sum(grad_first * standard_one, axis=0)
    d_shift_one = jnp.sum(grad_first, axis=0)
    grad_sum = normalize_back(grad_first, standard_one, inverse_one, vector_rows[6])
    low_attn = grad_sum.astype(jnp.bfloat16)
    d_bias_attn = jnp.sum(low_attn.astype(jnp.float32), axis=0)
    d_attn = matmul_left(low_mixed, low_attn)
    d_mixed = matmul_right(low_attn, full_attn).astype(jnp.bfloat16)
    grad_heads = d_mixed.reshape(seq_count, rows_dev, head_count, head_size)
    row_delta = jnp.einsum("sqhd,sqhd->shq", grad_heads.astype(jnp.float32), mixed_heads)
    full_lse, full_delta = (
        lax.all_gather(log_total, "ctx", axis=2, tiled=True),
        lax.all_gather(row_delta, "ctx", axis=2, tiled=True),
    )

    def query_block(running, portion, first_row):
        span_rows = portion.shape[2]
        key_heads = portion[0].reshape(seq_count, span_rows, head_count, head_size)
        value_heads = portion[1].reshape(seq_count, span_rows, head_count, head_size)
        counted = key_counted(first_row, span_rows)
        scores = (
            jnp.einsum(
                "sqhd,skhd->shqk", query_heads, key_heads, preferred_element_type=jnp.float32
            )
            * factor
        )
        scores = jnp.where(counted, scores, floor_score)
        weights = jnp.exp(scores - log_total[..., None])
        dprobs = jnp.einsum(
            "sqhd,skhd->shqk", grad_heads, value_heads, preferred_element_type=jnp.float32
        )
        dscores = (weights * (dprobs - row_delta[..., None])).astype(jnp.bfloat16)
        return (
            running
            + jnp.einsum("shqk,skhd->sqhd", dscores, key_heads, preferred_element_type=jnp.float32)
            * factor
        )

    dq_total = blockwise(
        query_block,
        jnp.zeros((seq_count, rows_dev, head_count, head_size), jnp.float32),
        lax.all_gather(keys_values, "ctx", axis=2, tiled=True),
        rows_dev,
        2,
    )
    local_keys = keys_values[0].reshape(seq_count, rows_dev, head_count, head_size)
    local_values = keys_values[1].reshape(seq_count, rows_dev, head_count, head_size)
    local_counted = key_counted(ctx_index * rows_dev, rows_dev)
    query_grads = jnp.stack(
        [
            queries.reshape(seq_count, rows_dev, model_width),
            d_mixed.reshape(seq_count, rows_dev, model_width),
        ]
    )

    def key_block(running, portion, first_row):
        span_rows = portion.shape[2]
        piece_queries = portion[0].reshape(seq_count, span_rows, head_count, head_size)
        piece_grads = portion[1].reshape(seq_count, span_rows, head_count, head_size)
        lse_part = lax.dynamic_slice_in_dim(full_lse, first_row, span_rows, 2)
        delta_part = lax.dynamic_slice_in_dim(full_delta, first_row, span_rows, 2)
        scores = (
            jnp.einsum(
                "sqhd,skhd->shqk", piece_queries, local_keys, preferred_element_type=jnp.float32
            )
            * factor
        )
        scores = jnp.where(local_counted, scores, floor_score)
        weights = jnp.exp(scores - lse_part[..., None])
        dprobs = jnp.einsum(
            "sqhd,skhd->shqk", piece_grads, local_values, preferred_element_type=jnp.float32
        )
        dscores = (weights * (dprobs - delta_part[..., None])).astype(jnp.bfloat16)
        d_keys = (
            running[0]
            + jnp.einsum(
                "shqk,sqhd->skhd", dscores, piece_queries, preferred_element_type=jnp.float32
            )
            * factor
        )
        d_values = running[1] + jnp.einsum(
            "shqk,sqhd->skhd",
            weights.astype(jnp.bfloat16),
            piece_grads,
            preferred_element_type=jnp.float32,
        )
        return jnp.stack([d_keys, d_values])

    dkv_total = blockwise(
        key_block,
        jnp.zeros((2, seq_count, rows_dev, head_count, head_size), jnp.float32),
        lax.all_gather(query_grads, "ctx", axis=2, tiled=True),
        rows_dev,
        2,
    )
    d_query_rows = dq_total.reshape(row_count, model_width).astype(jnp.bfloat16)
    d_key_rows = dkv_total[0].reshape(row_count, model_width).astype(jnp.bfloat16)
    d_value_rows = dkv_total[1].reshape(row_count, model_width).astype(jnp.bfloat16)
    d_bias_query = jnp.sum(d_query_rows.astype(jnp.float32), axis=0)
    d_bias_value = jnp.sum(d_value_rows.astype(jnp.float32), axis=0)
    d_wquery = matmul_left(low_in, d_query_rows)
    d_wkey = matmul_left(low_in, d_key_rows)
    d_wvalue = matmul_left(low_in, d_value_rows)
    grad_in = (
        grad_sum
        + matmul_right(d_query_rows, full_query)
        + matmul_right(d_key_rows, full_key)
        + matmul_right(d_value_rows, full_value)
    )
    d_vector_rows = jnp.stack(
        [
            d_bias_query,
            d_bias_value,
            d_bias_attn,
            d_bias_down,
            d_shift_one,
            d_shift_two,
            d_gain_one,
            d_gain_two,
        ]
    )
    attn_grads = (
        lax.psum_scatter(d_wquery, ("dp", "ctx"), scatter_dimension=0, tiled=True),
        lax.psum_scatter(d_wkey, ("dp", "ctx"), scatter_dimension=0, tiled=True),
        lax.psum_scatter(d_wvalue, ("dp", "ctx"), scatter_dimension=0, tiled=True),
        lax.psum_scatter(d_attn, ("dp", "ctx"), scatter_dimension=0, tiled=True),
        lax.psum_scatter(d_vector_rows, ("dp", "ctx"), scatter_dimension=1, tiled=True),
    )
    grad_tokens = grad_in.reshape(seq_count, rows_dev, model_width)
    grad_tokens = jnp.take(
        lax.all_to_all(grad_tokens, "dp", split_axis=0, concat_axis=0, tiled=True),
        destination,
        axis=0,
    )
    return (
        output,
        grad_tokens,
        attn_grads[0],
        attn_grads[1],
        attn_grads[2],
        attn_grads[3],
        ffn_grads[0],
        ffn_grads[1],
        ffn_grads[2],
        attn_grads[4],
    )


def solution(mesh):
    in_specs = (
        P("dp", "ctx", None),
        P("dp", "ctx", None),
        P(),
        P(("dp", "ctx"), None),
        P(("dp", "ctx"), None),
        P(("dp", "ctx"), None),
        P(("dp", "ctx"), None),
        P(("dp", "ctx"), None),
        P(("dp", "ctx")),
        P(("dp", "ctx"), None),
        P(None, ("dp", "ctx")),
    )
    out_specs = (
        P("dp", "ctx", None),
        P("dp", "ctx", None),
        P(("dp", "ctx"), None),
        P(("dp", "ctx"), None),
        P(("dp", "ctx"), None),
        P(("dp", "ctx"), None),
        P(("dp", "ctx"), None),
        P(("dp", "ctx")),
        P(("dp", "ctx"), None),
        P(None, ("dp", "ctx")),
    )
    return jax.shard_map(
        on_device, mesh=mesh, in_specs=in_specs, out_specs=out_specs, check_vma=False
    )
```

profile of v0, /device:TPU:1, one launch (start us, length us, event | category | flops | bytes accessed | tf_op | source)
XLA Modules:
  0.0 1645.1 jit_solution(7793926144034642270)
XLA Ops:
  28.5 86.9 %all-gather = bf16[32,24,8]{1,2,0:T(8,128)(2,1)S(1)} all-gather(bf16[1,24,8]{1,2,0:T(8,128)(2,1)S(1)} %bitcast.258), channel_id=1, replica_groups=mesh['dp'=4,'ctx'=8] {'dp','ctx'}, dimensions={0}, use_global_device_ids=true | all-gather | bytes 12672 | tf_op jit(solution)/shard_map/all_gather | solution.py:116
  123.9 39.8 %all-gather.10.cloned.1.call-done = bf16[768,768]{1,0:T(8,128)(2,1)} async-done(((bf16[24,768]{1,0:T(8,128)(2,1)}), bf16[768,768]{1,0:T(8,128)(2,1)}) %all-gather.10.cloned.1.call-update) | async-done | bytes 1179664 | tf_op jit(solution)/shard_map/all_gather | solution.py:110
  181.0 93.1 %all-reduce = bf16[3072]{0:T(1024)(128)(2,1)S(1)} all-reduce(bf16[3072]{0:T(1024)(128)(2,1)S(1)} %dynamic-update-slice), channel_id=1, replica_groups=mesh['dp'=4,'ctx'=8] {'dp','ctx'}, use_global_device_ids=true, to_apply=%add | all-reduce | flops 3072 | bytes 12288
  287.0 101.6 %all-gather.14.cloned.1.call-done = bf16[2,4,2048,768]{2,3,1,0:T(8,128)(2,1)} async-done(((bf16[2,4,256,768]{2,3,1,0:T(8,128)(2,1)}), bf16[2,4,2048,768]{2,3,1,0:T(8,128)(2,1)}) %all-gather.14.cloned.1.call-update) | async-done | bytes 25165840 | tf_op jit(solution)/shard_map/all_gather | solution.py:175
  388.6 198.9 %while.51 = (s32[]{:T(128)}, f32[4,12,256]{2,1,0:T(8,128)S(1)}, f32[4,12,256]{2,1,0:T(8,128)S(1)}, f32[4,256,12,64]{1,3,2,0:T(8,128)}, s32[4]{0:T(128)S(1)}, /*i...) while((s32[]{:T(128)}, f32[4,12,256]{2,1,0:T(8,128)S(1)}, ...), condition=%wide.region_6.9_spmd.clone, body=%wide.region_3.8_spmd.clone.sunk | while | flops 848642048 | bytes 93591832 | solution.py:45
  422.1 10.9 bitcast_add_fusion.7
  447.0 10.9 bitcast_add_fusion.7
  471.9 11.1 bitcast_add_fusion.7
  496.9 11.0 bitcast_add_fusion.7
  521.9 11.0 bitcast_add_fusion.7
  546.9 10.9 bitcast_add_fusion.7
  571.9 11.1 bitcast_add_fusion.7
  598.1 36.3 %multiply_convert_fusion.8 = (bf16[1024,3072]{1,0:T(8,128)(2,1)}, f32[1024,3072]{1,0:T(8,128)}, f32[1024,3072]{1,0:T(8,128)}) fusion(f32[3072]{0:T(1024)S(1)} %convert_element_type.131, bf16[768,3072]{1,0:T(8,128)(2,1)} %all-gather.20.cloned.1.call-done, f32[1024,768]{1,0:T(8,128)S(1)} %get-tuple-element.823, f32[768]{0:T(1024)S(1)} %get-tuple-element.736, ...), kind=kOutput, calls=%fused_computation.81 | convolution fusion | flops 5043388416 | bytes 39348224 | tf_op jit(solution)/shard_map/dot_general | solution.py:49
  653.2 19.3 %convert_reduce_fusion = (f32[3072]{0:T(1024)}, bf16[1024,3072]{1,0:T(8,128)(2,1)}) fusion(f32[1024,3072]{1,0:T(8,128)} %get-tuple-element.804, bf16[3072,768]{1,0:T(8,128)(2,1)} %all-gather.22.cloned.1.call-done, f32[1024,768]{1,0:T(8,128)} %get-tuple-element.794, f32[1024,3072]{1,0:T(8,128)} %get-tuple-element.824, f32[3072]{0:T(1024)S(1)} %convert_element_type.131), kind=kOutput, calls=%fused_computation.79 | convolution fusion | flops 4886098944 | bytes 39346176 | tf_op jit(solution)/shard_map/dot_general | solution.py:59
  702.4 162.1 %while.52 = (s32[]{:T(128)}, f32[4,256,12,64]{1,3,2,0:T(8,128)}, bf16[2,4,2048,768]{2,3,1,0:T(8,128)(2,1)}, s32[4]{0:T(128)S(1)}, bf16[4,256,12,64]{1,3,2,0:T(8,...) while((s32[]{:T(128)}, f32[4,256,12,64]{1,3,2,0:T(8,128)}, ...), condition=%wide.region_16.19_spmd.clone, body=%wide.region_15.18_spmd.clone.sunk | while | flops 1229201408 | bytes 45715676 | solution.py:45
  752.2 11.0 bitcast_add_fusion.8
  812.7 11.9 bitcast_add_fusion.8
  903.9 11.1 all_gather.55
  915.0 11.3 all_gather.54
  944.8 248.0 %while.50 = (s32[]{:T(128)}, f32[2,4,256,12,64]{2,4,3,1,0:T(8,128)}, bf16[2,4,2048,768]{2,3,1,0:T(8,128)(2,1)}, bf16[4,256,12,64]{1,3,2,0:T(8,128)(2,1)}, f32[4,...) while((s32[]{:T(128)}, ...), condition=%wide.region_18.21_spmd.clone, body=%wide.region_17.20_spmd.clone.sunk | while | flops 1646003200 | bytes 104157488 | solution.py:45
  1227.3 93.6 %all-reduce.3 = (f32[3072]{0:T(1024)S(1)}, f32[8,768]{1,0:T(8,128)S(1)}) all-reduce(f32[3072]{0:T(1024)S(1)} %copy-done.48, f32[8,768]{1,0:T(8,128)S(1)} %stack.75), channel_id=7, replica_groups=mesh['dp'=4,'ctx'=8] {'dp','ctx'}, use_global_device_ids=true, to_apply=%region_25.28.clone | all-reduce | flops 9216 | bytes 73728
  1331.3 98.4 %reduce-scatter.18.cloned.1.call-done = f32[96,768]{1,0:T(8,128)} async-done(((f32[3072,768]{1,0:T(8,128)}), f32[96,768]{1,0:T(8,128)}) %reduce-scatter.18.cloned.1.call-update) | async-done | bytes 294928 | tf_op jit(solution)/shard_map/reduce_scatter | solution.py:226
  1429.7 104.1 %reduce-scatter.12.cloned.1.call-done = f32[24,768]{1,0:T(8,128)} async-done(((f32[768,768]{1,0:T(8,128)}), f32[24,768]{1,0:T(8,128)}) %reduce-scatter.12.cloned.1.call-update) | async-done | bytes 73744 | tf_op jit(solution)/shard_map/reduce_scatter | solution.py:352
  1533.9 104.5 %reduce-scatter.10.cloned.1.call-done = f32[24,768]{1,0:T(8,128)} async-done(((f32[768,768]{1,0:T(8,128)}), f32[24,768]{1,0:T(8,128)}) %reduce-scatter.10.cloned.1.call-update) | async-done | bytes 73744 | tf_op jit(solution)/shard_map/reduce_scatter | solution.py:351
  (525 shorter events, 729.0 us)
Async XLA Ops:
  7.2 111.4 %all-gather.12.cloned.1.call-start = ((), (), s32[]{:S(2)}) async-start(), calls=%async_computation.11 | async-start | bytes 1216512 | tf_op jit(solution)/shard_map/all_gather | solution.py:111
  9.1 170.5 %copy-start.34 = (s32[4,4]{1,0:T(4,128)}, s32[4,4]{1,0:T(4,128)S(1)}, u32[]{:S(2)}) copy-start(s32[4,4]{1,0:T(4,128)S(1)} %convert_reduce_fusion.5) | copy-start | bytes 196
  21.5 95.0 %all-to-all-start = ((f32[4,256,768]{2,1,0:T(8,128)}), f32[4,256,768]{2,1,0:T(8,128)S(1)}, u32[]{:S(2)}, u32[]{:S(2)}) async-start(f32[4,256,768]{2,1,0:T(8,128)} %get-tuple-element.821), calls=%async_computation | async-start | bytes 6291456 | tf_op jit(solution)/shard_map/all_to_all | solution.py:89
  27.0 136.6 %all-gather.10.cloned.1.call-start = ((), (), s32[]{:S(2)}) async-start(), calls=%async_computation.10 | async-start | bytes 1216512 | tf_op jit(solution)/shard_map/all_gather | solution.py:110
  27.8 246.6 %all-gather.16.cloned.1.call-start = ((), (), s32[]{:S(2)}) async-start(), calls=%async_computation.13 | async-start | bytes 1216512 | tf_op jit(solution)/shard_map/all_gather | solution.py:109
  28.5 360.2 %all-gather.14.cloned.1.call-start = ((), (), s32[]{:S(2)}) async-start(), calls=%async_computation.12 | async-start | bytes 28311552 | tf_op jit(solution)/shard_map/all_gather | solution.py:175
  116.4 165.5 %copy-start.37 = (f32[768]{0:T(1024)}, f32[768]{0:T(1024)S(1)}, u32[]{:S(2)}) copy-start(f32[768]{0:T(1024)S(1)} %get-tuple-element.733) | copy-start | bytes 9220
  116.4 518.0 %copy-start.39 = (f32[768]{0:T(1024)}, f32[768]{0:T(1024)S(1)}, u32[]{:S(2)}) copy-start(f32[768]{0:T(1024)S(1)} %get-tuple-element.736) | copy-start | bytes 9220
  172.8 420.5 %all-gather.18.cloned.1.call-start = ((), (), s32[]{:S(2)}) async-start(), calls=%async_computation.14 | async-start | bytes 1216512 | tf_op jit(solution)/shard_map/all_gather | solution.py:112
  173.4 424.7 %all-gather.20.cloned.1.call-start = ((), (), s32[]{:S(2)}) async-start(), calls=%async_computation.15 | async-start | bytes 4866048 | tf_op jit(solution)/shard_map/all_gather | solution.py:113
  173.9 100.4 %copy-start.32 = (bf16[1024,768]{1,0:T(8,128)(2,1)S(1)}, bf16[1024,768]{1,0:T(8,128)(2,1)}, u32[]{:S(2)}) copy-start(bf16[1024,768]{1,0:T(8,128)(2,1)} %get-tuple-element.817) | copy-start | bytes 4718596
  174.0 108.0 %all-to-all-start.2 = ((f32[4,256,768]{2,1,0:T(8,128)}), f32[4,256,768]{2,1,0:T(8,128)}, u32[]{:S(2)}, u32[]{:S(2)}) async-start(f32[4,256,768]{2,1,0:T(8,128)} %get-tuple-element.820), calls=%async_computation.2 | async-start | bytes 6291456 | tf_op jit(solution)/shard_map/all_to_all | solution.py:92
  178.8 455.7 %all-gather.22.cloned.1.call-start = ((), (), s32[]{:S(2)}) async-start(), calls=%async_computation.16 | async-start | bytes 4866048 | tf_op jit(solution)/shard_map/all_gather | solution.py:115
  179.5 761.8 %all-gather.24.cloned.1.call-start = ((), (), s32[]{:S(2)}) async-start(), calls=%async_computation.17 | async-start | bytes 28311552 | tf_op jit(solution)/shard_map/all_gather | solution.py:319
  597.6 85.4 %copy-start.7 = (f32[1024,768]{1,0:T(8,128)}, f32[1024,768]{1,0:T(8,128)S(1)}, u32[]{:S(2)}) copy-start(f32[1024,768]{1,0:T(8,128)S(1)} %get-tuple-element.823) | copy-start | bytes 9437188
  691.6 639.7 %reduce-scatter.8.cloned.1.call-start = ((), (), s32[]{:S(2)}) async-start(), calls=%async_computation.18 | async-start | bytes 2433024 | tf_op jit(solution)/shard_map/reduce_scatter | solution.py:350
  871.8 459.5 %reduce-scatter.14.cloned.1.call-start = ((), (), s32[]{:S(2)}) async-start(), calls=%async_computation.21 | async-start | bytes 2433024 | tf_op jit(solution)/shard_map/reduce_scatter | solution.py:353
  877.2 454.1 %reduce-scatter.16.cloned.1.call-start = ((), (), s32[]{:S(2)}) async-start(), calls=%async_computation.22 | async-start | bytes 9732096 | tf_op jit(solution)/shard_map/reduce_scatter | solution.py:224
  899.0 313.1 %all-to-all-start.1 = ((f32[4,256,768]{2,1,0:T(8,128)}), f32[4,256,768]{2,1,0:T(8,128)}, u32[]{:S(2)}, u32[]{:S(2)}) async-start(f32[4,256,768]{2,1,0:T(8,128)} %bitcast.11), calls=%async_computation.1 | async-start | bytes 6291456 | tf_op jit(solution)/shard_map/all_to_all | solution.py:195
  903.9 525.9 %reduce-scatter.18.cloned.1.call-start = ((), (), s32[]{:S(2)}) async-start(), calls=%async_computation.23 | async-start | bytes 9732096 | tf_op jit(solution)/shard_map/reduce_scatter | solution.py:226
  936.5 597.3 %reduce-scatter.12.cloned.1.call-start = ((), (), s32[]{:S(2)}) async-start(), calls=%async_computation.20 | async-start | bytes 2433024 | tf_op jit(solution)/shard_map/reduce_scatter | solution.py:352
  1212.1 110.1 %all-to-all-start.3 = ((f32[4,256,768]{2,1,0:T(8,128)}), f32[4,256,768]{2,1,0:T(8,128)S(1)}, u32[]{:S(2)}, u32[]{:S(2)}) async-start(f32[4,256,768]{2,1,0:T(8,128)} %bitcast.234), calls=%async_computation.3 | async-start | bytes 6291456 | tf_op jit(solution)/shard_map/all_to_all | solution.py:358
  1217.0 421.3 %reduce-scatter.10.cloned.1.call-start = ((), (), s32[]{:S(2)}) async-start(), calls=%async_computation.19 | async-start | bytes 2433024 | tf_op jit(solution)/shard_map/reduce_scatter | solution.py:351
  1324.6 313.8 %copy-start.1 = (f32[4,256,768]{2,1,0:T(8,128)S(1)}, f32[4,256,768]{2,1,0:T(8,128)}, u32[]{:S(2)}) copy-start(f32[4,256,768]{2,1,0:T(8,128)} %param.22) | copy-start | bytes 9437188
  (95 other events, 675.8 us)
Sparse Core Ops, SparseCore 0:
  10.9 96.2 all-gather.11
  110.1 53.4 all-gather.9
  166.5 91.6 all-gather.15
  260.0 128.6 all-gather.13
  391.4 53.9 all-gather.17
  448.2 62.5 all-gather.19
  513.7 62.4 all-gather.21
  691.7 130.3 all-gather.23
  871.9 131.0 reduce-scatter.7
  1009.5 97.9 reduce-scatter.13
  1114.1 176.4 reduce-scatter.15
  1297.9 131.7 reduce-scatter.17
  1435.6 98.2 reduce-scatter.11
  1540.4 97.8 reduce-scatter.9
where the time goes:
time: 1650 us
  matrix products  602 us (36%)
  waiting for transfers between devices  452 us (27%)
  blocking collectives  296 us (18%)
  local copies, waits for them, and re-layouts  148 us (9%)
  other arithmetic  110 us (7%)
  starting transfers between devices  20.7 us (1%)
    unnamed x2, blocking collectives  187 us
    reduce_scatter x1, waiting for transfers between devices, on_device(): lax.psum_scatter(d_wkey, ('dp', 'ctx'), scatter_dimension=0, tiled=True)  104 us
    reduce_scatter x1, waiting for transfers between devices, on_device(): lax.psum_scatter(d_wvalue, ('dp', 'ctx'), scatter_dimension=0, tiled=True)  104 us
    all_gather x1, waiting for transfers between devices, on_device(): lax.all_gather(keys_values, 'ctx', axis=2, tiled=True)  102 us
    reduce_scatter x1, waiting for transfers between devices, on_device(): lax.psum_scatter(d_down, ('dp', 'ctx'), scatter_dimension=0, tiled=True)  98.4 us
    dot_general x8, matrix products, attend_block(): jnp.einsum('shqk,skhd->sqhd', weights.astype(jnp.bfloat16), value_heads,...  87 us
    all_gather x1, blocking collectives, on_device(): lax.all_gather(vectors, ('dp', 'ctx'), axis=1, tiled=True)  86.9 us
    dot_general x8, matrix products, query_block(): jnp.einsum('shqk,skhd->sqhd', dscores, key_heads, preferred_element_type=...  84.5 us
  transfers between devices with their start and end apart: 18, of which 5 were waited for; matrix products, arithmetic and copies ran while one was open for 48% of the time, Pallas kernels for 0%

commit v1 on v0

v1 whole, which is shorter than its diff:
```python
import functools
import jax
import jax.numpy as jnp
from jax import lax
from jax.experimental import pallas as pl
from jax.experimental.pallas import tpu as pltpu
from jax.sharding import PartitionSpec as P

HEAD_DIM = 64
F32 = jnp.float32
BF = jnp.bfloat16
NN = (((1,), (0,)), ((), ()))
NT = (((1,), (1,)), ((), ()))
TN = (((0,), (0,)), ((), ()))
epsilon = 1e-12
masked_score = -1e30


def dg(left, right, dims):
    return lax.dot_general(left, right, dims, preferred_element_type=F32)


def head_lanes(shape, h):
    lane=lax.broadcasted_iota(jnp.int32, shape, len(shape)-1)
    return (lane>=64)==(h==1), lane==(64 if h==0 else 0)

def fwd_kernel(q_ref, ko_ref, ks_ref, vo_ref, vs_ref, bias_ref, mb_ref, mix_ref, lse_ref, kh):
    half=ko_ref.shape[0]
    @pl.when(pl.program_id(1)==0)
    def _():
        for h in range(2):
            for i,kr in enumerate((ko_ref,ks_ref)):
                inside,spare=head_lanes((half,128),h)
                kh[h,i*half:(i+1)*half,:]=jnp.where(inside,kr[...],jnp.where(spare,bias_ref[i],jnp.zeros((),BF)))
    bq=q_ref.shape[0]
    q=q_ref[...]*jnp.asarray(0.125,BF)
    outs=[];lses=[]
    for h in range(2):
        inside,spare=head_lanes((bq,128),h)
        qm=jnp.where(inside,q,jnp.where(spare,jnp.ones((),BF),jnp.zeros((),BF)))
        s=dg(qm,kh[h],NT)
        m=jnp.max(s,axis=1,keepdims=True)
        e=jnp.exp(s-m)
        l=jnp.sum(e,axis=1,keepdims=True)
        eb=e.astype(BF)
        acc=dg(eb[:,:half],vo_ref[...],NN)+dg(eb[:,half:],vs_ref[...],NN)
        outs.append(acc/l); lses.append(m+jnp.log(l))
    lane=lax.broadcasted_iota(jnp.int32,(bq,128),1)
    mix=jnp.where(lane<64,outs[0],outs[1])
    mix_ref[...]=mix; mb_ref[...]=mix.astype(BF)
    packed=jnp.where(lane==0,lses[0],lses[1])
    lse_ref[0]=packed.T[:8]

def attention_forward(q, kv, kv_sib, bias, bq=256, vmem=48<<20):
    rows=q.shape[0]; pairs=q.shape[1]//128
    return pl.pallas_call(fwd_kernel, grid=(pairs, rows//bq),
        in_specs=[pl.BlockSpec((bq,128),lambda p,j:(j,p)),
                  pl.BlockSpec((rows,128),lambda p,j:(0,p)), pl.BlockSpec((rows,128),lambda p,j:(0,p)),
                  pl.BlockSpec((rows,128),lambda p,j:(0,pairs+p)), pl.BlockSpec((rows,128),lambda p,j:(0,pairs+p)),
                  pl.BlockSpec((2,rows,128),lambda p,j:(0,0,0))],
        out_specs=[pl.BlockSpec((bq,128),lambda p,j:(j,p)),pl.BlockSpec((bq,128),lambda p,j:(j,p)),pl.BlockSpec((1,8,bq),lambda p,j:(p,0,j))],
        out_shape=[jax.ShapeDtypeStruct(q.shape,BF),jax.ShapeDtypeStruct(q.shape,F32),jax.ShapeDtypeStruct((pairs,8,rows),F32)],
        scratch_shapes=[pltpu.VMEM((2,2*rows,128),BF)],
        compiler_params=pltpu.CompilerParams(vmem_limit_bytes=vmem),
        cost_estimate=pl.CostEstimate(flops=4*rows*2*rows*128*pairs*2,bytes_accessed=14*rows*768,transcendentals=rows*rows*4*pairs),
        name="attend")(q,kv,kv_sib,kv,kv_sib,bias)

def bwd_kernel(q_ref, do_ref, mix_ref, ko_ref, ks_ref, vo_ref, vs_ref, bias_ref, lse_ref, dq_ref, dko_ref, dvo_ref, dks_ref, dvs_ref, kh, dk, dv, *, ck):
    half=ko_ref.shape[0]; j=pl.program_id(1)
    @pl.when(j==0)
    def _():
        for h in range(2):
            for i,kr in enumerate((ko_ref,ks_ref)):
                inside,spare=head_lanes((half,128),h)
                kh[h,i*half:(i+1)*half,:]=jnp.where(inside,kr[...],jnp.where(spare,bias_ref[i],jnp.zeros((),BF)))
        dk[...]=jnp.zeros_like(dk); dv[...]=jnp.zeros_like(dv)
    bq=q_ref.shape[0]
    q=q_ref[...]*jnp.asarray(0.125,BF); do=do_ref[...]
    prod=(do.astype(F32)*mix_ref[...]).T
    zero=jnp.zeros((),BF); one=jnp.ones((),BF)
    hs=[]
    for h in range(2):
        inside,spare=head_lanes((bq,128),h)
        hs.append((jnp.where(inside,q,jnp.where(spare,one,zero)),jnp.where(inside,q,zero),jnp.where(inside,do,zero),
                   lse_ref[0,h:h+1,:],jnp.sum(prod[h*64:(h+1)*64],axis=0,keepdims=True)))
    dq=jnp.zeros((bq,128),F32)
    for c in range(2*half//ck):
        vr=vo_ref if c*ck<half else vs_ref
        off=c*ck if c*ck<half else c*ck-half
        v=vr[off:off+ck,:]
        sl=slice(c*ck,(c+1)*ck)
        for h in range(2):
            qm,qz,dom,lse,delta=hs[h]
            k=kh[h,sl,:]
            p=jnp.exp(dg(k,qm,NT)-lse)
            dp=dg(v,dom,NT)
            ds=(p*(dp-delta)).astype(BF)
            dv[sl,:]+=dg(p.astype(BF),dom,NN)
            dk[sl,:]+=dg(ds,qz,NN)
            dq=dq+dg(ds,k,TN)
    dq_ref[...]=(dq*0.125).astype(BF)
    @pl.when(j==pl.num_programs(1)-1)
    def _():
        dko_ref[...]=dk[:half,:]; dvo_ref[...]=dv[:half,:]
        dks_ref[...]=dk[half:,:].astype(BF); dvs_ref[...]=dv[half:,:].astype(BF)

def attention_backward(q, do, mix, kv, kv_sib, bias, lse, bq=256, ck=512, vmem=48<<20):
    rows=q.shape[0]; pairs=q.shape[1]//128
    blk=pl.BlockSpec((bq,128),lambda p,j:(j,p)); full=pl.BlockSpec((rows,128),lambda p,j:(0,p)); fullv=pl.BlockSpec((rows,128),lambda p,j:(0,pairs+p))
    S=jax.ShapeDtypeStruct
    return pl.pallas_call(functools.partial(bwd_kernel,ck=ck), grid=(pairs, rows//bq),
        in_specs=[blk,blk,blk,full,full,fullv,fullv,pl.BlockSpec((2,rows,128),lambda p,j:(0,0,0)),pl.BlockSpec((1,8,bq),lambda p,j:(p,0,j))],
        out_specs=[blk,full,full,full,full],
        out_shape=[S(q.shape,BF),S(q.shape,F32),S(q.shape,F32),S(q.shape,BF),S(q.shape,BF)],
        scratch_shapes=[pltpu.VMEM((2,2*rows,128),BF),pltpu.VMEM((2*rows,128),F32),pltpu.VMEM((2*rows,128),F32)],
        compiler_params=pltpu.CompilerParams(vmem_limit_bytes=vmem),
        cost_estimate=pl.CostEstimate(flops=10*rows*2*rows*128*pairs*2,bytes_accessed=26*rows*768,transcendentals=rows*rows*4*pairs),
        name="attend_back")(q,do,mix,kv,kv_sib,kv,kv_sib,bias,lse)


def normalize(hidden, scale_row, shift_row):
    centred = hidden - jnp.mean(hidden, axis=-1, keepdims=True)
    inverse = lax.rsqrt(jnp.mean(centred * centred, axis=-1, keepdims=True) + epsilon)
    standard = centred * inverse
    return (standard * scale_row + shift_row, standard, inverse)


def normalize_back(gradient, standard, inverse, scale_row):
    scaled = gradient * scale_row
    centred = scaled - jnp.mean(scaled, axis=-1, keepdims=True)
    return (centred - standard * jnp.mean(scaled * standard, axis=-1, keepdims=True)) * inverse


def reduce_blocks(grad, pair_perm, groups, dp, ctx):
    width = grad.shape[1]
    rows = grad.shape[0] // (dp * ctx)
    parity = lax.axis_index("ctx") % 2
    parts = grad.astype(BF).reshape(dp, ctx // 2, 2, rows, width)
    keep = lax.dynamic_index_in_dim(parts, parity, 2, keepdims=False)
    send = lax.dynamic_index_in_dim(parts, 1 - parity, 2, keepdims=False)
    got = lax.ppermute(send, "ctx", pair_perm)
    part = (keep.astype(F32) + got.astype(F32)).astype(BF)
    got = lax.all_to_all(part, "ctx", 1, 1, axis_index_groups=groups, tiled=True)
    part = jnp.sum(got.astype(F32), axis=1).astype(BF)
    got = lax.all_to_all(part, "dp", 0, 0, tiled=True)
    return jnp.sum(got.astype(F32), axis=0)


def on_device(
    tokens, cotangent, lengths, w_query, w_key, w_value, w_attn_out, w_up, b_up, w_down, vectors
):
    seqs, rows_dev, width = tokens.shape
    dp = lax.axis_size("dp")
    ctx = lax.axis_size("ctx")
    half = rows_dev // 2
    rows = half * ctx
    member = lax.axis_index("ctx") % 2
    own_seq = lax.axis_index("dp") * seqs + lax.axis_index("ctx") // 2
    length = lax.dynamic_index_in_dim(lengths, own_seq, 0, keepdims=False)
    pair_perm = [(i, i ^ 1) for i in range(ctx)]
    groups = [list(range(k, ctx, 2)) for k in range(2)]

    def exchange(array):
        return lax.all_to_all(array, "ctx", 0, 0, tiled=True)

    def collect(array, axis=0):
        return lax.all_gather(array, ("dp", "ctx"), axis=axis, tiled=True)

    split = tokens.reshape(ctx, half, width)
    low_in = exchange(split.astype(BF)).reshape(rows, width)
    full_qkv = collect(jnp.concatenate([w_query, w_key, w_value], axis=1))
    small = collect(jnp.concatenate([b_up.reshape(1, -1), vectors.reshape(1, -1)], axis=1))
    up_slots = b_up.shape[0]
    full_bias_up = small[:, :up_slots].reshape(-1).astype(F32)
    vector_rows = (
        small[:, up_slots:].reshape(dp * ctx, 8, -1).transpose(1, 0, 2).reshape(8, width).astype(F32)
    )
    full_attn = collect(w_attn_out)
    full_up = collect(w_up)
    full_down = collect(w_down)
    residual = exchange(split).reshape(rows, width)
    upstream = exchange(cotangent.reshape(ctx, half, width)).reshape(rows, width)

    slot = jnp.arange(rows, dtype=jnp.int32)
    source = slot // half
    high = (2 * ctx - 1 - source) * half + slot % half

    def key_bias(kind):
        position = jnp.where(kind == 0, slot, high)
        return jnp.where(position < length, 0.0, masked_score).astype(BF)

    bias = jnp.stack([key_bias(member), key_bias(1 - member)])
    bias = jnp.broadcast_to(bias[:, :, None], (2, rows, 128))

    row_of = jnp.concatenate([jnp.zeros_like(vector_rows[1]), vector_rows[1]])
    kv = (dg(low_in, full_qkv[:, width:], NN) + row_of).astype(BF)
    kv_sib = lax.ppermute(kv, "ctx", pair_perm)
    queries = (dg(low_in, full_qkv[:, :width], NN) + vector_rows[0]).astype(BF)
    low_mixed, mixed, lse = attention_forward(queries, kv, kv_sib, bias)

    attention = dg(low_mixed, full_attn, NN) + vector_rows[2]
    normed_one, standard_one, inverse_one = normalize(
        residual + attention, vector_rows[6], vector_rows[4]
    )
    low_first = normed_one.astype(BF)
    inner = dg(low_first, full_up, NN) + full_bias_up
    active = jax.nn.gelu(inner, approximate=False).astype(BF)
    branch = dg(active, full_down, NN) + vector_rows[3]
    result, standard_two, inverse_two = normalize(
        normed_one + branch, vector_rows[7], vector_rows[5]
    )
    output = exchange(result.reshape(ctx, half, width)).reshape(seqs, rows_dev, width)

    d_gain_two = jnp.sum(upstream * standard_two, axis=0)
    d_shift_two = jnp.sum(upstream, axis=0)
    grad_second = normalize_back(upstream, standard_two, inverse_two, vector_rows[7])
    low_branch = grad_second.astype(BF)
    d_bias_down = jnp.sum(low_branch.astype(F32), axis=0)
    d_down = dg(active, low_branch, TN)
    d_active = dg(low_branch, full_down, NT)
    gelu_back = jax.vjp(lambda v: jax.nn.gelu(v, approximate=False), inner)[1]
    low_inner = gelu_back(d_active)[0].astype(BF)
    d_bias_up = jnp.sum(low_inner.astype(F32), axis=0)
    d_up = dg(low_first, low_inner, TN)
    own_down = reduce_blocks(d_down, pair_perm, groups, dp, ctx)
    own_up = reduce_blocks(d_up, pair_perm, groups, dp, ctx)
    grad_first = grad_second + dg(low_inner, full_up, NT)
    d_gain_one = jnp.sum(grad_first * standard_one, axis=0)
    d_shift_one = jnp.sum(grad_first, axis=0)
    grad_sum = normalize_back(grad_first, standard_one, inverse_one, vector_rows[6])
    low_attn = grad_sum.astype(BF)
    d_bias_attn = jnp.sum(low_attn.astype(F32), axis=0)
    d_attn = dg(low_mixed, low_attn, TN)
    d_mixed = dg(low_attn, full_attn, NT).astype(BF)

    dq, dk_own, dv_own, dk_sib, dv_sib = attention_backward(
        queries, d_mixed, mixed, kv, kv_sib, bias, lse
    )
    dk_got = lax.ppermute(dk_sib, "ctx", pair_perm)
    dv_got = lax.ppermute(dv_sib, "ctx", pair_perm)
    dk = (dk_own + dk_got.astype(F32)).astype(BF)
    dv = (dv_own + dv_got.astype(F32)).astype(BF)
    grad_in = grad_sum + (
        dg(dq, full_qkv[:, :width], NT)
        + dg(dk, full_qkv[:, width : 2 * width], NT)
        + dg(dv, full_qkv[:, 2 * width :], NT)
    )
    grad_tokens = exchange(grad_in.reshape(ctx, half, width)).reshape(seqs, rows_dev, width)
    d_vector_rows = jnp.stack(
        [
            jnp.sum(dq.astype(F32), axis=0),
            jnp.sum(dv.astype(F32), axis=0),
            d_bias_attn,
            d_bias_down,
            d_shift_one,
            d_shift_two,
            d_gain_one,
            d_gain_two,
        ]
    )
    extra = jnp.concatenate([d_vector_rows.T, d_bias_up.reshape(width, -1)], axis=1)
    extra = jnp.pad(extra, ((0, 0), (0, 128 - extra.shape[1])))
    joined = jnp.concatenate(
        [d_attn, dg(low_in, dq, TN), dg(low_in, dk, TN), dg(low_in, dv, TN), extra], axis=1
    )
    own = reduce_blocks(joined, pair_perm, groups, dp, ctx)
    own_attn, own_query, own_key, own_value = (
        own[:, i * width : (i + 1) * width] for i in range(4)
    )
    own_extra = own[:, 4 * width :]
    own_vectors = own_extra[:, :8].T
    own_bias_up = own_extra[:, 8 : 8 + d_bias_up.shape[0] // width].reshape(-1)
    return (
        output,
        grad_tokens,
        own_query,
        own_key,
        own_value,
        own_attn,
        own_up,
        own_bias_up,
        own_down,
        own_vectors,
    )


def solution(mesh):
    in_specs = (
        P("dp", "ctx", None),
        P("dp", "ctx", None),
        P(),
        P(("dp", "ctx"), None),
        P(("dp", "ctx"), None),
        P(("dp", "ctx"), None),
        P(("dp", "ctx"), None),
        P(("dp", "ctx"), None),
        P(("dp", "ctx")),
        P(("dp", "ctx"), None),
        P(None, ("dp", "ctx")),
    )
    out_specs = (
        P("dp", "ctx", None),
        P("dp", "ctx", None),
        P(("dp", "ctx"), None),
        P(("dp", "ctx"), None),
        P(("dp", "ctx"), None),
        P(("dp", "ctx"), None),
        P(("dp", "ctx"), None),
        P(("dp", "ctx")),
        P(("dp", "ctx"), None),
        P(None, ("dp", "ctx")),
    )
    return jax.shard_map(
        on_device, mesh=mesh, in_specs=in_specs, out_specs=out_specs, check_vma=False
    )
```

time: 1650 us -> 683 us (0.41)
  matrix products: 602 us -> 131 us
  waiting for transfers between devices: 452 us -> 179 us
  blocking collectives: 296 us -> 76.2 us
  Pallas kernels: 0 us -> 133 us
  local copies, waits for them, and re-layouts: 148 us -> 39.9 us
  other arithmetic: 110 us -> 45.5 us
  starting transfers between devices: 20.7 us -> 56.9 us
    dot_general x74 -> x17, matrix products: 602 us -> 131 us  [dg(): return lax.dot_general(left, right, dims, preferred_element_type=F32)]
    reduce_scatter x6 -> x0, waiting for transfers between devices: 307 us -> none  [the longest x1 104 us: on_device(): lax.psum_scatter(d_wkey, ('dp', 'ctx'), scatter_dimension=0, tiled=True)]
    unnamed x2 -> x0, blocking collectives: 187 us -> none
    pallas_call x0 -> x2, Pallas kernels: none -> 133 us  [the longest x1 82.8 us: attention_backward(): pl.pallas_call(functools.partial(bwd_kernel, ck=ck), grid=(pairs, rows //...]
    all_to_all x4 -> x11, waiting for transfers between devices: 0.01 us -> 131 us  [the longest x3 55 us: reduce_blocks(): lax.all_to_all(part, 'ctx', 1, 1, axis_index_groups=groups, tiled=True)]
    all_gather x8 -> x4, waiting for transfers between devices: 141 us -> 46.1 us  [collect(): return lax.all_gather(array, ('dp', 'ctx'), axis=axis, tiled=True)]
    slice x25 -> x2, local copies, waits for them, and re-layouts: 72.6 us -> 0.79 us  [the longest x1 0.71 us: on_device(): own[:, i * width:(i + 1) * width]]
    all_to_all x4 -> x11, starting transfers between devices: 20.2 us -> 55.5 us  [the longest x5 26.6 us: exchange(): return lax.all_to_all(array, 'ctx', 0, 0, tiled=True)]
  transfers between devices with their start and end apart: 18 -> 21, of which waited for: 5 -> 10; matrix products, arithmetic and copies ran while one was open for 48% -> 26% of each run, Pallas kernels for 0% -> 20%
where the time goes in v1:
time: 683 us; the launch traced here: 676 us
  waiting for transfers between devices  179 us (26%)
  Pallas kernels  133 us (19%)
  matrix products  131 us (19%)
  blocking collectives  76.2 us (11%)
  starting transfers between devices  56.9 us (8%)
  other arithmetic  45.5 us (7%)
  local copies, waits for them, and re-layouts  39.9 us (6%)
  between operations  14.6 us (2%)
    dot_general x17, matrix products, dg(): return lax.dot_general(left, right, dims, preferred_element_type=F32)  131 us
    pallas_call x1, Pallas kernels, attention_backward(): pl.pallas_call(functools.partial(bwd_kernel, ck=ck), grid=(pairs, rows //...  82.8 us
    all_gather x1, blocking collectives, collect(): return lax.all_gather(array, ('dp', 'ctx'), axis=axis, tiled=True)  76.2 us
    all_to_all x3, waiting for transfers between devices, reduce_blocks(): lax.all_to_all(part, 'ctx', 1, 1, axis_index_groups=groups, tiled=True)  55 us
    pallas_call x1, Pallas kernels, attention_forward(): pl.pallas_call(fwd_kernel, grid=(pairs, rows // bq), in_specs=[pl.BlockSp...  49.9 us
    all_gather x4, waiting for transfers between devices, collect(): return lax.all_gather(array, ('dp', 'ctx'), axis=axis, tiled=True)  46.1 us
    all_to_all x5, waiting for transfers between devices, exchange(): return lax.all_to_all(array, 'ctx', 0, 0, tiled=True)  43.7 us
    all_to_all x3, waiting for transfers between devices, reduce_blocks(): got = lax.all_to_all(part, 'dp', 0, 0, tiled=True)  32.3 us
  transfers between devices with their start and end apart: 21, of which 10 were waited for; matrix products, arithmetic and copies ran while one was open for 26% of the time, Pallas kernels for 20%

profile of v1, /device:TPU:1, one launch (start us, length us, event | category | flops | bytes accessed | tf_op | source)
XLA Modules:
  0.0 675.8 jit_solution(1553309113792791773)
XLA Ops:
  13.4 5.2 all-to-all-start.1
  18.7 18.3 %all-to-all-done.1 = bf16[8,128,768]{2,1,0:T(8,128)(2,1)S(1)} async-done(((bf16[8,128,768]{2,1,0:T(8,128)(2,1)}), bf16[8,128,768]{2,1,0:T(8,128)(2,1)S(1)}, u32[]{:S(2)}, u32[]{:S(2)}) %all-to-all-start.1) | async-done | bytes 1572896 | tf_op jit(solution)/shard_map/all_to_all | solution.py:164
  38.2 7.0 %all-to-all-start.3 = ((f32[8,128,768]{2,1,0:T(8,128)}), f32[8,128,768]{2,1,0:T(8,128)S(1)}, u32[]{:S(2)}, u32[]{:S(2)}) async-start(f32[8,128,768]{2,1,0:T(8,128)} %bitcast.101), calls=%async_computation.3 | async-start | bytes 6291456 | tf_op jit(solution)/shard_map/all_to_all | solution.py:164
  45.2 76.2 %all-gather = bf16[32,1,288]{2,1,0:T(2,128)(2,1)S(1)} all-gather(bf16[1,1,288]{2,1,0:T(2,128)(2,1)S(1)} %maximum_bitcast_fusion), channel_id=1, replica_groups=mesh['dp'=4,'ctx'=8] {'dp','ctx'}, dimensions={0}, use_global_device_ids=true | all-gather | bytes 19008 | tf_op jit(solution)/shard_map/all_gather | solution.py:167
  122.2 6.4 fusion.9.ko_ref.vo_ref
  140.2 49.9 %attend.1 = (bf16[1024,768]{1,0:T(8,128)(2,1)S(1)}, f32[1024,768]{1,0:T(8,128)}, f32[6,8,1024]{2,1,0:T(8,128)S(1)}) custom-call(bf16[1024,768]{1,0:T(8,128)(2,1)S(1)} %fusion.13.q_ref, bf16[1024,1536]{1,0:T(8,128)(2,1)} %fusion.9.ko_ref.vo_ref, bf16[1024,1536]{1,0:T(8,128)(2,1)} %collective-permute-done.ks_ref.vs_ref, ...), custom_call_target="tpu_custom_call" | custom-call | flops 12884901888 | bytes 11010048 | tf_op jit(solution)/shard_map/attend/pallas_call | solution.py:56
  198.6 18.8 %all-gather.10.cloned.1.call-done = bf16[768,3072]{1,0:T(8,128)(2,1)} async-done(((bf16[24,3072]{1,0:T(8,128)(2,1)}), bf16[768,3072]{1,0:T(8,128)(2,1)}) %all-gather.10.cloned.1.call-update) | async-done | bytes 4718608 | tf_op jit(solution)/shard_map/all_gather | solution.py:167
  217.4 38.0 %multiply_convert_fusion = (bf16[1024,3072]{1,0:T(8,128)(2,1)}, f32[1024,3072]{1,0:T(8,128)}, f32[1024,3072]{1,0:T(8,128)}) fusion(f32[3072]{0:T(1024)S(1)} %reshape.269, bf16[768,3072]{1,0:T(8,128)(2,1)} %all-gather.10.cloned.1.call-done, f32[1024,768]{1,0:T(8,128)} %copy-done.7, f32[768]{0:T(1024)S(1)} %add.212, f32[768]{0:T(1024)S(1)} %mul.156, ...), kind=kOutput, calls=%fused_computation.3 | convolution fusion | flops 5043388416 | bytes 39348224 | tf_op jit(solution)/shard_map/dot_general | solution.py:20
  255.3 27.3 %all-gather.12.cloned.1.call-done = bf16[3072,768]{1,0:T(8,128)(2,1)} async-done(((bf16[96,768]{1,0:T(8,128)(2,1)}), bf16[3072,768]{1,0:T(8,128)(2,1)}) %all-gather.12.cloned.1.call-update) | async-done | bytes 4718608 | tf_op jit(solution)/shard_map/all_gather | solution.py:167
  282.6 9.4 %fusion.40 = (f32[1024]{0:T(1024)S(1)}, f32[1024,768]{1,0:T(8,128)S(1)}) fusion(f32[768]{0:T(1024)S(1)} %add.217, bf16[1024,3072]{1,0:T(8,128)(2,1)} %get-tuple-element.98, bf16[3072,768]{1,0:T(8,128)(2,1)} %all-gather.12.cloned.1.call-done, f32[768]{0:T(1024)S(1)} %add.212, f32[768]{0:T(1024)S(1)} %mul.156, f32[1024]{0:T(1024)S(1)} %add_rsqrt_fusion.1, ...), kind=kOutput, calls=%fused_computation.134 | convolution fusion | flops 4837342208 | bytes 17323008 | tf_op jit(solution)/shard_map/dot_general | solution.py:20
  298.4 5.6 convolution_convert_fusion
  307.7 18.9 %fusion.41 = (bf16[3072]{0:T(1024)(128)(2,1)S(1)}, bf16[1024,3072]{1,0:T(8,128)(2,1)}) fusion(f32[1024,3072]{1,0:T(8,128)} %get-tuple-element.99, bf16[3072,768]{1,0:T(8,128)(2,1)} %all-gather.12.cloned.1.call-done, f32[1024,768]{1,0:T(8,128)} %copy-done.17, f32[1024,3072]{1,0:T(8,128)} %get-tuple-element.113, f32[3072]{0:T(1024)S(1)} %reshape.269), kind=kOutput, calls=%fused_computation.135 | convolution fusion | flops 4882953216 | bytes 39340032 | tf_op jit(solution)/shard_map/dot_general | solution.py:20
  326.6 11.3 %multiply_reduce_fusion = (bf16[768]{0:T(1024)(128)(2,1)S(1)}, f32[1024]{0:T(1024)S(1)}, f32[1024]{0:T(1024)S(1)}, bf16[768]{0:T(1024)(128)(2,1)S(1)}, f32[1024,768]{1,0:T(8,128)}) fusion(f32[1024,768]{1,0:T(8,128)S(1)} %copy-done.8, f32[1024]{0:T(1024)S(1)} %add_rsqrt_fusion.1, f32[1024]{0:T(1024)S(1)} %broadcast_multiply_fusion.4, f32[768]{0:T(1024)S(1)} %mul.156, ...), kind=kOutput, calls=%fused_computation.31 | convolution fusion | flops 4839698432 | bytes 20469760 | tf_op jit(solution)/shard_map/dot_general | solution.py:20
  348.8 82.8 %attend_back.1 = (bf16[1024,768]{1,0:T(8,128)(2,1)S(1)}, f32[1024,768]{1,0:T(8,128)}, f32[1024,768]{1,0:T(8,128)}, bf16[1024,768]{1,0:T(8,128)(2,1)S(1)}, bf16[1024,768]{1,0:T(8,128)(2,1)}) custom-call(bf16[1024,768]{1,0:T(8,128)(2,1)} %copy-done.4, bf16[1024,768]{1,0:T(8,128)(2,1)} %convolution_convert_fusion.2.do_ref, ...), custom_call_target="tpu_custom_call" | custom-call | flops 32212254720 | bytes 20447232 | tf_op jit(solution)/shard_map/attend_back/pallas_call | solution.py:111
  431.6 8.9 %convolution_convert_fusion.1 = bf16[768,3072]{1,0:T(8,128)(2,1)S(1)} fusion(bf16[1024,3072]{1,0:T(8,128)(2,1)} %get-tuple-element.118, f32[1024,768]{1,0:T(8,128)S(1)} %copy-done.9, f32[768]{0:T(1024)S(1)} %add.212, f32[768]{0:T(1024)S(1)} %mul.156, f32[1024]{0:T(1024)S(1)} %add_rsqrt_fusion.1, f32[1024]{0:T(1024)S(1)} %broadcast_multiply_fusion.4), kind=kOutput, calls=%fused_computation.19 | convolution fusion | flops 4838129664 | bytes 14170112 | tf_op jit(solution)/shard_map/dot_general | solution.py:20
  481.3 13.5 %all-to-all-done.9 = bf16[4,4,96,768]{3,2,0,1:T(8,128)(2,1)} async-done(((bf16[4,4,96,768]{3,2,0,1:T(8,128)(2,1)}), bf16[4,4,96,768]{3,2,0,1:T(8,128)(2,1)}, u32[]{:S(2)}, u32[]{:S(2)}) %all-to-all-start.9) | async-done | bytes 2359328 | tf_op jit(solution)/shard_map/all_to_all | solution.py:143
  510.9 14.8 %all-to-all-done.7 = bf16[4,4,24,3072]{3,2,0,1:T(8,128)(2,1)S(1)} async-done(((bf16[4,4,24,3072]{3,2,0,1:T(8,128)(2,1)}), bf16[4,4,24,3072]{3,2,0,1:T(8,128)(2,1)S(1)}, u32[]{:S(2)}, u32[]{:S(2)}) %all-to-all-start.7) | async-done | bytes 2359328 | tf_op jit(solution)/shard_map/all_to_all | solution.py:143
  527.1 5.0 all-to-all-start.4
  541.1 25.4 %all-to-all-done.4 = f32[8,128,768]{2,1,0:T(8,128)S(1)} async-done(((f32[8,128,768]{2,1,0:T(8,128)}), f32[8,128,768]{2,1,0:T(8,128)S(1)}, u32[]{:S(2)}, u32[]{:S(2)}) %all-to-all-start.4) | async-done | bytes 3145760 | tf_op jit(solution)/shard_map/all_to_all | solution.py:164
  575.2 7.7 %all-to-all-done.10 = bf16[4,96,768]{2,1,0:T(8,128)(2,1)} async-done(((bf16[4,96,768]{2,1,0:T(8,128)(2,1)}), bf16[4,96,768]{2,1,0:T(8,128)(2,1)}, u32[]{:S(2)}, u32[]{:S(2)}) %all-to-all-start.10) | async-done | bytes 589856 | tf_op jit(solution)/shard_map/all_to_all | solution.py:145
  582.9 8.1 %all-to-all-start.5 = ((bf16[4,4,24,3200]{3,2,0,1:T(8,128)(2,1)}), bf16[4,4,24,3200]{3,2,0,1:T(8,128)(2,1)}, u32[]{:S(2)}, u32[]{:S(2)}) async-start(bf16[4,4,24,3200]{3,2,0,1:T(8,128)(2,1)} %fusion.6), calls=%async_computation.5 | async-start | bytes 4915200 | tf_op jit(solution)/shard_map/all_to_all | solution.py:143
  594.0 26.6 %all-to-all-done.5 = bf16[4,4,24,3200]{3,2,0,1:T(8,128)(2,1)} async-done(((bf16[4,4,24,3200]{3,2,0,1:T(8,128)(2,1)}), bf16[4,4,24,3200]{3,2,0,1:T(8,128)(2,1)}, u32[]{:S(2)}, u32[]{:S(2)}) %all-to-all-start.5) | async-done | bytes 2457632 | tf_op jit(solution)/shard_map/all_to_all | solution.py:143
  627.8 12.4 %all-to-all-done.8 = bf16[4,24,3072]{2,1,0:T(8,128)(2,1)} async-done(((bf16[4,24,3072]{2,1,0:T(8,128)(2,1)}), bf16[4,24,3072]{2,1,0:T(8,128)(2,1)}, u32[]{:S(2)}, u32[]{:S(2)}) %all-to-all-start.8) | async-done | bytes 589856 | tf_op jit(solution)/shard_map/all_to_all | solution.py:145
  648.1 12.2 %all-to-all-done.6 = bf16[4,24,3200]{2,1,0:T(8,128)(2,1)} async-done(((bf16[4,24,3200]{2,1,0:T(8,128)(2,1)}), bf16[4,24,3200]{2,1,0:T(8,128)(2,1)}, u32[]{:S(2)}, u32[]{:S(2)}) %all-to-all-start.6) | async-done | bytes 614432 | tf_op jit(solution)/shard_map/all_to_all | solution.py:145
  (187 shorter events, 151.5 us)
Async XLA Ops:
  7.2 115.0 %all-gather.6.cloned.1.call-start = ((), (), s32[]{:S(2)}) async-start(), calls=%async_computation.11 | async-start | bytes 3649536 | tf_op jit(solution)/shard_map/all_gather | solution.py:167
  8.7 183.4 %all-gather.8.cloned.1.call-start = ((), (), s32[]{:S(2)}) async-start(), calls=%async_computation.12 | async-start | bytes 1216512 | tf_op jit(solution)/shard_map/all_gather | solution.py:167
  9.5 207.9 %all-gather.10.cloned.1.call-start = ((), (), s32[]{:S(2)}) async-start(), calls=%async_computation.13 | async-start | bytes 4866048 | tf_op jit(solution)/shard_map/all_gather | solution.py:167
  13.4 23.6 %all-to-all-start.1 = ((bf16[8,128,768]{2,1,0:T(8,128)(2,1)}), bf16[8,128,768]{2,1,0:T(8,128)(2,1)S(1)}, u32[]{:S(2)}, u32[]{:S(2)}) async-start(bf16[8,128,768]{2,1,0:T(8,128)(2,1)} %convert_element_type.159), calls=%async_computation.1 | async-start | bytes 3145728 | tf_op jit(solution)/shard_map/all_to_all | solution.py:164
  38.2 90.6 %all-to-all-start.3 = ((f32[8,128,768]{2,1,0:T(8,128)}), f32[8,128,768]{2,1,0:T(8,128)S(1)}, u32[]{:S(2)}, u32[]{:S(2)}) async-start(f32[8,128,768]{2,1,0:T(8,128)} %bitcast.101), calls=%async_computation.3 | async-start | bytes 6291456 | tf_op jit(solution)/shard_map/all_to_all | solution.py:164
  128.6 11.3 %collective-permute-start = (bf16[1024,1536]{1,0:T(8,128)(2,1)}, bf16[1024,1536]{1,0:T(8,128)(2,1)}, u32[]{:S(2)}, u32[]{:S(2)}) collective-permute-start(bf16[1024,1536]{1,0:T(8,128)(2,1)} %fusion.9.ko_ref.vo_ref), channel_id=1, source_target_pairs={{0,1},{1,0},{2,3},{3,2},{4,5},{5,4},{6,7},{7,6},{8,9},{9,8},{10,11... | collective-permute-start | bytes 9437192 | tf_op jit(solution)/shard_map/ppermute | solution.py:197
  128.8 63.3 %all-to-all-start = ((f32[8,128,768]{2,1,0:T(8,128)}), f32[8,128,768]{2,1,0:T(8,128)}, u32[]{:S(2)}, u32[]{:S(2)}) async-start(f32[8,128,768]{2,1,0:T(8,128)} %bitcast.95), calls=%async_computation | async-start | bytes 6291456 | tf_op jit(solution)/shard_map/all_to_all | solution.py:164
  133.5 149.1 %all-gather.12.cloned.1.call-start = ((), (), s32[]{:S(2)}) async-start(), calls=%async_computation.14 | async-start | bytes 4866048 | tf_op jit(solution)/shard_map/all_gather | solution.py:167
  307.4 151.2 %collective-permute-start.5 = (bf16[4,4,96,768]{3,2,0,1:T(8,128)(2,1)}, bf16[4,4,96,768]{3,2,0,1:T(8,128)(2,1)}, u32[]{:S(2)}, u32[]{:S(2)}) collective-permute-start(bf16[4,4,96,768]{3,2,0,1:T(8,128)(2,1)} %bitcast.91), channel_id=1, source_target_pairs={{0,1},{1,0},{2,3},{3,2},{4,5},{5,4},{6,7},{7,6},{8,9},{9,8},{10,11... | collective-permute-start | bytes 7077896 | tf_op jit(solution)/shard_map/ppermute | solution.py:141
  307.7 18.9 %copy-start.8 = (f32[1024,768]{1,0:T(8,128)S(1)}, f32[1024,768]{1,0:T(8,128)}, u32[]{:S(2)}) copy-start(f32[1024,768]{1,0:T(8,128)} %copy-done.7) | copy-start | bytes 9437188
  338.0 124.5 %all-to-all-start.2 = ((f32[8,128,768]{2,1,0:T(8,128)}), f32[8,128,768]{2,1,0:T(8,128)}, u32[]{:S(2)}, u32[]{:S(2)}) async-start(f32[8,128,768]{2,1,0:T(8,128)} %bitcast.97), calls=%async_computation.2 | async-start | bytes 6291456 | tf_op jit(solution)/shard_map/all_to_all | solution.py:164
  346.1 96.3 %copy-start.10 = (f32[1024,768]{1,0:T(8,128)}, f32[1024,768]{1,0:T(8,128)S(1)}, u32[]{:S(2)}) copy-start(f32[1024,768]{1,0:T(8,128)S(1)} %get-tuple-element.95) | copy-start | bytes 9437188
  348.8 82.8 %copy-start.9 = (f32[1024,768]{1,0:T(8,128)S(1)}, f32[1024,768]{1,0:T(8,128)}, u32[]{:S(2)}) copy-start(f32[1024,768]{1,0:T(8,128)} %copy-done.7) | copy-start | bytes 9437188
  440.5 26.5 %collective-permute-start.2 = (bf16[1024,768]{1,0:T(8,128)(2,1)}, bf16[1024,768]{1,0:T(8,128)(2,1)}, u32[]{:S(2)}, u32[]{:S(2)}) collective-permute-start(bf16[1024,768]{1,0:T(8,128)(2,1)} %get-tuple-element.25), channel_id=1, source_target_pairs={{0,1},{1,0},{2,3},{3,2},{4,5},{5,4},{6,7},{7,6},{8,9},{9,8},{10,11... | collective-permute-start | bytes 4718600 | tf_op jit(solution)/shard_map/ppermute | solution.py:240
  446.5 29.8 %collective-permute-start.4 = (bf16[4,4,24,3072]{3,2,0,1:T(8,128)(2,1)}, bf16[4,4,24,3072]{3,2,0,1:T(8,128)(2,1)}, u32[]{:S(2)}, u32[]{:S(2)}) collective-permute-start(bf16[4,4,24,3072]{3,2,0,1:T(8,128)(2,1)} %bitcast.92), channel_id=1, source_target_pairs={{0,1},{1,0},{2,3},{3,2},{4,5},{5,4},{6,7},{7,6},{8,9},{9,8},{10,11... | collective-permute-start | bytes 7077896 | tf_op jit(solution)/shard_map/ppermute | solution.py:141
  446.9 24.5 %collective-permute-start.1 = (bf16[1024,768]{1,0:T(8,128)(2,1)S(1)}, bf16[1024,768]{1,0:T(8,128)(2,1)}, u32[]{:S(2)}, u32[]{:S(2)}) collective-permute-start(bf16[1024,768]{1,0:T(8,128)(2,1)S(1)} %get-tuple-element.23), channel_id=1, source_target_pairs={{0,1},{1,0},{2,3},{3,2},{4,5},{5,4},{6,7},{7,6},{8,9},{9,8},{10,11... | collective-permute-start | bytes 4718600 | tf_op jit(solution)/shard_map/ppermute | solution.py:239
  462.4 32.4 %all-to-all-start.9 = ((bf16[4,4,96,768]{3,2,0,1:T(8,128)(2,1)}), bf16[4,4,96,768]{3,2,0,1:T(8,128)(2,1)}, u32[]{:S(2)}, u32[]{:S(2)}) async-start(bf16[4,4,96,768]{3,2,0,1:T(8,128)(2,1)} %fusion.7), calls=%async_computation.9 | async-start | bytes 4718592 | tf_op jit(solution)/shard_map/all_to_all | solution.py:143
  494.8 30.9 %all-to-all-start.7 = ((bf16[4,4,24,3072]{3,2,0,1:T(8,128)(2,1)}), bf16[4,4,24,3072]{3,2,0,1:T(8,128)(2,1)S(1)}, u32[]{:S(2)}, u32[]{:S(2)}) async-start(bf16[4,4,24,3072]{3,2,0,1:T(8,128)(2,1)} %fusion.8), calls=%async_computation.7 | async-start | bytes 4718592 | tf_op jit(solution)/shard_map/all_to_all | solution.py:143
  527.1 39.4 %all-to-all-start.4 = ((f32[8,128,768]{2,1,0:T(8,128)}), f32[8,128,768]{2,1,0:T(8,128)S(1)}, u32[]{:S(2)}, u32[]{:S(2)}) async-start(f32[8,128,768]{2,1,0:T(8,128)} %bitcast.98), calls=%async_computation.4 | async-start | bytes 6291456 | tf_op jit(solution)/shard_map/all_to_all | solution.py:164
  538.0 32.7 %collective-permute-start.3 = (bf16[4,4,24,3200]{3,2,0,1:T(8,128)(2,1)}, bf16[4,4,24,3200]{3,2,0,1:T(8,128)(2,1)}, u32[]{:S(2)}, u32[]{:S(2)}) collective-permute-start(bf16[4,4,24,3200]{3,2,0,1:T(8,128)(2,1)} %bitcast.90), channel_id=1, source_target_pairs={{0,1},{1,0},{2,3},{3,2},{4,5},{5,4},{6,7},{7,6},{8,9},{9,8},{10,11... | collective-permute-start | bytes 7372808 | tf_op jit(solution)/shard_map/ppermute | solution.py:141
  566.6 16.3 %all-to-all-start.10 = ((bf16[4,96,768]{2,1,0:T(8,128)(2,1)}), bf16[4,96,768]{2,1,0:T(8,128)(2,1)}, u32[]{:S(2)}, u32[]{:S(2)}) async-start(bf16[4,96,768]{2,1,0:T(8,128)(2,1)} %reduce_sum.237), calls=%async_computation.10 | async-start | bytes 1179648 | tf_op jit(solution)/shard_map/all_to_all | solution.py:145
  582.9 37.7 %all-to-all-start.5 = ((bf16[4,4,24,3200]{3,2,0,1:T(8,128)(2,1)}), bf16[4,4,24,3200]{3,2,0,1:T(8,128)(2,1)}, u32[]{:S(2)}, u32[]{:S(2)}) async-start(bf16[4,4,24,3200]{3,2,0,1:T(8,128)(2,1)} %fusion.6), calls=%async_computation.5 | async-start | bytes 4915200 | tf_op jit(solution)/shard_map/all_to_all | solution.py:143
  620.6 19.6 %all-to-all-start.8 = ((bf16[4,24,3072]{2,1,0:T(8,128)(2,1)}), bf16[4,24,3072]{2,1,0:T(8,128)(2,1)}, u32[]{:S(2)}, u32[]{:S(2)}) async-start(bf16[4,24,3072]{2,1,0:T(8,128)(2,1)} %reduce_sum.235), calls=%async_computation.8 | async-start | bytes 1179648 | tf_op jit(solution)/shard_map/all_to_all | solution.py:145
  640.2 20.1 %all-to-all-start.6 = ((bf16[4,24,3200]{2,1,0:T(8,128)(2,1)}), bf16[4,24,3200]{2,1,0:T(8,128)(2,1)}, u32[]{:S(2)}, u32[]{:S(2)}) async-start(bf16[4,24,3200]{2,1,0:T(8,128)(2,1)} %reduce_sum.233), calls=%async_computation.6 | async-start | bytes 1228800 | tf_op jit(solution)/shard_map/all_to_all | solution.py:145
  (29 other events, 104.5 us)
Sparse Core Ops, SparseCore 0:
  11.5 75.7 all-gather.5
  90.2 56.3 all-gather.7
  149.4 67.8 all-gather.9
  220.1 62.4 all-gather.11

commit v2 on v1

v2 whole, which is shorter than its diff:
```python
import functools
import jax
import jax.numpy as jnp
from jax import lax
from jax.experimental import pallas as pl
from jax.experimental.pallas import tpu as pltpu
from jax.sharding import PartitionSpec as P

HEAD_DIM = 64
F32 = jnp.float32
BF = jnp.bfloat16
NN = (((1,), (0,)), ((), ()))
NT = (((1,), (1,)), ((), ()))
TN = (((0,), (0,)), ((), ()))
epsilon = 1e-12
masked_score = -1e30


def dg(left, right, dims):
    return lax.dot_general(left, right, dims, preferred_element_type=F32)


MESH = pl.DeviceIdType.MESH


class Mover:
    def __init__(self, local_sem, send_sem, recv_sem):
        self.local_sem, self.send_sem, self.recv_sem = local_sem, send_sem, recv_sem
        self.locals = self.remotes = 0

    def local(self, source, target):
        copy = pltpu.make_async_copy(source, target, self.local_sem.at[self.locals])
        self.locals += 1
        return copy

    def remote(self, source, target, device):
        number = self.remotes
        self.remotes += 1
        return pltpu.make_async_remote_copy(
            src_ref=source,
            dst_ref=target,
            send_sem=self.send_sem.at[number],
            recv_sem=self.recv_sem.at[number],
            device_id=device,
            device_id_type=MESH,
        )


def greet(devices):
    barrier = pltpu.get_barrier_semaphore()
    for device in devices:
        pl.semaphore_signal(barrier, inc=1, device_id=device, device_id_type=MESH)
    pl.semaphore_wait(barrier, len(devices))


def place(dp, ctx):
    d, c = lax.axis_index("dp"), lax.axis_index("ctx")
    groups = ctx // 2
    g, m = c // 2, c % 2
    over_dp = [((d + k) % dp, c) for k in range(1, dp)]
    over_groups = [(d, (g + k) % groups * 2 + m) for k in range(1, groups)]
    return d, c, g, m, over_dp, over_groups, (d, g * 2 + 1 - m)


def gather_kernel(dp, ctx, x, w, wo, wu, wd, x_in, w_full, zo, zu, zd, local_sem, send_sem, recv_sem):
    d, c, g, m, over_dp, over_groups, sibling = place(dp, ctx)
    groups = ctx // 2
    greet(over_dp + [(d, (c + k) % ctx) for k in range(1, ctx)])
    mover = Mover(local_sem, send_sem, recv_sem)
    own = [
        mover.local(source, target)
        for source, target in (
            (w, w_full.at[d, c]),
            (x.at[c], x_in.at[c]),
            (wo, zo.at[d]),
            (wu, zu.at[d]),
            (wd, zd.at[d]),
        )
    ]
    along = [mover.remote(w, w_full.at[d, c], device) for device in over_dp]
    across = [[mover.remote(w, w_full.at[d, c], device) for device in over_groups]]
    rows = [
        mover.remote(x.at[(c + k) % ctx], x_in.at[c], (d, (c + k) % ctx)) for k in range(1, ctx)
    ]
    rest = [
        mover.remote(source, target.at[d], device)
        for source, target in ((wo, zo), (wu, zu), (wd, zd))
        for device in over_dp
    ]
    for copy in own + along + across[0] + rows + rest:
        copy.start()
    for k in range(1, dp):
        along[k - 1].wait_recv()
        piece = w_full.at[(d - k + dp) % dp, c]
        across.append([mover.remote(piece, piece, device) for device in over_groups])
        for copy in across[-1]:
            copy.start()
    own[0].wait()
    mine = w_full.at[:, c]
    over = [mover.remote(mine, mine, sibling)]
    over[0].start()
    for k in range(1, groups):
        for batch in across:
            batch[k - 1].wait_recv()
        block = w_full.at[:, (g - k + groups) % groups * 2 + m]
        over.append(mover.remote(block, block, sibling))
        over[-1].start()
    for copy in over + rows + rest:
        copy.wait()
    for copy in along + [copy for batch in across for copy in batch]:
        copy.wait_send()
    for copy in own[1:]:
        copy.wait()


def gather_first(x, w, wo, wu, wd, dp, ctx):
    groups = ctx // 2
    remotes = (dp - 1) + dp * (groups - 1) + (ctx - 1) + 3 * (dp - 1) + groups
    any_space = pl.BlockSpec(memory_space=pl.ANY)
    return pl.pallas_call(
        functools.partial(gather_kernel, dp, ctx),
        in_specs=[any_space] * 5,
        out_specs=[any_space] * 5,
        out_shape=[
            jax.ShapeDtypeStruct(x.shape, BF),
            jax.ShapeDtypeStruct((dp, ctx) + w.shape, BF),
        ]
        + [jax.ShapeDtypeStruct((dp,) + array.shape, BF) for array in (wo, wu, wd)],
        scratch_shapes=[
            pltpu.SemaphoreType.DMA((5,)),
            pltpu.SemaphoreType.DMA((remotes,)),
            pltpu.SemaphoreType.DMA((remotes,)),
        ],
        compiler_params=pltpu.CompilerParams(collective_id=0, has_side_effects=True),
        name="gather_first",
    )(x, w, wo, wu, wd)


class Spread:
    def __init__(self, dp, ctx, sources, targets, mover):
        d, c, g, m, over_dp, over_groups, sibling = place(dp, ctx)
        groups = ctx // 2
        self.devices = over_groups + [sibling]
        self.own = [mover.local(s, t.at[:, c]) for s, t in zip(sources, targets)]
        self.direct = [mover.remote(s, t.at[:, c], sibling) for s, t in zip(sources, targets)]
        self.across = [
            [mover.remote(s, t.at[:, c], device) for device in over_groups]
            for s, t in zip(sources, targets)
        ]
        self.onward = []
        for t in targets:
            blocks = [t.at[:, (g - k + groups) % groups * 2 + m] for k in range(1, groups)]
            self.onward.append([mover.remote(block, block, sibling) for block in blocks])

    @staticmethod
    def count(groups, arrays):
        return arrays * (1 + 2 * (groups - 1))

    def begin(self):
        greet(self.devices)
        for copy in self.own + [copy for batch in self.across for copy in batch] + self.direct:
            copy.start()

    def forward(self, index):
        for came, copy in zip(self.across[index], self.onward[index]):
            came.wait_recv()
            copy.start()

    def finish(self):
        for copy in self.own + self.direct + [copy for batch in self.onward for copy in batch]:
            copy.wait()
        for batch in self.across:
            for copy in batch:
                copy.wait_send()


class Scatter:
    def __init__(self, dp, ctx, sources, outs, buffers, mover):
        d, c, g, m, over_dp, over_groups, sibling = place(dp, ctx)
        groups = ctx // 2
        self.dp, self.groups, self.d = dp, groups, d
        self.devices = over_groups + over_dp
        self.outs = outs
        self.mine = [b[0] for b in buffers]
        self.came = [b[1] for b in buffers]
        self.sums = [b[2] for b in buffers]
        self.last = [b[3] for b in buffers]
        self.own = [mover.local(s.at[:, g], b) for s, b in zip(sources, self.mine)]
        self.across = [
            [
                mover.remote(s.at[:, (g + k) % groups], b.at[k - 1], over_groups[k - 1])
                for k in range(1, groups)
            ]
            for s, b in zip(sources, self.came)
        ]
        self.along = [
            [
                mover.remote(s.at[(d + k) % dp], b.at[k - 1], over_dp[k - 1])
                for k in range(1, dp)
            ]
            for s, b in zip(self.sums, self.last)
        ]

    @staticmethod
    def count(dp, groups, arrays):
        return arrays * (groups - 1 + dp - 1)

    @staticmethod
    def scratch(dp, groups, sources):
        shapes = []
        for s in sources:
            block = s.shape[2:]
            shapes += [
                pltpu.VMEM((dp,) + block, BF),
                pltpu.VMEM((groups - 1, dp) + block, BF),
                pltpu.VMEM((dp,) + block, BF),
                pltpu.VMEM((dp - 1,) + block, BF),
            ]
        return shapes

    def begin(self):
        for copy in self.own + [copy for batch in self.across for copy in batch]:
            copy.start()

    def middle(self, index):
        self.own[index].wait()
        for copy in self.across[index]:
            copy.wait_recv()
        for k in range(self.dp):
            total = self.mine[index][k].astype(F32)
            for j in range(self.groups - 1):
                total = total + self.came[index][j, k].astype(F32)
            self.sums[index][k] = total.astype(BF)
        for copy in self.along[index]:
            copy.start()

    def finish(self):
        for index, out in enumerate(self.outs):
            for copy in self.along[index]:
                copy.wait_recv()
            total = self.sums[index][self.d].astype(F32)
            for j in range(self.dp - 1):
                total = total + self.last[index][j].astype(F32)
            out[...] = total
        for batch in self.across + self.along:
            for copy in batch:
                copy.wait_send()


def finish_kernel(dp, ctx, s, x, out, x_out, *scratch):
    buffers, (local_sem, send_sem, recv_sem) = scratch[:-3], scratch[-3:]
    d, c, g, m, over_dp, over_groups, sibling = place(dp, ctx)
    mover = Mover(local_sem, send_sem, recv_sem)
    scatter = Scatter(dp, ctx, [s], [out], [buffers], mover)
    own = mover.local(x.at[c], x_out.at[c])
    rows = [
        mover.remote(x.at[(c + k) % ctx], x_out.at[c], (d, (c + k) % ctx)) for k in range(1, ctx)
    ]
    greet(over_dp + [(d, (c + k) % ctx) for k in range(1, ctx)])
    scatter.begin()
    own.start()
    for copy in rows:
        copy.start()
    scatter.middle(0)
    scatter.finish()
    for copy in rows:
        copy.wait()
    own.wait()


def finish_gradients(s, x, dp, ctx):
    groups = ctx // 2
    remotes = Scatter.count(dp, groups, 1) + ctx - 1
    any_space = pl.BlockSpec(memory_space=pl.ANY)
    return pl.pallas_call(
        functools.partial(finish_kernel, dp, ctx),
        in_specs=[any_space] * 2,
        out_specs=[pl.BlockSpec(memory_space=pltpu.VMEM), any_space],
        out_shape=[jax.ShapeDtypeStruct(s.shape[2:], F32), jax.ShapeDtypeStruct(x.shape, x.dtype)],
        scratch_shapes=Scatter.scratch(dp, groups, [s])
        + [
            pltpu.SemaphoreType.DMA((2,)),
            pltpu.SemaphoreType.DMA((remotes,)),
            pltpu.SemaphoreType.DMA((remotes,)),
        ],
        compiler_params=pltpu.CompilerParams(
            collective_id=3, has_side_effects=True, vmem_limit_bytes=32 << 20
        ),
        name="finish_gradients",
    )(s, x)


def head_lanes(shape, h):
    lane = lax.broadcasted_iota(jnp.int32, shape, len(shape) - 1)
    return (lane >= 64) == (h == 1), lane == (64 if h == 0 else 0)


def load_keys(keys, own_ref, sib_ref, bias_ref):
    half = own_ref.shape[0]
    for h in range(2):
        for i, ref in enumerate((own_ref, sib_ref)):
            inside, spare = head_lanes((half, 128), h)
            rest = jnp.where(spare, bias_ref[i], jnp.zeros((), BF))
            keys[h, i * half : (i + 1) * half, :] = jnp.where(inside, ref[...], rest)


def forward_kernel(dp, ctx, *refs):
    (q_ref, ko_ref, ks_ref, vo_ref, vs_ref, bias_ref), refs = refs[:6], refs[6:]
    gathered, (mb_ref, mix_ref, lse_ref), spread_to, refs = refs[:3], refs[3:6], refs[6:9], refs[9:]
    keys, local_sem, send_sem, recv_sem = refs
    spread = Spread(dp, ctx, gathered, spread_to, Mover(local_sem, send_sem, recv_sem))
    steps = pl.num_programs(1)
    step = pl.program_id(0) * steps + pl.program_id(1)
    last = forward_steps(pl.num_programs(0), steps)

    @pl.when(step == 0)
    def _():
        spread.begin()

    @pl.when(pl.program_id(1) == 0)
    def _():
        load_keys(keys, ko_ref, ks_ref, bias_ref)

    half, bq = ko_ref.shape[0], q_ref.shape[0]
    q = q_ref[...] * jnp.asarray(0.125, BF)
    outs, lses = [], []
    for h in range(2):
        inside, spare = head_lanes((bq, 128), h)
        rest = jnp.where(spare, jnp.ones((), BF), jnp.zeros((), BF))
        scores = dg(jnp.where(inside, q, rest), keys[h], NT)
        top = jnp.max(scores, axis=1, keepdims=True)
        weights = jnp.exp(scores - top)
        total = jnp.sum(weights, axis=1, keepdims=True)
        low = weights.astype(BF)
        mixed = dg(low[:, :half], vo_ref[...], NN) + dg(low[:, half:], vs_ref[...], NN)
        outs.append(mixed / total)
        lses.append(top + jnp.log(total))
    lane = lax.broadcasted_iota(jnp.int32, (bq, 128), 1)
    mixed = jnp.where(lane < 64, outs[0], outs[1])
    mix_ref[...] = mixed
    mb_ref[...] = mixed.astype(BF)
    lse_ref[0] = jnp.where(lane == 0, lses[0], lses[1]).T[:8]

    for index, at in enumerate(last):

        @pl.when(step == at)
        def _(index=index):
            spread.forward(index)

    @pl.when(step == last[-1])
    def _():
        spread.finish()


def attention_forward(q, kv, kv_sib, bias, gathered, dp, ctx, bq=256):
    rows = q.shape[0]
    pairs = q.shape[1] // 128
    S = jax.ShapeDtypeStruct
    blk = pl.BlockSpec((bq, 128), lambda p, j: (j, p))
    k_spec = pl.BlockSpec((rows, 128), lambda p, j: (0, p))
    v_spec = pl.BlockSpec((rows, 128), lambda p, j: (0, pairs + p))
    any_space = pl.BlockSpec(memory_space=pl.ANY)
    remotes = Spread.count(ctx // 2, 3)
    return pl.pallas_call(
        functools.partial(forward_kernel, dp, ctx),
        grid=(pairs, rows // bq),
        in_specs=[blk, k_spec, k_spec, v_spec, v_spec]
        + [pl.BlockSpec((2, rows, 128), lambda p, j: (0, 0, 0))]
        + [any_space] * 3,
        out_specs=[blk, blk, pl.BlockSpec((1, 8, bq), lambda p, j: (p, 0, j))] + [any_space] * 3,
        out_shape=[S(q.shape, BF), S(q.shape, F32), S((pairs, 8, rows), F32)]
        + [S((dp, ctx) + array.shape[1:], BF) for array in gathered],
        scratch_shapes=[
            pltpu.VMEM((2, 2 * rows, 128), BF),
            pltpu.SemaphoreType.DMA((3,)),
            pltpu.SemaphoreType.DMA((remotes,)),
            pltpu.SemaphoreType.DMA((remotes,)),
        ],
        compiler_params=pltpu.CompilerParams(
            vmem_limit_bytes=48 << 20, collective_id=1, has_side_effects=True
        ),
        cost_estimate=pl.CostEstimate(
            flops=16 * rows * rows * 128 * pairs,
            bytes_accessed=14 * rows * 768,
            transcendentals=4 * rows * rows * pairs,
        ),
        name="attend",
    )(q, kv, kv_sib, kv, kv_sib, bias, *gathered)


def forward_steps(pairs, steps):
    count = pairs * steps
    return (count * 5 // 24, count * 15 // 24, count - 1)


def backward_steps(pairs, steps):
    count = pairs * steps
    return (count * 8 // 16, count * 3 // 16, count * 13 // 16)


def backward_kernel(dp, ctx, ck, *refs):
    (q_ref, do_ref, mix_ref, ko_ref, ks_ref, vo_ref, vs_ref, bias_ref, lse_ref), refs = (
        refs[:9],
        refs[9:],
    )
    sources, refs = refs[:3], refs[3:]
    (dq_ref, dko_ref, dvo_ref, dks_ref, dvs_ref), refs = refs[:5], refs[5:]
    summed, refs = refs[:3], refs[3:]
    (keys, dk, dv), refs = refs[:3], refs[3:]
    buffers, (local_sem, send_sem, recv_sem) = refs[:12], refs[12:]
    scatter = Scatter(
        dp,
        ctx,
        sources,
        summed,
        [buffers[i * 4 : i * 4 + 4] for i in range(3)],
        Mover(local_sem, send_sem, recv_sem),
    )
    steps = pl.num_programs(1)
    j = pl.program_id(1)
    step = pl.program_id(0) * steps + j

    @pl.when(step == 0)
    def _():
        greet(scatter.devices)
        scatter.begin()

    @pl.when(j == 0)
    def _():
        load_keys(keys, ko_ref, ks_ref, bias_ref)
        dk[...] = jnp.zeros_like(dk)
        dv[...] = jnp.zeros_like(dv)

    half, bq = ko_ref.shape[0], q_ref.shape[0]
    q = q_ref[...] * jnp.asarray(0.125, BF)
    do = do_ref[...]
    prod = (do.astype(F32) * mix_ref[...]).T
    zero, one = jnp.zeros((), BF), jnp.ones((), BF)
    heads = []
    for h in range(2):
        inside, spare = head_lanes((bq, 128), h)
        heads.append(
            (
                jnp.where(inside, q, jnp.where(spare, one, zero)),
                jnp.where(inside, q, zero),
                jnp.where(inside, do, zero),
                lse_ref[0, h : h + 1, :],
                jnp.sum(prod[h * 64 : (h + 1) * 64], axis=0, keepdims=True),
            )
        )
    dq = jnp.zeros((bq, 128), F32)
    for first in range(0, 2 * half, ck):
        rows = slice(first, first + ck)
        v = vo_ref[rows, :] if first < half else vs_ref[first - half : first - half + ck, :]
        for h in range(2):
            qm, qz, dom, lse, delta = heads[h]
            k = keys[h, rows, :]
            p = jnp.exp(dg(k, qm, NT) - lse)
            ds = (p * (dg(v, dom, NT) - delta)).astype(BF)
            dv[rows, :] += dg(p.astype(BF), dom, NN)
            dk[rows, :] += dg(ds, qz, NN)
            dq = dq + dg(ds, k, TN)
    dq_ref[...] = (dq * 0.125).astype(BF)

    @pl.when(j == steps - 1)
    def _():
        dko_ref[...] = dk[:half, :]
        dvo_ref[...] = dv[:half, :]
        dks_ref[...] = dk[half:, :].astype(BF)
        dvs_ref[...] = dv[half:, :].astype(BF)

    for index, at in enumerate(backward_steps(pl.num_programs(0), steps)):

        @pl.when(step == at)
        def _(index=index):
            scatter.middle(index)

    @pl.when(step == pl.num_programs(0) * steps - 1)
    def _():
        scatter.finish()


def attention_backward(q, do, mix, kv, kv_sib, bias, lse, sources, dp, ctx, bq=512, ck=512):
    rows = q.shape[0]
    pairs = q.shape[1] // 128
    S = jax.ShapeDtypeStruct
    blk = pl.BlockSpec((bq, 128), lambda p, j: (j, p))
    full = pl.BlockSpec((rows, 128), lambda p, j: (0, p))
    v_spec = pl.BlockSpec((rows, 128), lambda p, j: (0, pairs + p))
    any_space = pl.BlockSpec(memory_space=pl.ANY)
    remotes = Scatter.count(dp, ctx // 2, 3)
    sums = [s.shape[2:] for s in sources]
    return pl.pallas_call(
        functools.partial(backward_kernel, dp, ctx, ck),
        grid=(pairs, rows // bq),
        in_specs=[blk, blk, blk, full, full, v_spec, v_spec]
        + [pl.BlockSpec((2, rows, 128), lambda p, j: (0, 0, 0))]
        + [pl.BlockSpec((1, 8, bq), lambda p, j: (p, 0, j))]
        + [any_space] * 3,
        out_specs=[blk, full, full, full, full]
        + [pl.BlockSpec(shape, lambda p, j: (0, 0)) for shape in sums],
        out_shape=[
            S(q.shape, BF),
            S(q.shape, F32),
            S(q.shape, F32),
            S(q.shape, BF),
            S(q.shape, BF),
        ]
        + [S(shape, F32) for shape in sums],
        scratch_shapes=[
            pltpu.VMEM((2, 2 * rows, 128), BF),
            pltpu.VMEM((2 * rows, 128), F32),
            pltpu.VMEM((2 * rows, 128), F32),
        ]
        + Scatter.scratch(dp, ctx // 2, sources)
        + [
            pltpu.SemaphoreType.DMA((3,)),
            pltpu.SemaphoreType.DMA((remotes,)),
            pltpu.SemaphoreType.DMA((remotes,)),
        ],
        compiler_params=pltpu.CompilerParams(
            vmem_limit_bytes=56 << 20, collective_id=2, has_side_effects=True
        ),
        cost_estimate=pl.CostEstimate(
            flops=40 * rows * rows * 128 * pairs,
            bytes_accessed=26 * rows * 768,
            transcendentals=4 * rows * rows * pairs,
        ),
        name="attend_back",
    )(q, do, mix, kv, kv_sib, kv, kv_sib, bias, lse, *sources)


def normalize(hidden, scale_row, shift_row):
    centred = hidden - jnp.mean(hidden, axis=-1, keepdims=True)
    inverse = lax.rsqrt(jnp.mean(centred * centred, axis=-1, keepdims=True) + epsilon)
    standard = centred * inverse
    return (standard * scale_row + shift_row, standard, inverse)


def normalize_back(gradient, standard, inverse, scale_row):
    scaled = gradient * scale_row
    centred = scaled - jnp.mean(scaled, axis=-1, keepdims=True)
    return (centred - standard * jnp.mean(scaled * standard, axis=-1, keepdims=True)) * inverse


def on_device(
    tokens, cotangent, lengths, w_query, w_key, w_value, w_attn_out, w_up, b_up, w_down, vectors
):
    seqs, rows_dev, width = tokens.shape
    dp = lax.axis_size("dp")
    ctx = lax.axis_size("ctx")
    half = rows_dev // 2
    rows = half * ctx
    member = lax.axis_index("ctx") % 2
    own_seq = lax.axis_index("dp") * seqs + lax.axis_index("ctx") // 2
    length = lax.dynamic_index_in_dim(lengths, own_seq, 0, keepdims=False)
    pair_perm = [(i, i ^ 1) for i in range(ctx)]

    def exchange(array):
        return lax.all_to_all(array, "ctx", 0, 0, tiled=True)

    def over_pair(grad):
        parts = grad.astype(BF).reshape(dp, ctx // 2, 2, -1, grad.shape[1])
        keep = lax.dynamic_index_in_dim(parts, member, 2, keepdims=False)
        send = lax.dynamic_index_in_dim(parts, 1 - member, 2, keepdims=False)
        got = lax.ppermute(send, "ctx", pair_perm)
        return (keep.astype(F32) + got.astype(F32)).astype(BF)

    split = tokens.reshape(ctx, half, width)
    held = w_query.shape[0]
    extra = jnp.concatenate([vectors.T, b_up.reshape(held, -1)], axis=1)
    extra = jnp.pad(extra, ((0, 0), (0, 128 - extra.shape[1])))
    low_in, full_first, *over_dp = gather_first(
        split.astype(BF),
        jnp.concatenate([w_query, w_key, w_value, extra], axis=1),
        w_attn_out,
        w_up,
        w_down,
        dp,
        ctx,
    )
    low_in = low_in.reshape(rows, width)
    full_first = full_first.reshape(width, -1)
    full_qkv = full_first[:, : 3 * width]
    vector_rows = full_first[:, 3 * width : 3 * width + 8].T.astype(F32)
    bias_columns = b_up.shape[0] // held
    full_bias_up = full_first[:, 3 * width + 8 : 3 * width + 8 + bias_columns].reshape(-1).astype(F32)
    residual = exchange(split).reshape(rows, width)
    upstream = exchange(cotangent.reshape(ctx, half, width)).reshape(rows, width)

    slot = jnp.arange(rows, dtype=jnp.int32)
    source = slot // half
    high = (2 * ctx - 1 - source) * half + slot % half

    def key_bias(kind):
        position = jnp.where(kind == 0, slot, high)
        return jnp.where(position < length, 0.0, masked_score).astype(BF)

    bias = jnp.stack([key_bias(member), key_bias(1 - member)])
    bias = jnp.broadcast_to(bias[:, :, None], (2, rows, 128))

    row_of = jnp.concatenate([jnp.zeros_like(vector_rows[1]), vector_rows[1]])
    kv = (dg(low_in, full_qkv[:, width:], NN) + row_of).astype(BF)
    kv_sib = lax.ppermute(kv, "ctx", pair_perm)
    queries = (dg(low_in, full_qkv[:, :width], NN) + vector_rows[0]).astype(BF)
    low_mixed, mixed, lse, full_attn, full_up, full_down = attention_forward(
        queries, kv, kv_sib, bias, over_dp, dp, ctx
    )
    full_attn = full_attn.reshape(width, width)
    full_up = full_up.reshape(width, -1)
    full_down = full_down.reshape(-1, width)

    attention = dg(low_mixed, full_attn, NN) + vector_rows[2]
    normed_one, standard_one, inverse_one = normalize(
        residual + attention, vector_rows[6], vector_rows[4]
    )
    low_first = normed_one.astype(BF)
    inner = dg(low_first, full_up, NN) + full_bias_up
    active = jax.nn.gelu(inner, approximate=False).astype(BF)
    branch = dg(active, full_down, NN) + vector_rows[3]
    result, standard_two, inverse_two = normalize(
        normed_one + branch, vector_rows[7], vector_rows[5]
    )
    output = exchange(result.reshape(ctx, half, width)).reshape(seqs, rows_dev, width)

    d_gain_two = jnp.sum(upstream * standard_two, axis=0)
    d_shift_two = jnp.sum(upstream, axis=0)
    grad_second = normalize_back(upstream, standard_two, inverse_two, vector_rows[7])
    low_branch = grad_second.astype(BF)
    d_bias_down = jnp.sum(low_branch.astype(F32), axis=0)
    d_down = dg(active, low_branch, TN)
    d_active = dg(low_branch, full_down, NT)
    gelu_back = jax.vjp(lambda v: jax.nn.gelu(v, approximate=False), inner)[1]
    low_inner = gelu_back(d_active)[0].astype(BF)
    d_bias_up = jnp.sum(low_inner.astype(F32), axis=0)
    d_up = dg(low_first, low_inner, TN)
    part_down = over_pair(d_down)
    part_up = over_pair(d_up)
    grad_first = grad_second + dg(low_inner, full_up, NT)
    d_gain_one = jnp.sum(grad_first * standard_one, axis=0)
    d_shift_one = jnp.sum(grad_first, axis=0)
    grad_sum = normalize_back(grad_first, standard_one, inverse_one, vector_rows[6])
    low_attn = grad_sum.astype(BF)
    d_bias_attn = jnp.sum(low_attn.astype(F32), axis=0)
    d_attn = dg(low_mixed, low_attn, TN)
    d_mixed = dg(low_attn, full_attn, NT).astype(BF)

    d_vector_rows = jnp.stack(
        [d_bias_attn, d_bias_down, d_shift_one, d_shift_two, d_gain_one, d_gain_two]
    )
    extra = jnp.concatenate([d_vector_rows.T, d_bias_up.reshape(width, -1)], axis=1)
    extra = jnp.pad(extra, ((0, 0), (0, 128 - extra.shape[1])))
    part_attn = over_pair(jnp.concatenate([d_attn, extra], axis=1))
    dq, dk_own, dv_own, dk_sib, dv_sib, own_up, own_down, own_attn = attention_backward(
        queries, d_mixed, mixed, kv, kv_sib, bias, lse, [part_up, part_down, part_attn], dp, ctx
    )
    dk_got = lax.ppermute(dk_sib, "ctx", pair_perm)
    dv_got = lax.ppermute(dv_sib, "ctx", pair_perm)
    dk = (dk_own + dk_got.astype(F32)).astype(BF)
    dv = (dv_own + dv_got.astype(F32)).astype(BF)
    grad_in = grad_sum + (
        dg(dq, full_qkv[:, :width], NT)
        + dg(dk, full_qkv[:, width : 2 * width], NT)
        + dg(dv, full_qkv[:, 2 * width :], NT)
    )
    sums = jnp.stack([jnp.sum(dq.astype(F32), axis=0), jnp.sum(dv.astype(F32), axis=0)])
    sums = jnp.pad(sums.T, ((0, 0), (0, 126)))
    part = over_pair(
        jnp.concatenate([dg(low_in, dq, TN), dg(low_in, dk, TN), dg(low_in, dv, TN), sums], axis=1)
    )
    own, grad_tokens = finish_gradients(
        part, grad_in.astype(BF).reshape(ctx, half, width), dp, ctx
    )
    grad_tokens = grad_tokens.astype(F32).reshape(seqs, rows_dev, width)
    own_query, own_key, own_value = (own[:, i * width : (i + 1) * width] for i in range(3))
    own_vectors = jnp.concatenate(
        [own[:, 3 * width : 3 * width + 2], own_attn[:, width : width + 6]], axis=1
    ).T
    own_bias_up = own_attn[:, width + 6 : width + 6 + bias_columns].reshape(-1)
    own_attn = own_attn[:, :width]
    return (
        output,
        grad_tokens,
        own_query,
        own_key,
        own_value,
        own_attn,
        own_up,
        own_bias_up,
        own_down,
        own_vectors,
    )


def solution(mesh):
    in_specs = (
        P("dp", "ctx", None),
        P("dp", "ctx", None),
        P(),
        P(("dp", "ctx"), None),
        P(("dp", "ctx"), None),
        P(("dp", "ctx"), None),
        P(("dp", "ctx"), None),
        P(("dp", "ctx"), None),
        P(("dp", "ctx")),
        P(("dp", "ctx"), None),
        P(None, ("dp", "ctx")),
    )
    out_specs = (
        P("dp", "ctx", None),
        P("dp", "ctx", None),
        P(("dp", "ctx"), None),
        P(("dp", "ctx"), None),
        P(("dp", "ctx"), None),
        P(("dp", "ctx"), None),
        P(("dp", "ctx"), None),
        P(("dp", "ctx")),
        P(("dp", "ctx"), None),
        P(None, ("dp", "ctx")),
    )
    return jax.shard_map(
        on_device, mesh=mesh, in_specs=in_specs, out_specs=out_specs, check_vma=False
    )
```

time: 683 us -> 542 us (0.79)
  Pallas kernels: 133 us -> 321 us
  waiting for transfers between devices: 179 us -> 8.44 us
  blocking collectives: 76.2 us -> 0 us
  starting transfers between devices: 56.9 us -> 16.4 us
  local copies, waits for them, and re-layouts: 39.9 us -> 26.4 us
  between operations: 14.6 us -> 1.68 us
  other arithmetic: 45.5 us -> 33.2 us
    pallas_call x2 -> x4, Pallas kernels: 133 us -> 321 us  [the longest x1 117 us: attention_backward(): pl.pallas_call(functools.partial(backward_kernel, dp, ctx, ck), grid=(pai...]
    all_to_all x6 -> x0, waiting for transfers between devices: 87.2 us -> none  [the longest x3 55 us: reduce_blocks(): lax.all_to_all(part, 'ctx', 1, 1, axis_index_groups=groups, tiled=True)]
    all_gather x1 -> x0, blocking collectives: 76.2 us -> none  [collect(): return lax.all_gather(array, ('dp', 'ctx'), axis=axis, tiled=True)]
    all_gather x4 -> x0, waiting for transfers between devices: 46.1 us -> none  [collect(): return lax.all_gather(array, ('dp', 'ctx'), axis=axis, tiled=True)]
    all_to_all x5 -> x3, waiting for transfers between devices: 43.7 us -> 8.42 us  [exchange(): return lax.all_to_all(array, 'ctx', 0, 0, tiled=True)]
    all_to_all x6 -> x0, starting transfers between devices: 28.9 us -> none  [the longest x3 16.4 us: reduce_blocks(): lax.all_to_all(part, 'ctx', 1, 1, axis_index_groups=groups, tiled=True)]
    reduce_sum x6 -> x0, other arithmetic: 14.1 us -> none  [the longest x3 9.14 us: reduce_blocks(): part = jnp.sum(got.astype(F32), axis=1).astype(BF)]
    all_to_all x5 -> x3, starting transfers between devices: 26.6 us -> 14.5 us  [exchange(): return lax.all_to_all(array, 'ctx', 0, 0, tiled=True)]
  transfers between devices with their start and end apart: 21 -> 10, of which waited for: 10 -> 1; matrix products, arithmetic and copies ran while one was open for 26% -> 14% of each run, Pallas kernels for 20% -> 30%
where the time goes in v2:
time: 542 us; the launch traced here: 538 us
  Pallas kernels  321 us (59%)
  matrix products  131 us (24%)
  other arithmetic  33.2 us (6%)
  local copies, waits for them, and re-layouts  26.4 us (5%)
  starting transfers between devices  16.4 us (3%)
  waiting for transfers between devices  8.44 us (2%)
    dot_general x17, matrix products, dg(): return lax.dot_general(left, right, dims, preferred_element_type=F32)  131 us
    pallas_call x1, Pallas kernels, attention_backward(): pl.pallas_call(functools.partial(backward_kernel, dp, ctx, ck), grid=(pai...  117 us
    pallas_call x1, Pallas kernels, attention_forward(): pl.pallas_call(functools.partial(forward_kernel, dp, ctx), grid=(pairs, r...  88.1 us
    pallas_call x1, Pallas kernels, gather_first(): pl.pallas_call(functools.partial(gather_kernel, dp, ctx), in_specs=[any_s...  72.8 us
    pallas_call x1, Pallas kernels, finish_gradients(): pl.pallas_call(functools.partial(finish_kernel, dp, ctx), in_specs=[any_s...  43.4 us
    all_to_all x3, starting transfers between devices, exchange(): return lax.all_to_all(array, 'ctx', 0, 0, tiled=True)  14.5 us
    unnamed x107, local copies, waits for them, and re-layouts  12.4 us
    convert_element_type x4, other arithmetic, over_pair(): return (keep.astype(F32) + got.astype(F32)).astype(BF)  11.5 us
  transfers between devices with their start and end apart: 10, of which 1 were waited for; matrix products, arithmetic and copies ran while one was open for 14% of the time, Pallas kernels for 30%

profile of v2, /device:TPU:1, one launch (start us, length us, event | category | flops | bytes accessed | tf_op | source)
XLA Modules:
  0.0 538.1 jit_solution(8838723670186577813)
XLA Ops:
  0.7 5.4 all-to-all-start.2
  10.2 72.8 %gather_first.1 = (bf16[8,128,768]{2,1,0:T(8,128)(2,1)}, bf16[4,8,24,2432]{3,2,1,0:T(8,128)(2,1)}, bf16[4,24,768]{2,1,0:T(8,128)(2,1)}, bf16[4,24,3072]{2,1,0:T(8,128)(2,1)}, bf16[4,96,768]{2,1,0:T(8,128)(2,1)}) custom-call(bf16[8,128,768]{2,1,0:T(8,128)(2,1)} %convert_element_type.158.x, bf16[24,2432]{1,0:T(8,128)(2,1)} %pad_maximum_fusion.1.w, ...), custom_call_target="tpu_custom_call" | custom-call | tf_op jit(solution)/shard_map/gather_first/pallas_call | solution.py:120
  84.8 6.4 %add_convert_fusion.1.refs_1_.refs_3_.refs_5_ = bf16[1024,1536]{1,0:T(8,128)(2,1)} fusion(bf16[1024,768]{1,0:T(8,128)(2,1)} %bitcast.138, f32[1536]{0:T(1024)S(1)} %concatenate.34, bf16[768,2432]{1,0:T(8,128)(2,1)} %bitcast.130), kind=kOutput, calls=%fused_computation.17 | convolution fusion | flops 2419064832 | bytes 7084032 | tf_op jit(solution)/shard_map/dot_general | solution.py:20
  91.4 4.9 all-to-all-start
  100.1 4.4 add_convert_fusion.5.refs_0_
  105.8 88.1 %attend.1 = (bf16[1024,768]{1,0:T(8,128)(2,1)S(1)}, f32[1024,768]{1,0:T(8,128)}, f32[6,8,1024]{2,1,0:T(8,128)S(1)}, bf16[4,8,24,768]{3,2,1,0:T(8,128)(2,1)S(1)},...) custom-call(bf16[1024,768]{1,0:T(8,128)(2,1)} %add_convert_fusion.5.refs_0_, ...), custom_call_target="tpu_custom_call" | custom-call | flops 12884901888 | bytes 11010048 | tf_op jit(solution)/shard_map/attend/pallas_call | solution.py:364
  195.4 4.4 fusion.63
  200.9 35.2 %multiply_convert_fusion = (bf16[1024,3072]{1,0:T(8,128)(2,1)S(1)}, f32[1024,3072]{1,0:T(8,128)}, f32[1024,3072]{1,0:T(8,128)}) fusion(f32[3072]{0:T(1024)S(1)} %copy-done.37, bf16[768,3072]{1,0:T(8,128)(2,1)S(1)} %bitcast.150, f32[1024,768]{1,0:T(8,128)S(1)} %get-tuple-element.111, f32[768]{0:T(1024)S(1)} %get-tuple-element.93, ...), kind=kOutput, calls=%fused_computation.3 | convolution fusion | flops 5043388416 | bytes 39348224 | tf_op jit(solution)/shard_map/dot_general | solution.py:20
  236.1 5.5 %fusion.64 = (f32[1024]{0:T(1024)S(1)}, f32[1024,768]{1,0:T(8,128)S(1)}) fusion(f32[768]{0:T(1024)S(1)} %copy-done.39, bf16[1024,3072]{1,0:T(8,128)(2,1)S(1)} %get-tuple-element.104, bf16[3072,768]{1,0:T(8,128)(2,1)S(1)} %bitcast.154, f32[768]{0:T(1024)S(1)} %get-tuple-element.93, f32[768]{0:T(1024)S(1)} %get-tuple-element.94, ...), kind=kOutput, calls=%fused_computation.139 | convolution fusion | flops 4837342208 | bytes 17323008 | tf_op jit(solution)/shard_map/dot_general | solution.py:20
  247.8 7.0 %convolution_convert_fusion = bf16[3072,768]{1,0:T(8,128)(2,1)} fusion(bf16[1024,3072]{1,0:T(8,128)(2,1)S(1)} %get-tuple-element.104, f32[1024,768]{1,0:T(8,128)S(1)} %get-tuple-element.101), kind=kOutput, calls=%fused_computation.18 | convolution fusion | flops 4834983936 | bytes 14155776 | tf_op jit(solution)/shard_map/dot_general | solution.py:20
  254.9 19.3 %fusion.65 = (bf16[3072]{0:T(1024)(128)(2,1)S(1)}, bf16[1024,3072]{1,0:T(8,128)(2,1)}) fusion(f32[1024,3072]{1,0:T(8,128)} %get-tuple-element.105, bf16[3072,768]{1,0:T(8,128)(2,1)} %bitcast.151, f32[1024,768]{1,0:T(8,128)} %copy-done.26, f32[1024,3072]{1,0:T(8,128)} %get-tuple-element.112, f32[3072]{0:T(1024)S(1)} %copy-done.37), kind=kOutput, calls=%fused_computation.140 | convolution fusion | flops 4882953216 | bytes 39340032 | tf_op jit(solution)/shard_map/dot_general | solution.py:20
  274.2 10.2 %multiply_reduce_fusion = (bf16[768]{0:T(1024)(128)(2,1)S(1)}, f32[1024]{0:T(1024)S(1)}, f32[1024]{0:T(1024)S(1)}, bf16[768]{0:T(1024)(128)(2,1)S(1)}, f32[1024,768]{1,0:T(8,128)S(1)}) fusion(f32[1024,768]{1,0:T(8,128)S(1)} %copy-done.16, f32[1024]{0:T(1024)S(1)} %add_rsqrt_fusion.1, f32[1024]{0:T(1024)S(1)} %broadcast_multiply_fusion.4, ...), kind=kOutput, calls=%fused_computation.34 | convolution fusion | flops 4839698432 | bytes 20469760 | tf_op jit(solution)/shard_map/dot_general | solution.py:20
  284.4 6.5 %convolution_convert_fusion.1 = bf16[768,3072]{1,0:T(8,128)(2,1)S(1)} fusion(bf16[1024,3072]{1,0:T(8,128)(2,1)S(1)} %copy-done.43, f32[1024,768]{1,0:T(8,128)S(1)} %copy-done.16, f32[768]{0:T(1024)S(1)} %get-tuple-element.93, f32[768]{0:T(1024)S(1)} %get-tuple-element.94, f32[1024]{0:T(1024)S(1)} %add_rsqrt_fusion.1, f32[1024]{0:T(1024)S(1)} %broadcast_multiply_fusion.4), kind=kOutput, calls=%fused_computation.19 | convolution fusion | flops 4838129664 | bytes 14170112 | tf_op jit(solution)/shard_map/dot_general | solution.py:20
  304.2 4.6 convolution_convert_fusion.2.refs_1_
  309.9 4.5 fusion.6.refs_10_
  314.4 4.0 fusion.7.refs_9_
  318.4 116.7 %attend_back.1 = (bf16[1024,768]{1,0:T(8,128)(2,1)}, f32[1024,768]{1,0:T(8,128)}, f32[1024,768]{1,0:T(8,128)}, bf16[1024,768]{1,0:T(8,128)(2,1)}, bf16[1024,768]...) custom-call(bf16[1024,768]{1,0:T(8,128)(2,1)} %add_convert_fusion.5.refs_0_, ...), custom_call_target="tpu_custom_call" | custom-call | flops 32212254720 | bytes 20447232 | tf_op jit(solution)/shard_map/attend_back/pallas_call | solution.py:493
  437.8 4.2 all-to-all-start.1
  443.8 4.5 fusion.18
  451.7 3.4 fusion.24
  463.2 4.8 fusion.37
  468.0 8.4 %all-to-all-done.1 = f32[8,128,768]{2,1,0:T(8,128)S(1)} async-done(((f32[8,128,768]{2,1,0:T(8,128)}), f32[8,128,768]{2,1,0:T(8,128)S(1)}, u32[]{:S(2)}, u32[]{:S(2)}) %all-to-all-start.1) | async-done | bytes 3145760 | tf_op jit(solution)/shard_map/all_to_all | solution.py:560
  476.4 5.3 fusion.33
  487.6 43.4 %finish_gradients.1 = (f32[24,2432]{1,0:T(8,128)S(1)}, bf16[8,128,768]{2,1,0:T(8,128)(2,1)S(1)}) custom-call(bf16[4,4,24,2432]{3,2,1,0:T(8,128)(2,1)S(1)} %fusion.8.s, bf16[8,128,768]{2,1,0:T(8,128)(2,1)S(1)} %bitcast.112), custom_call_target="tpu_custom_call" | custom-call | tf_op jit(solution)/shard_map/finish_gradients/pallas_call | solution.py:275
  (192 shorter events, 62.5 us)
Async XLA Ops:
  0.7 5.7 %copy-start.34 = (bf16[24,768]{1,0:T(8,128)(2,1)S(1)}, bf16[24,768]{1,0:T(8,128)(2,1)}, u32[]{:S(2)}) copy-start(bf16[24,768]{1,0:T(8,128)(2,1)} %param.16) | copy-start | bytes 110596
  0.7 90.7 %all-to-all-start.2 = ((f32[8,128,768]{2,1,0:T(8,128)}), f32[8,128,768]{2,1,0:T(8,128)S(1)}, u32[]{:S(2)}, u32[]{:S(2)}) async-start(f32[8,128,768]{2,1,0:T(8,128)} %bitcast.128), calls=%async_computation.2 | async-start | bytes 6291456 | tf_op jit(solution)/shard_map/all_to_all | solution.py:560
  91.2 14.3 %collective-permute-start = (bf16[1024,1536]{1,0:T(8,128)(2,1)}, bf16[1024,1536]{1,0:T(8,128)(2,1)}, u32[]{:S(2)}, u32[]{:S(2)}) collective-permute-start(bf16[1024,1536]{1,0:T(8,128)(2,1)} %add_convert_fusion.1.refs_1_.refs_3_.refs_5_), channel_id=1, source_target_pairs={{0,1},{1,0},{2,3},{3,2},{4,5},{5,4},{6,7},{7,6},{8,9},{9,8},{10,11... | collective-permute-start | bytes 9437192 | tf_op jit(solution)/shard_map/ppermute | solution.py:604
  91.4 13.1 %copy-start.9 = (f32[8,128,768]{2,1,0:T(8,128)}, f32[8,128,768]{2,1,0:T(8,128)S(1)}, u32[]{:S(2)}) copy-start(f32[8,128,768]{2,1,0:T(8,128)S(1)} %all-to-all-done.2) | copy-start | bytes 9437188
  91.4 104.1 %all-to-all-start = ((f32[8,128,768]{2,1,0:T(8,128)}), f32[8,128,768]{2,1,0:T(8,128)}, u32[]{:S(2)}, u32[]{:S(2)}) async-start(f32[8,128,768]{2,1,0:T(8,128)} %bitcast.117), calls=%async_computation | async-start | bytes 6291456 | tf_op jit(solution)/shard_map/all_to_all | solution.py:560
  105.8 89.6 %copy-start.40 = (f32[768]{0:T(1024)S(1)}, f32[768]{0:T(1024)}, u32[]{:S(2)}) copy-start(f32[768]{0:T(1024)} %get-tuple-element.95) | copy-start | bytes 9220
  195.4 40.6 %slice-start.4 = ((s8[4718592]{0:T(1024)(128)(4,1)}), s8[4194304]{0:T(1024)(128)(4,1)S(1)}, s32[]{:S(2)}) async-start(s8[4718592]{0:T(1024)(128)(4,1)} %bitcast.152), calls=%async_computation.7 | async-start | bytes 8388608
  199.9 36.2 %copy-start.15 = (f32[1024,768]{1,0:T(8,128)}, f32[1024,768]{1,0:T(8,128)S(1)}, u32[]{:S(2)}) copy-start(f32[1024,768]{1,0:T(8,128)S(1)} %get-tuple-element.111) | copy-start | bytes 9437188
  200.9 35.2 %copy-start.39 = (f32[768]{0:T(1024)S(1)}, f32[768]{0:T(1024)}, u32[]{:S(2)}) copy-start(f32[768]{0:T(1024)} %get-tuple-element.92) | copy-start | bytes 9220
  200.9 35.2 %slice-start.5 = ((s8[4718592]{0:T(1024)(128)(4,1)}), s8[524288]{0:T(1024)(128)(4,1)S(1)}, s32[]{:S(2)}) async-start(s8[4718592]{0:T(1024)(128)(4,1)} %bitcast.152), calls=%async_computation.8 | async-start | bytes 1048576
  247.8 7.0 %copy-start.26 = (f32[1024,768]{1,0:T(8,128)}, f32[1024,768]{1,0:T(8,128)S(1)}, u32[]{:S(2)}) copy-start(f32[1024,768]{1,0:T(8,128)S(1)} %get-tuple-element.101) | copy-start | bytes 9437188
  254.9 19.3 %copy-start.16 = (f32[1024,768]{1,0:T(8,128)S(1)}, f32[1024,768]{1,0:T(8,128)}, u32[]{:S(2)}) copy-start(f32[1024,768]{1,0:T(8,128)} %copy-done.15) | copy-start | bytes 9437188
  274.2 10.2 %copy-start.43 = (bf16[1024,3072]{1,0:T(8,128)(2,1)S(1)}, bf16[1024,3072]{1,0:T(8,128)(2,1)}, u32[]{:S(2)}) copy-start(bf16[1024,3072]{1,0:T(8,128)(2,1)} %get-tuple-element.117) | copy-start | bytes 18874372
  284.4 6.5 %copy-start.20 = (bf16[3072,768]{1,0:T(8,128)(2,1)S(1)}, bf16[3072,768]{1,0:T(8,128)(2,1)}, u32[]{:S(2)}) copy-start(bf16[3072,768]{1,0:T(8,128)(2,1)} %convolution_convert_fusion) | copy-start | bytes 14155780
  292.7 17.2 %collective-permute-start.2 = (bf16[4,4,96,768]{3,2,1,0:T(8,128)(2,1)}, bf16[4,4,96,768]{3,2,1,0:T(8,128)(2,1)}, u32[]{:S(2)}, u32[]{:S(2)}) collective-permute-start(bf16[4,4,96,768]{3,2,1,0:T(8,128)(2,1)} %dynamic-slice_bitcast_fusion), channel_id=1, source_target_pairs={{0,1},{1,0},{2,3},{3,2},{4,5},{5,4},{6,7},{7,6},{8,9},{9,8},{10,11... | collective-permute-start | bytes 7077896 | tf_op jit(solution)/shard_map/ppermute | solution.py:566
  294.6 19.8 %collective-permute-start.1 = (bf16[4,4,24,3072]{3,2,1,0:T(8,128)(2,1)}, bf16[4,4,24,3072]{3,2,1,0:T(8,128)(2,1)}, u32[]{:S(2)}, u32[]{:S(2)}) collective-permute-start(bf16[4,4,24,3072]{3,2,1,0:T(8,128)(2,1)} %dynamic-slice_bitcast_fusion.1), channel_id=1, source_target_pairs={{0,1},{1,0},{2,3},{3,2},{4,5},{5,4},{6,7},{7,6},{8,9},{9,8},{10,11... | collective-permute-start | bytes 7077896 | tf_op jit(solution)/shard_map/ppermute | solution.py:566
  303.9 4.9 collective-permute-start.3
  304.2 10.2 %slice-start = ((s8[4718592]{0:T(1024)(128)(4,1)}), s8[4194304]{0:T(1024)(128)(4,1)S(1)}, s32[]{:S(2)}) async-start(s8[4718592]{0:T(1024)(128)(4,1)} %bitcast.123), calls=%async_computation.3 | async-start | bytes 8388608
  318.4 117.8 %copy-start.28 = (bf16[8,128,768]{2,1,0:T(8,128)(2,1)S(1)}, bf16[8,128,768]{2,1,0:T(8,128)(2,1)}, u32[]{:S(2)}) copy-start(bf16[8,128,768]{2,1,0:T(8,128)(2,1)} %get-tuple-element.31) | copy-start | bytes 4718596
  435.1 13.2 %collective-permute-start.5 = (bf16[1024,768]{1,0:T(8,128)(2,1)}, bf16[1024,768]{1,0:T(8,128)(2,1)}, u32[]{:S(2)}, u32[]{:S(2)}) collective-permute-start(bf16[1024,768]{1,0:T(8,128)(2,1)} %get-tuple-element.46), channel_id=1, source_target_pairs={{0,1},{1,0},{2,3},{3,2},{4,5},{5,4},{6,7},{7,6},{8,9},{9,8},{10,11... | collective-permute-start | bytes 4718600 | tf_op jit(solution)/shard_map/ppermute | solution.py:658
  436.1 19.0 %collective-permute-start.4 = (bf16[1024,768]{1,0:T(8,128)(2,1)}, bf16[1024,768]{1,0:T(8,128)(2,1)}, u32[]{:S(2)}, u32[]{:S(2)}) collective-permute-start(bf16[1024,768]{1,0:T(8,128)(2,1)} %get-tuple-element.44), channel_id=1, source_target_pairs={{0,1},{1,0},{2,3},{3,2},{4,5},{5,4},{6,7},{7,6},{8,9},{9,8},{10,11... | collective-permute-start | bytes 4718600 | tf_op jit(solution)/shard_map/ppermute | solution.py:657
  437.8 38.6 %all-to-all-start.1 = ((f32[8,128,768]{2,1,0:T(8,128)}), f32[8,128,768]{2,1,0:T(8,128)S(1)}, u32[]{:S(2)}, u32[]{:S(2)}) async-start(f32[8,128,768]{2,1,0:T(8,128)} %bitcast.119), calls=%async_computation.1 | async-start | bytes 6291456 | tf_op jit(solution)/shard_map/all_to_all | solution.py:560
  461.7 23.9 %collective-permute-start.6 = (bf16[4,4,24,2432]{3,2,1,0:T(8,128)(2,1)}, bf16[4,4,24,2432]{3,2,1,0:T(8,128)(2,1)}, u32[]{:S(2)}, u32[]{:S(2)}) collective-permute-start(bf16[4,4,24,2432]{3,2,1,0:T(8,128)(2,1)} %dynamic-slice_bitcast_fusion.2), channel_id=1, source_target_pairs={{0,1},{1,0},{2,3},{3,2},{4,5},{5,4},{6,7},{7,6},{8,9},{9,8},{10,11... | collective-permute-start | bytes 5603336 | tf_op jit(solution)/shard_map/ppermute | solution.py:566
  476.4 6.2 %copy-start.27 = (f32[1024,768]{1,0:T(8,128)S(1)}, f32[1024,768]{1,0:T(8,128)}, u32[]{:S(2)}) copy-start(f32[1024,768]{1,0:T(8,128)} %fusion.37) | copy-start | bytes 9437188
  (36 other events, 123.0 us)

commit v3 on v2

--- a/solution.py
+++ b/solution.py
@@ -395,7 +395,7 @@
 
 def backward_steps(pairs, steps):
     count = pairs * steps
-    return (count * 8 // 16, count * 3 // 16, count * 13 // 16)
+    return (count * 7 // 12, count * 8 // 12, count * 9 // 12)
 
 
 def backward_kernel(dp, ctx, ck, *refs):
@@ -585,8 +585,10 @@
     vector_rows = full_first[:, 3 * width : 3 * width + 8].T.astype(F32)
     bias_columns = b_up.shape[0] // held
     full_bias_up = full_first[:, 3 * width + 8 : 3 * width + 8 + bias_columns].reshape(-1).astype(F32)
-    residual = exchange(split).reshape(rows, width)
-    upstream = exchange(cotangent.reshape(ctx, half, width)).reshape(rows, width)
+    left_out, low_in = lax.optimization_barrier(
+        ((split - split.astype(BF).astype(F32)).astype(BF), low_in)
+    )
+    residual = low_in.astype(F32) + exchange(left_out).reshape(rows, width).astype(F32)
 
     slot = jnp.arange(rows, dtype=jnp.int32)
     source = slot // half
@@ -606,6 +608,8 @@
     low_mixed, mixed, lse, full_attn, full_up, full_down = attention_forward(
         queries, kv, kv_sib, bias, over_dp, dp, ctx
     )
+    late, low_mixed = lax.optimization_barrier((cotangent, low_mixed))
+    upstream = exchange(late.reshape(ctx, half, width)).reshape(rows, width)
     full_attn = full_attn.reshape(width, width)
     full_up = full_up.reshape(width, -1)
     full_down = full_down.reshape(-1, width)
@@ -645,6 +649,7 @@
     d_attn = dg(low_mixed, low_attn, TN)
     d_mixed = dg(low_attn, full_attn, NT).astype(BF)
 
+    output, d_mixed = lax.optimization_barrier((output, d_mixed))
     d_vector_rows = jnp.stack(
         [d_bias_attn, d_bias_down, d_shift_one, d_shift_two, d_gain_one, d_gain_two]
     )

time: 542 us -> 481 us (0.89)
  Pallas kernels: 321 us -> 249 us
  waiting for transfers between devices: 8.44 us -> 15.2 us
    pallas_call x1, Pallas kernels: 117 us -> 86 us  [attention_backward(): pl.pallas_call(functools.partial(backward_kernel, dp, ctx, ck), grid=(pai...]
    pallas_call x1, Pallas kernels: 72.8 us -> 47.6 us  [gather_first(): pl.pallas_call(functools.partial(gather_kernel, dp, ctx), in_specs=[any_s...]
    pallas_call x1, Pallas kernels: 88.1 us -> 73.5 us  [attention_forward(): pl.pallas_call(functools.partial(forward_kernel, dp, ctx), grid=(pairs, r...]
    all_to_all x3, waiting for transfers between devices: 8.42 us -> 15.2 us  [exchange(): return lax.all_to_all(array, 'ctx', 0, 0, tiled=True)]
    unnamed x107 -> x93, local copies, waits for them, and re-layouts: 12.4 us -> 15.9 us
  transfers between devices with their start and end apart: 10 -> 10, of which waited for: 1 -> 1; matrix products, arithmetic and copies ran while one was open for 14% -> 21% of each run, Pallas kernels for 30% -> 16%
where the time goes in v3:
time: 481 us; the launch traced here: 474 us
  Pallas kernels  249 us (52%)
  matrix products  133 us (28%)
  other arithmetic  32.3 us (7%)
  local copies, waits for them, and re-layouts  25.9 us (5%)
  starting transfers between devices  16.9 us (4%)
  waiting for transfers between devices  15.2 us (3%)
    dot_general x17, matrix products, dg(): return lax.dot_general(left, right, dims, preferred_element_type=F32)  133 us
    pallas_call x1, Pallas kernels, attention_backward(): pl.pallas_call(functools.partial(backward_kernel, dp, ctx, ck), grid=(pai...  86 us
    pallas_call x1, Pallas kernels, attention_forward(): pl.pallas_call(functools.partial(forward_kernel, dp, ctx), grid=(pairs, r...  73.5 us
    pallas_call x1, Pallas kernels, gather_first(): pl.pallas_call(functools.partial(gather_kernel, dp, ctx), in_specs=[any_s...  47.6 us
    pallas_call x1, Pallas kernels, finish_gradients(): pl.pallas_call(functools.partial(finish_kernel, dp, ctx), in_specs=[any_s...  42 us
    unnamed x93, local copies, waits for them, and re-layouts  15.9 us
    all_to_all x3, waiting for transfers between devices, exchange(): return lax.all_to_all(array, 'ctx', 0, 0, tiled=True)  15.2 us
    all_to_all x3, starting transfers between devices, exchange(): return lax.all_to_all(array, 'ctx', 0, 0, tiled=True)  13.4 us
  transfers between devices with their start and end apart: 10, of which 1 were waited for; matrix products, arithmetic and copies ran while one was open for 21% of the time, Pallas kernels for 16%

profile of v3, /device:TPU:1, one launch (start us, length us, event | category | flops | bytes accessed | tf_op | source)
XLA Modules:
  0.0 473.8 jit_solution(3882636202255060813)
XLA Ops:
  0.7 5.2 %subtract_convert_fusion = (bf16[8,128,768]{2,1,0:T(8,128)(2,1)}, bf16[8,128,768]{2,1,0:T(8,128)(2,1)}) fusion(f32[8,128,768]{2,1,0:T(8,128)} %bitcast.113), kind=kLoop, calls=%fused_computation.47 | loop fusion | flops 3145728 | bytes 6291456 | tf_op jit(solution)/shard_map/convert_element_type | solution.py:589
  6.8 47.6 %gather_first.1 = (bf16[8,128,768]{2,1,0:T(8,128)(2,1)}, bf16[4,8,24,2432]{3,2,1,0:T(8,128)(2,1)}, bf16[4,24,768]{2,1,0:T(8,128)(2,1)}, bf16[4,24,3072]{2,1,0:T(8,128)(2,1)}, bf16[4,96,768]{2,1,0:T(8,128)(2,1)}) custom-call(bf16[8,128,768]{2,1,0:T(8,128)(2,1)} %get-tuple-element.119.x, bf16[24,2432]{1,0:T(8,128)(2,1)} %pad_maximum_fusion.1.w, ...), custom_call_target="tpu_custom_call" | custom-call | tf_op jit(solution)/shard_map/gather_first/pallas_call | solution.py:120
  55.6 6.4 %add_convert_fusion.1.refs_1_.refs_3_.refs_5_ = bf16[1024,1536]{1,0:T(8,128)(2,1)} fusion(bf16[1024,768]{1,0:T(8,128)(2,1)} %bitcast.130, f32[1536]{0:T(1024)S(1)} %concatenate.40, bf16[768,2432]{1,0:T(8,128)(2,1)} %bitcast.116), kind=kOutput, calls=%fused_computation.17 | convolution fusion | flops 2419064832 | bytes 7084032 | tf_op jit(solution)/shard_map/dot_general | solution.py:20
  62.2 4.5 all-to-all-start
  68.4 4.4 add_convert_fusion.5.refs_0_
  74.1 73.5 %attend.1 = (bf16[1024,768]{1,0:T(8,128)(2,1)S(1)}, f32[1024,768]{1,0:T(8,128)}, f32[6,8,1024]{2,1,0:T(8,128)S(1)}, bf16[4,8,24,768]{3,2,1,0:T(8,128)(2,1)S(1)},...) custom-call(bf16[1024,768]{1,0:T(8,128)(2,1)} %add_convert_fusion.5.refs_0_, ...), custom_call_target="tpu_custom_call" | custom-call | flops 12884901888 | bytes 11010048 | tf_op jit(solution)/shard_map/attend/pallas_call | solution.py:364
  149.5 4.4 fusion.46
  156.1 3.9 all-to-all-start.2
  160.0 38.0 %multiply_convert_fusion = (bf16[1024,3072]{1,0:T(8,128)(2,1)S(1)}, f32[1024,3072]{1,0:T(8,128)}, f32[1024,3072]{1,0:T(8,128)}) fusion(f32[3072]{0:T(1024)S(1)} %reshape.269, bf16[768,3072]{1,0:T(8,128)(2,1)} %bitcast.136, f32[1024,768]{1,0:T(8,128)} %copy-done.13, f32[768]{0:T(1024)S(1)} %get-tuple-element.105, f32[768]{0:T(1024)S(1)} %get-tuple-element.106, ...), kind=kOutput, calls=%fused_computation.3 | convolution fusion | flops 5043388416 | bytes 39348224 | tf_op jit(solution)/shard_map/dot_general | solution.py:20
  198.0 10.1 %fusion.47 = (f32[1024]{0:T(1024)S(1)}, f32[1024,768]{1,0:T(8,128)S(1)}) fusion(f32[768]{0:T(1024)S(1)} %get-tuple-element.104, bf16[1024,3072]{1,0:T(8,128)(2,1)S(1)} %get-tuple-element.116, bf16[3072,768]{1,0:T(8,128)(2,1)} %bitcast.138, f32[768]{0:T(1024)S(1)} %get-tuple-element.105, f32[768]{0:T(1024)S(1)} %get-tuple-element.106, ...), kind=kOutput, calls=%fused_computation.132 | convolution fusion | flops 4837342208 | bytes 17323008 | tf_op jit(solution)/shard_map/dot_general | solution.py:20
  209.8 4.2 fusion.10
  217.4 7.0 %convolution_convert_fusion = bf16[3072,768]{1,0:T(8,128)(2,1)} fusion(bf16[1024,3072]{1,0:T(8,128)(2,1)S(1)} %bitcast.141, f32[1024,768]{1,0:T(8,128)S(1)} %get-tuple-element.113), kind=kOutput, calls=%fused_computation.18 | convolution fusion | flops 4834983936 | bytes 14155776 | tf_op jit(solution)/shard_map/dot_general | solution.py:20
  224.4 19.0 %fusion.48 = (bf16[3072]{0:T(1024)(128)(2,1)S(1)}, bf16[1024,3072]{1,0:T(8,128)(2,1)}) fusion(f32[1024,3072]{1,0:T(8,128)} %get-tuple-element.117, bf16[3072,768]{1,0:T(8,128)(2,1)} %bitcast.139, f32[1024,768]{1,0:T(8,128)} %copy-done.24, f32[1024,3072]{1,0:T(8,128)} %get-tuple-element.126, f32[3072]{0:T(1024)S(1)} %reshape.269), kind=kOutput, calls=%fused_computation.133 | convolution fusion | flops 4882953216 | bytes 39340032 | tf_op jit(solution)/shard_map/dot_general | solution.py:20
  243.4 10.2 %multiply_reduce_fusion = (bf16[768]{0:T(1024)(128)(2,1)S(1)}, f32[1024]{0:T(1024)S(1)}, f32[1024]{0:T(1024)S(1)}, bf16[768]{0:T(1024)(128)(2,1)S(1)}, f32[1024,768]{1,0:T(8,128)S(1)}) fusion(f32[1024,768]{1,0:T(8,128)S(1)} %copy-done.15, f32[1024]{0:T(1024)S(1)} %add_rsqrt_fusion.1, f32[1024]{0:T(1024)S(1)} %broadcast_multiply_fusion.4, ...), kind=kOutput, calls=%fused_computation.35 | convolution fusion | flops 4839698432 | bytes 20469760 | tf_op jit(solution)/shard_map/dot_general | solution.py:20
  253.6 6.5 %convolution_convert_fusion.1 = bf16[768,3072]{1,0:T(8,128)(2,1)S(1)} fusion(bf16[1024,3072]{1,0:T(8,128)(2,1)S(1)} %copy-done.37, f32[1024,768]{1,0:T(8,128)S(1)} %copy-done.15, f32[768]{0:T(1024)S(1)} %get-tuple-element.105, f32[768]{0:T(1024)S(1)} %get-tuple-element.106, f32[1024]{0:T(1024)S(1)} %add_rsqrt_fusion.1, f32[1024]{0:T(1024)S(1)} %broadcast_multiply_fusion.4), kind=kOutput, calls=%fused_computation.19 | convolution fusion | flops 4838129664 | bytes 14170112 | tf_op jit(solution)/shard_map/dot_general | solution.py:20
  267.0 5.0 %all-to-all-start.1 = ((f32[8,128,768]{2,1,0:T(8,128)}), f32[8,128,768]{2,1,0:T(8,128)}, u32[]{:S(2)}, u32[]{:S(2)}) async-start(f32[8,128,768]{2,1,0:T(8,128)} %bitcast.104), calls=%async_computation.1 | async-start | bytes 6291456 | tf_op jit(solution)/shard_map/all_to_all | solution.py:560
  277.0 4.6 convolution_convert_fusion.2.refs_1_
  282.6 4.5 fusion.6.refs_10_
  287.2 4.0 fusion.7.refs_9_
  291.2 15.2 %all-to-all-done.1 = f32[8,128,768]{2,1,0:T(8,128)} async-done(((f32[8,128,768]{2,1,0:T(8,128)}), f32[8,128,768]{2,1,0:T(8,128)}, u32[]{:S(2)}, u32[]{:S(2)}) %all-to-all-start.1) | async-done | bytes 3145760 | tf_op jit(solution)/shard_map/all_to_all | solution.py:560
  306.3 86.0 %attend_back.1 = (bf16[1024,768]{1,0:T(8,128)(2,1)}, f32[1024,768]{1,0:T(8,128)}, f32[1024,768]{1,0:T(8,128)}, bf16[1024,768]{1,0:T(8,128)(2,1)}, bf16[1024,768]...) custom-call(bf16[1024,768]{1,0:T(8,128)(2,1)} %add_convert_fusion.5.refs_0_, ...), custom_call_target="tpu_custom_call" | custom-call | flops 32212254720 | bytes 20447232 | tf_op jit(solution)/shard_map/attend_back/pallas_call | solution.py:493
  396.4 4.5 convolution_convert_fusion.5
  422.7 42.0 %finish_gradients.1 = (f32[24,2432]{1,0:T(8,128)S(1)}, bf16[8,128,768]{2,1,0:T(8,128)(2,1)S(1)}) custom-call(bf16[4,4,24,2432]{3,2,1,0:T(8,128)(2,1)S(1)} %fusion.8.s, bf16[8,128,768]{2,1,0:T(8,128)(2,1)S(1)} %bitcast.100), custom_call_target="tpu_custom_call" | custom-call | tf_op jit(solution)/shard_map/finish_gradients/pallas_call | solution.py:275
  468.0 3.9 copy.77
  (176 shorter events, 57.3 us)
Async XLA Ops:
  0.7 5.5 %copy-start.30 = (bf16[24,768]{1,0:T(8,128)(2,1)S(1)}, bf16[24,768]{1,0:T(8,128)(2,1)}, u32[]{:S(2)}) copy-start(bf16[24,768]{1,0:T(8,128)(2,1)} %param.16) | copy-start | bytes 110596
  62.0 11.7 %collective-permute-start = (bf16[1024,1536]{1,0:T(8,128)(2,1)}, bf16[1024,1536]{1,0:T(8,128)(2,1)}, u32[]{:S(2)}, u32[]{:S(2)}) collective-permute-start(bf16[1024,1536]{1,0:T(8,128)(2,1)} %add_convert_fusion.1.refs_1_.refs_3_.refs_5_), channel_id=1, source_target_pairs={{0,1},{1,0},{2,3},{3,2},{4,5},{5,4},{6,7},{7,6},{8,9},{9,8},{10,11... | collective-permute-start | bytes 9437192 | tf_op jit(solution)/shard_map/ppermute | solution.py:606
  62.2 87.3 %all-to-all-start = ((bf16[8,128,768]{2,1,0:T(8,128)(2,1)}), bf16[8,128,768]{2,1,0:T(8,128)(2,1)}, u32[]{:S(2)}, u32[]{:S(2)}) async-start(bf16[8,128,768]{2,1,0:T(8,128)(2,1)} %get-tuple-element.39), calls=%async_computation | async-start | bytes 3145728 | tf_op jit(solution)/shard_map/all_to_all | solution.py:560
  68.3 5.7 %copy-start.1 = (bf16[4,24,3072]{2,1,0:T(8,128)(2,1)S(1)}, bf16[4,24,3072]{2,1,0:T(8,128)(2,1)}, u32[]{:S(2)}) copy-start(bf16[4,24,3072]{2,1,0:T(8,128)(2,1)} %get-tuple-element.42.refs_7_) | copy-start | bytes 1769476
  68.4 5.7 %copy-start.2 = (bf16[4,96,768]{2,1,0:T(8,128)(2,1)S(1)}, bf16[4,96,768]{2,1,0:T(8,128)(2,1)}, u32[]{:S(2)}) copy-start(bf16[4,96,768]{2,1,0:T(8,128)(2,1)} %get-tuple-element.43.refs_8_) | copy-start | bytes 1769476
  68.4 5.7 %copy-start.3 = (bf16[4,24,768]{2,1,0:T(8,128)(2,1)S(1)}, bf16[4,24,768]{2,1,0:T(8,128)(2,1)}, u32[]{:S(2)}) copy-start(bf16[4,24,768]{2,1,0:T(8,128)(2,1)} %get-tuple-element.41.refs_6_) | copy-start | bytes 442372
  74.1 73.5 %copy-start = (bf16[2,1024,128]{2,1,0:T(8,128)(2,1)}, bf16[2,1024,128]{2,1,0:T(8,128)(2,1)S(1)}, u32[]{:S(2)}) copy-start(bf16[2,1024,128]{2,1,0:T(8,128)(2,1)S(1)} %broadcast_in_dim.14.refs_5_.refs_7_) | copy-start | bytes 1572868
  156.1 53.7 %all-to-all-start.2 = ((f32[8,128,768]{2,1,0:T(8,128)}), f32[8,128,768]{2,1,0:T(8,128)S(1)}, u32[]{:S(2)}, u32[]{:S(2)}) async-start(f32[8,128,768]{2,1,0:T(8,128)} %bitcast.114), calls=%async_computation.2 | async-start | bytes 6291456 | tf_op jit(solution)/shard_map/all_to_all | solution.py:560
  160.0 38.0 %copy-start.14 = (f32[1024,768]{1,0:T(8,128)S(1)}, f32[1024,768]{1,0:T(8,128)}, u32[]{:S(2)}) copy-start(f32[1024,768]{1,0:T(8,128)} %copy-done.13) | copy-start | bytes 9437188
  198.0 10.1 %copy-start.38 = (bf16[1024,3072]{1,0:T(8,128)(2,1)}, bf16[1024,3072]{1,0:T(8,128)(2,1)S(1)}, u32[]{:S(2)}) copy-start(bf16[1024,3072]{1,0:T(8,128)(2,1)S(1)} %get-tuple-element.116) | copy-start | bytes 18874372
  209.8 7.6 %slice-start.2 = ((s8[6291456]{0:T(1024)(128)(4,1)}), s8[4194304]{0:T(1024)(128)(4,1)S(1)}, s32[]{:S(2)}) async-start(s8[6291456]{0:T(1024)(128)(4,1)} %bitcast.140), calls=%async_computation.5 | async-start | bytes 8388608
  217.3 7.1 %copy-start.24 = (f32[1024,768]{1,0:T(8,128)}, f32[1024,768]{1,0:T(8,128)S(1)}, u32[]{:S(2)}) copy-start(f32[1024,768]{1,0:T(8,128)S(1)} %get-tuple-element.113) | copy-start | bytes 9437188
  224.4 19.0 %copy-start.15 = (f32[1024,768]{1,0:T(8,128)S(1)}, f32[1024,768]{1,0:T(8,128)}, u32[]{:S(2)}) copy-start(f32[1024,768]{1,0:T(8,128)} %copy-done.13) | copy-start | bytes 9437188
  243.4 10.2 %copy-start.37 = (bf16[1024,3072]{1,0:T(8,128)(2,1)S(1)}, bf16[1024,3072]{1,0:T(8,128)(2,1)}, u32[]{:S(2)}) copy-start(bf16[1024,3072]{1,0:T(8,128)(2,1)} %get-tuple-element.131) | copy-start | bytes 18874372
  253.6 6.6 %copy-start.17 = (bf16[3072,768]{1,0:T(8,128)(2,1)S(1)}, bf16[3072,768]{1,0:T(8,128)(2,1)}, u32[]{:S(2)}) copy-start(bf16[3072,768]{1,0:T(8,128)(2,1)} %convolution_convert_fusion) | copy-start | bytes 14155780
  261.9 20.7 %collective-permute-start.2 = (bf16[4,4,96,768]{3,2,1,0:T(8,128)(2,1)}, bf16[4,4,96,768]{3,2,1,0:T(8,128)(2,1)}, u32[]{:S(2)}, u32[]{:S(2)}) collective-permute-start(bf16[4,4,96,768]{3,2,1,0:T(8,128)(2,1)} %dynamic-slice_bitcast_fusion), channel_id=1, source_target_pairs={{0,1},{1,0},{2,3},{3,2},{4,5},{5,4},{6,7},{7,6},{8,9},{9,8},{10,11... | collective-permute-start | bytes 7077896 | tf_op jit(solution)/shard_map/ppermute | solution.py:566
  263.8 23.4 %collective-permute-start.1 = (bf16[4,4,24,3072]{3,2,1,0:T(8,128)(2,1)}, bf16[4,4,24,3072]{3,2,1,0:T(8,128)(2,1)}, u32[]{:S(2)}, u32[]{:S(2)}) collective-permute-start(bf16[4,4,24,3072]{3,2,1,0:T(8,128)(2,1)} %dynamic-slice_bitcast_fusion.1), channel_id=1, source_target_pairs={{0,1},{1,0},{2,3},{3,2},{4,5},{5,4},{6,7},{7,6},{8,9},{9,8},{10,11... | collective-permute-start | bytes 7077896 | tf_op jit(solution)/shard_map/ppermute | solution.py:566
  267.0 39.3 %all-to-all-start.1 = ((f32[8,128,768]{2,1,0:T(8,128)}), f32[8,128,768]{2,1,0:T(8,128)}, u32[]{:S(2)}, u32[]{:S(2)}) async-start(f32[8,128,768]{2,1,0:T(8,128)} %bitcast.104), calls=%async_computation.1 | async-start | bytes 6291456 | tf_op jit(solution)/shard_map/all_to_all | solution.py:560
  276.8 4.8 %collective-permute-start.3 = (bf16[4,4,24,896]{3,2,1,0:T(8,128)(2,1)S(1)}, bf16[4,4,24,896]{3,2,1,0:T(8,128)(2,1)S(1)}, u32[]{:S(2)}, u32[]{:S(2)}) collective-permute-start(bf16[4,4,24,896]{3,2,1,0:T(8,128)(2,1)S(1)} %fusion.24), channel_id=1, source_target_pairs={{0,1},{1,0},{2,3},{3,2},{4,5},{5,4},{6,7},{7,6},{8,9},{9,8},{10,11... | collective-permute-start | bytes 2064392 | tf_op jit(solution)/shard_map/ppermute | solution.py:566
  277.0 10.2 %slice-start = ((s8[4718592]{0:T(1024)(128)(4,1)}), s8[4194304]{0:T(1024)(128)(4,1)S(1)}, s32[]{:S(2)}) async-start(s8[4718592]{0:T(1024)(128)(4,1)} %bitcast.108), calls=%async_computation.3 | async-start | bytes 8388608
  281.6 5.6 %slice-start.1 = ((s8[4718592]{0:T(1024)(128)(4,1)}), s8[524288]{0:T(1024)(128)(4,1)S(1)}, s32[]{:S(2)}) async-start(s8[4718592]{0:T(1024)(128)(4,1)} %bitcast.108), calls=%async_computation.4 | async-start | bytes 1048576
  392.3 8.6 %collective-permute-start.5 = (bf16[1024,768]{1,0:T(8,128)(2,1)}, bf16[1024,768]{1,0:T(8,128)(2,1)S(1)}, u32[]{:S(2)}, u32[]{:S(2)}) collective-permute-start(bf16[1024,768]{1,0:T(8,128)(2,1)} %get-tuple-element.58), channel_id=1, source_target_pairs={{0,1},{1,0},{2,3},{3,2},{4,5},{5,4},{6,7},{7,6},{8,9},{9,8},{10,11... | collective-permute-start | bytes 4718600 | tf_op jit(solution)/shard_map/ppermute | solution.py:663
  394.6 10.2 %collective-permute-start.4 = (bf16[1024,768]{1,0:T(8,128)(2,1)}, bf16[1024,768]{1,0:T(8,128)(2,1)}, u32[]{:S(2)}, u32[]{:S(2)}) collective-permute-start(bf16[1024,768]{1,0:T(8,128)(2,1)} %get-tuple-element.56), channel_id=1, source_target_pairs={{0,1},{1,0},{2,3},{3,2},{4,5},{5,4},{6,7},{7,6},{8,9},{9,8},{10,11... | collective-permute-start | bytes 4718600 | tf_op jit(solution)/shard_map/ppermute | solution.py:662
  411.4 10.4 %collective-permute-start.6 = (bf16[4,4,24,2432]{3,2,1,0:T(8,128)(2,1)}, bf16[4,4,24,2432]{3,2,1,0:T(8,128)(2,1)S(1)}, u32[]{:S(2)}, u32[]{:S(2)}) collective-permute-start(bf16[4,4,24,2432]{3,2,1,0:T(8,128)(2,1)} %dynamic-slice_bitcast_fusion.2), channel_id=1, source_target_pairs={{0,1},{1,0},{2,3},{3,2},{4,5},{5,4},{6,7},{7,6},{8,9},{9,8},{10,11... | collective-permute-start | bytes 5603336 | tf_op jit(solution)/shard_map/ppermute | solution.py:566
  (29 other events, 98.2 us)

commit v4 on v2

--- a/solution.py
+++ b/solution.py
@@ -175,92 +175,162 @@
 
 
 class Scatter:
-    def __init__(self, dp, ctx, sources, outs, buffers, mover):
+    def __init__(self, dp, ctx, sources, outs, buffers, small, small_out, small_buffers, mover):
         d, c, g, m, over_dp, over_groups, sibling = place(dp, ctx)
         groups = ctx // 2
-        self.dp, self.groups, self.d = dp, groups, d
-        self.devices = over_groups + over_dp
-        self.outs = outs
-        self.mine = [b[0] for b in buffers]
-        self.came = [b[1] for b in buffers]
-        self.sums = [b[2] for b in buffers]
-        self.last = [b[3] for b in buffers]
-        self.own = [mover.local(s.at[:, g], b) for s, b in zip(sources, self.mine)]
-        self.across = [
-            [
-                mover.remote(s.at[:, (g + k) % groups], b.at[k - 1], over_groups[k - 1])
-                for k in range(1, groups)
-            ]
-            for s, b in zip(sources, self.came)
-        ]
-        self.along = [
-            [
-                mover.remote(s.at[(d + k) % dp], b.at[k - 1], over_dp[k - 1])
-                for k in range(1, dp)
-            ]
-            for s, b in zip(self.sums, self.last)
-        ]
+        self.dp, self.groups, self.d, self.g = dp, groups, d, g
+        self.devices = over_groups + over_dp + [sibling]
+        self.outs = list(outs)
+        self.buffers = buffers
+        self.own, self.pair, self.across, self.along = [], [], [], []
+        for source, (mine, other, came, sums, last) in zip(sources, buffers):
+            self.own.append(mover.local(source.at[:, :, m], mine))
+            self.pair.append([mover.remote(source.at[:, :, 1 - m], other, sibling)])
+            self.across.append(
+                [
+                    mover.remote(mine.at[:, (g + k) % groups], came.at[k - 1], over_groups[k - 1])
+                    for k in range(1, groups)
+                ]
+            )
+            self.along.append(
+                [
+                    mover.remote(sums.at[(d + k) % dp], last.at[k - 1], over_dp[k - 1])
+                    for k in range(1, dp)
+                ]
+            )
+        self.small, self.small_out = small, small_out
+        one, came, two, groups_in, three, dp_in = small_buffers
+        self.small_buffers = small_buffers
+        self.pair.append([mover.remote(one, came, sibling)])
+        self.across.append(
+            [mover.remote(two, groups_in.at[k - 1], over_groups[k - 1]) for k in range(1, groups)]
+        )
+        self.along.append(
+            [mover.remote(three, dp_in.at[k - 1], over_dp[k - 1]) for k in range(1, dp)]
+        )
 
     @staticmethod
-    def count(dp, groups, arrays):
-        return arrays * (groups - 1 + dp - 1)
+    def count(dp, ctx, arrays):
+        return (arrays + 1) * (1 + ctx // 2 - 1 + dp - 1)
 
     @staticmethod
-    def scratch(dp, groups, sources):
+    def scratch(dp, ctx, sources, small):
+        groups = ctx // 2
         shapes = []
         for s in sources:
-            block = s.shape[2:]
+            block = s.shape[3:]
             shapes += [
-                pltpu.VMEM((dp,) + block, BF),
+                pltpu.VMEM((dp, groups) + block, BF),
+                pltpu.VMEM((dp, groups) + block, BF),
                 pltpu.VMEM((groups - 1, dp) + block, BF),
                 pltpu.VMEM((dp,) + block, BF),
                 pltpu.VMEM((dp - 1,) + block, BF),
             ]
+        shape = small.shape
+        shapes += [pltpu.VMEM(shape, F32)] * 3
+        shapes += [
+            pltpu.VMEM((groups - 1,) + shape, F32),
+            pltpu.VMEM(shape, F32),
+            pltpu.VMEM((dp - 1,) + shape, F32),
+        ]
         return shapes
 
     def begin(self):
-        for copy in self.own + [copy for batch in self.across for copy in batch]:
+        self.small_buffers[0][...] = self.small[...]
+        for batch in self.pair[-1:] + self.pair[:-1]:
+            batch[0].start()
+        for copy in self.own:
             copy.start()
 
+    def first(self, index):
+        mine, other = self.buffers[index][:2]
+        groups = self.groups
+        self.own[index].wait()
+        self.pair[index][0].wait_recv()
+
+        def add(i, carry):
+            at = (i // groups, i % groups)
+            mine[at] = (mine[at].astype(F32) + other[at].astype(F32)).astype(BF)
+            return carry
+
+        lax.fori_loop(0, self.dp * groups, add, 0)
+        for copy in self.across[index]:
+            copy.start()
+
+    def first_small(self):
+        one, came, two = self.small_buffers[:3]
+        self.pair[-1][0].wait_recv()
+        two[...] = one[...] + came[...]
+        for copy in self.across[-1]:
+            copy.start()
+
     def middle(self, index):
-        self.own[index].wait()
+        mine, _, came, sums, _ = self.buffers[index]
         for copy in self.across[index]:
             copy.wait_recv()
-        for k in range(self.dp):
-            total = self.mine[index][k].astype(F32)
+
+        def add(k, carry):
+            total = mine[k, self.g].astype(F32)
             for j in range(self.groups - 1):
-                total = total + self.came[index][j, k].astype(F32)
-            self.sums[index][k] = total.astype(BF)
+                total = total + came[j, k].astype(F32)
+            sums[k] = total.astype(BF)
+            return carry
+
+        lax.fori_loop(0, self.dp, add, 0)
         for copy in self.along[index]:
             copy.start()
 
+    def middle_small(self):
+        _, _, two, groups_in, three, _ = self.small_buffers
+        for copy in self.across[-1]:
+            copy.wait_recv()
+        total = two[...]
+        for j in range(self.groups - 1):
+            total = total + groups_in[j]
+        three[...] = total
+        for copy in self.along[-1]:
+            copy.start()
+
     def finish(self):
         for index, out in enumerate(self.outs):
+            sums, last = self.buffers[index][3:]
             for copy in self.along[index]:
                 copy.wait_recv()
-            total = self.sums[index][self.d].astype(F32)
+            total = sums[self.d].astype(F32)
             for j in range(self.dp - 1):
-                total = total + self.last[index][j].astype(F32)
+                total = total + last[j].astype(F32)
             out[...] = total
-        for batch in self.across + self.along:
+        three, dp_in = self.small_buffers[4:]
+        for copy in self.along[-1]:
+            copy.wait_recv()
+        total = three[...]
+        for j in range(self.dp - 1):
+            total = total + dp_in[j]
+        self.small_out[...] = total
+        for batch in self.pair + self.across + self.along:
             for copy in batch:
                 copy.wait_send()
 
 
-def finish_kernel(dp, ctx, s, x, out, x_out, *scratch):
+def finish_kernel(dp, ctx, s, small, x, out, small_out, x_out, *scratch):
     buffers, (local_sem, send_sem, recv_sem) = scratch[:-3], scratch[-3:]
-    d, c, g, m, over_dp, over_groups, sibling = place(dp, ctx)
+    d, c = lax.axis_index("dp"), lax.axis_index("ctx")
     mover = Mover(local_sem, send_sem, recv_sem)
-    scatter = Scatter(dp, ctx, [s], [out], [buffers], mover)
+    scatter = Scatter(
+        dp, ctx, [s], [out], [buffers[:5]], small, small_out, buffers[5:], mover
+    )
     own = mover.local(x.at[c], x_out.at[c])
     rows = [
         mover.remote(x.at[(c + k) % ctx], x_out.at[c], (d, (c + k) % ctx)) for k in range(1, ctx)
     ]
-    greet(over_dp + [(d, (c + k) % ctx) for k in range(1, ctx)])
+    greet([((d + k) % dp, c) for k in range(1, dp)] + [(d, (c + k) % ctx) for k in range(1, ctx)])
     scatter.begin()
     own.start()
+    scatter.first_small()
+    scatter.first(0)
     for copy in rows:
         copy.start()
+    scatter.middle_small()
     scatter.middle(0)
     scatter.finish()
     for copy in rows:
@@ -268,16 +338,20 @@
     own.wait()
 
 
-def finish_gradients(s, x, dp, ctx):
-    groups = ctx // 2
-    remotes = Scatter.count(dp, groups, 1) + ctx - 1
+def finish_gradients(s, small, x, dp, ctx):
+    remotes = Scatter.count(dp, ctx, 1) + ctx - 1
     any_space = pl.BlockSpec(memory_space=pl.ANY)
+    vmem = pl.BlockSpec(memory_space=pltpu.VMEM)
     return pl.pallas_call(
         functools.partial(finish_kernel, dp, ctx),
-        in_specs=[any_space] * 2,
-        out_specs=[pl.BlockSpec(memory_space=pltpu.VMEM), any_space],
-        out_shape=[jax.ShapeDtypeStruct(s.shape[2:], F32), jax.ShapeDtypeStruct(x.shape, x.dtype)],
-        scratch_shapes=Scatter.scratch(dp, groups, [s])
+        in_specs=[any_space, vmem, any_space],
+        out_specs=[vmem, vmem, any_space],
+        out_shape=[
+            jax.ShapeDtypeStruct(s.shape[3:], F32),
+            jax.ShapeDtypeStruct(small.shape, F32),
+            jax.ShapeDtypeStruct(x.shape, x.dtype),
+        ],
+        scratch_shapes=Scatter.scratch(dp, ctx, [s], small)
         + [
             pltpu.SemaphoreType.DMA((2,)),
             pltpu.SemaphoreType.DMA((remotes,)),
@@ -287,7 +361,7 @@
             collective_id=3, has_side_effects=True, vmem_limit_bytes=32 << 20
         ),
         name="finish_gradients",
-    )(s, x)
+    )(s, small, x)
 
 
 def head_lanes(shape, h):
@@ -395,7 +469,9 @@
 
 def backward_steps(pairs, steps):
     count = pairs * steps
-    return (count * 8 // 16, count * 3 // 16, count * 13 // 16)
+    first = [count * at // 12 for at in (1, 1, 2)]
+    middle = [count * at // 12 for at in (6, 7, 9)]
+    return first, middle
 
 
 def backward_kernel(dp, ctx, ck, *refs):
@@ -403,17 +479,20 @@
         refs[:9],
         refs[9:],
     )
-    sources, refs = refs[:3], refs[3:]
+    sources, small, refs = refs[:3], refs[3], refs[4:]
     (dq_ref, dko_ref, dvo_ref, dks_ref, dvs_ref), refs = refs[:5], refs[5:]
-    summed, refs = refs[:3], refs[3:]
+    summed, small_out, refs = refs[:3], refs[3], refs[4:]
     (keys, dk, dv), refs = refs[:3], refs[3:]
-    buffers, (local_sem, send_sem, recv_sem) = refs[:12], refs[12:]
+    buffers, small_buffers, (local_sem, send_sem, recv_sem) = refs[:15], refs[15:21], refs[21:]
     scatter = Scatter(
         dp,
         ctx,
         sources,
         summed,
-        [buffers[i * 4 : i * 4 + 4] for i in range(3)],
+        [buffers[i * 5 : i * 5 + 5] for i in range(3)],
+        small,
+        small_out,
+        small_buffers,
         Mover(local_sem, send_sem, recv_sem),
     )
     steps = pl.num_programs(1)
@@ -469,9 +548,23 @@
         dks_ref[...] = dk[half:, :].astype(BF)
         dvs_ref[...] = dv[half:, :].astype(BF)
 
-    for index, at in enumerate(backward_steps(pl.num_programs(0), steps)):
-
-        @pl.when(step == at)
+    first, middle_at = backward_steps(pl.num_programs(0), steps)
+
+    @pl.when(step == first[0])
+    def _():
+        scatter.first_small()
+
+    @pl.when(step == middle_at[0])
+    def _():
+        scatter.middle_small()
+
+    for index in range(3):
+
+        @pl.when(step == first[index])
+        def _(index=index):
+            scatter.first(index)
+
+        @pl.when(step == middle_at[index])
         def _(index=index):
             scatter.middle(index)
 
@@ -480,7 +573,9 @@
         scatter.finish()
 
 
-def attention_backward(q, do, mix, kv, kv_sib, bias, lse, sources, dp, ctx, bq=512, ck=512):
+def attention_backward(
+    q, do, mix, kv, kv_sib, bias, lse, sources, small, dp, ctx, bq=512, ck=512
+):
     rows = q.shape[0]
     pairs = q.shape[1] // 128
     S = jax.ShapeDtypeStruct
@@ -488,17 +583,20 @@
     full = pl.BlockSpec((rows, 128), lambda p, j: (0, p))
     v_spec = pl.BlockSpec((rows, 128), lambda p, j: (0, pairs + p))
     any_space = pl.BlockSpec(memory_space=pl.ANY)
-    remotes = Scatter.count(dp, ctx // 2, 3)
-    sums = [s.shape[2:] for s in sources]
+    remotes = Scatter.count(dp, ctx, 3)
+    whole = pl.BlockSpec(small.shape, lambda p, j: (0, 0))
+    sums = [s.shape[3:] for s in sources]
     return pl.pallas_call(
         functools.partial(backward_kernel, dp, ctx, ck),
         grid=(pairs, rows // bq),
         in_specs=[blk, blk, blk, full, full, v_spec, v_spec]
         + [pl.BlockSpec((2, rows, 128), lambda p, j: (0, 0, 0))]
         + [pl.BlockSpec((1, 8, bq), lambda p, j: (p, 0, j))]
-        + [any_space] * 3,
+        + [any_space] * 3
+        + [whole],
         out_specs=[blk, full, full, full, full]
-        + [pl.BlockSpec(shape, lambda p, j: (0, 0)) for shape in sums],
+        + [pl.BlockSpec(shape, lambda p, j: (0, 0)) for shape in sums]
+        + [whole],
         out_shape=[
             S(q.shape, BF),
             S(q.shape, F32),
@@ -506,13 +604,14 @@
             S(q.shape, BF),
             S(q.shape, BF),
         ]
-        + [S(shape, F32) for shape in sums],
+        + [S(shape, F32) for shape in sums]
+        + [S(small.shape, F32)],
         scratch_shapes=[
             pltpu.VMEM((2, 2 * rows, 128), BF),
             pltpu.VMEM((2 * rows, 128), F32),
             pltpu.VMEM((2 * rows, 128), F32),
         ]
-        + Scatter.scratch(dp, ctx // 2, sources)
+        + Scatter.scratch(dp, ctx, sources, small)
         + [
             pltpu.SemaphoreType.DMA((3,)),
             pltpu.SemaphoreType.DMA((remotes,)),
@@ -527,7 +626,220 @@
             transcendentals=4 * rows * rows * pairs,
         ),
         name="attend_back",
-    )(q, do, mix, kv, kv_sib, kv, kv_sib, bias, lse, *sources)
+    )(q, do, mix, kv, kv_sib, kv, kv_sib, bias, lse, *sources, small)
+
+
+class Exchange:
+    def __init__(self, ctx, mover, source, target, bringing):
+        d, c = lax.axis_index("dp"), lax.axis_index("ctx")
+        groups = ctx // 2
+        self.steps = []
+        for t in range(groups):
+            group = (c // 2 + (groups - t if bringing else t)) % groups
+            same, other = group * 2 + c % 2, group * 2 + 1 - c % 2
+            if t == 0:
+                self.own = mover.local(source.at[c], target.at[c])
+                batch = []
+            else:
+                batch = [mover.remote(source.at[same], target.at[c], (d, same))]
+            batch.append(mover.remote(source.at[other], target.at[c], (d, other)))
+            self.steps.append(batch)
+
+    @staticmethod
+    def count(ctx):
+        return ctx - 1
+
+    def start(self, t):
+        if t == 0:
+            self.own.start()
+        for copy in self.steps[t]:
+            copy.start()
+
+    def arrive(self, t):
+        if t == 0:
+            self.own.wait()
+        for copy in self.steps[t]:
+            copy.wait_recv()
+
+    def sent(self):
+        for batch in self.steps:
+            for copy in batch:
+                copy.wait_send()
+
+
+def gelu_and_slope(x):
+    t = 1.0 / (1.0 + 0.2316419 * jnp.abs(x))
+    bell = 0.3989422804 * jnp.exp(-0.5 * x * x)
+    poly = 1.330274429 * t - 1.821255978
+    poly = poly * t + 1.781477937
+    poly = poly * t - 0.356563782
+    poly = poly * t + 0.319381530
+    tail = bell * (poly * t)
+    below = jnp.where(x < 0.0, tail, 1.0 - tail)
+    return x * below, below + x * bell
+
+
+def columns(values):
+    return jnp.sum(values, axis=0, keepdims=True)
+
+
+def middle_kernel(dp, ctx, *refs):
+    (mb, xb, rest_src, up_src, vec, bias_up, wo_src, wu_src, wd_src), refs = refs[:9], refs[9:]
+    (dm, grad_sum, out_to, go_to, gu_to, gd_to, small), refs = refs[:7], refs[7:]
+    (wo, wu, wd, rest, upstream, result, active, dinner, slope, fb, db, da), refs = (
+        refs[:12],
+        refs[12:],
+    )
+    load_sem, local_sem, send_sem, recv_sem = refs
+    groups = ctx // 2
+    g = lax.axis_index("ctx") // 2
+    half, width = result.shape[1:]
+    tile = 2 * half
+    chunks = range(wu.shape[1] // width)
+    step = pl.program_id(0)
+    mover = Mover(local_sem, send_sem, recv_sem)
+    rest_in = Exchange(ctx, mover, rest_src, rest, True)
+    up_in = Exchange(ctx, mover, up_src, upstream, True)
+    give = Exchange(ctx, mover, result, out_to, False)
+    loads = [
+        pltpu.make_async_copy(source, target, load_sem.at[i])
+        for i, (source, target) in enumerate(((wo_src, wo), (wu_src, wu), (wd_src, wd)))
+    ]
+    stores = [
+        pltpu.make_async_copy(source, target, load_sem.at[i])
+        for i, (source, target) in enumerate(((wo, go_to), (wu, gu_to), (wd, gd_to)))
+    ]
+
+    def load(index):
+        @pl.when(step == 0)
+        def _():
+            loads[index].wait()
+
+    @pl.when(step == 0)
+    def _():
+        for copy in loads:
+            copy.start()
+        d, c = lax.axis_index("dp"), lax.axis_index("ctx")
+        greet([(d, (c + k) % ctx) for k in range(1, ctx)])
+        for t in range(groups):
+            rest_in.start(t)
+            up_in.start(t)
+        small[...] = jnp.zeros_like(small)
+
+    @pl.when(step < groups)
+    def _():
+        block = (g + step) % groups
+        rows = pl.ds(pl.multiple_of(block * tile, tile), tile)
+        pair = pl.ds(block * 2, 2)
+        load(0)
+        hidden = dg(mb[rows, :], wo[...], NN) + vec[2:3, :] + xb[rows, :].astype(F32)
+        for t in range(groups):
+
+            @pl.when(step == t)
+            def _(t=t):
+                rest_in.arrive(t)
+
+        hidden = hidden + rest[pair].reshape(tile, width).astype(F32)
+        normed, standard_one, inverse_one = normalize(hidden, vec[6:7, :], vec[4:5, :])
+        low = normed.astype(BF)
+        fb[rows, :] = low
+        load(1)
+        for i in chunks:
+            part = slice(i * width, (i + 1) * width)
+            inner = dg(low, wu[:, part], NN) + bias_up[:, part]
+            value, slope[:, part] = gelu_and_slope(inner)
+            active[rows, part] = value.astype(BF)
+        load(2)
+        hidden = normed + dg(active[rows, :], wd[...], NN) + vec[3:4, :]
+        out, standard, inverse = normalize(hidden, vec[7:8, :], vec[5:6, :])
+        result[pair] = out.astype(BF).reshape(2, half, width)
+        for t in range(groups):
+
+            @pl.when(step == t)
+            def _(t=t):
+                give.start(t)
+                up_in.arrive(t)
+
+        error = upstream[pair].reshape(tile, width).astype(F32)
+        grad = normalize_back(error, standard, inverse, vec[7:8, :])
+        low_grad = grad.astype(BF)
+        db[rows, :] = low_grad
+        small[1:2, :] += columns(low_grad.astype(F32))
+        small[3:4, :] += columns(error)
+        small[5:6, :] += columns(error * standard)
+        for i in chunks:
+            part = slice(i * width, (i + 1) * width)
+            change = dg(low_grad, wd[part, :], NT) * slope[:, part]
+            change = change.astype(BF)
+            dinner[rows, part] = change
+            small[6 + i : 7 + i, :] += columns(change.astype(F32))
+        grad = grad + dg(dinner[rows, :], wu[...], NT)
+        small[2:3, :] += columns(grad)
+        small[4:5, :] += columns(grad * standard_one)
+        grad = normalize_back(grad, standard_one, inverse_one, vec[6:7, :])
+        grad_sum[rows, :] = grad
+        low_grad = grad.astype(BF)
+        da[rows, :] = low_grad
+        small[0:1, :] += columns(low_grad.astype(F32))
+        dm[rows, :] = dg(low_grad, wo[...], NT).astype(BF)
+
+    @pl.when(step == groups)
+    def _():
+        for i in chunks:
+            part = slice(i * width, (i + 1) * width)
+            wd[part, :] = dg(active[:, part], db[...], TN).astype(BF)
+        stores[2].start()
+        for i in chunks:
+            part = slice(i * width, (i + 1) * width)
+            wu[:, part] = dg(fb[...], dinner[:, part], TN).astype(BF)
+        stores[1].start()
+        wo[...] = dg(mb[...], da[...], TN).astype(BF)
+        stores[0].start()
+        for t in range(groups):
+            give.arrive(t)
+        for move in (rest_in, up_in, give):
+            move.sent()
+        for copy in stores:
+            copy.wait()
+
+
+def middle(mb, xb, rest, upstream, vec, bias_up, wo, wu, wd, dp, ctx):
+    rows, width = mb.shape
+    hidden = wu.shape[1]
+    half = rows // ctx
+    S = jax.ShapeDtypeStruct
+    any_space = pl.BlockSpec(memory_space=pl.ANY)
+    vmem = pl.BlockSpec(memory_space=pltpu.VMEM)
+    remotes = 3 * Exchange.count(ctx)
+    return pl.pallas_call(
+        functools.partial(middle_kernel, dp, ctx),
+        grid=(ctx // 2 + 1,),
+        in_specs=[vmem, vmem, any_space, any_space, vmem, vmem] + [any_space] * 3,
+        out_specs=[vmem, vmem] + [any_space] * 4 + [vmem],
+        out_shape=[S(mb.shape, BF), S(mb.shape, F32), S(rest.shape, BF)]
+        + [S(array.shape, BF) for array in (wo, wu, wd)]
+        + [S((16, width), F32)],
+        scratch_shapes=[pltpu.VMEM(array.shape, BF) for array in (wo, wu, wd)]
+        + [pltpu.VMEM(rest.shape, BF)] * 3
+        + [pltpu.VMEM((rows, hidden), BF)] * 2
+        + [pltpu.VMEM((2 * half, hidden), F32)]
+        + [pltpu.VMEM((rows, width), BF)] * 3
+        + [
+            pltpu.SemaphoreType.DMA((3,)),
+            pltpu.SemaphoreType.DMA((3,)),
+            pltpu.SemaphoreType.DMA((remotes,)),
+            pltpu.SemaphoreType.DMA((remotes,)),
+        ],
+        compiler_params=pltpu.CompilerParams(
+            vmem_limit_bytes=58 << 20, collective_id=4, has_side_effects=True
+        ),
+        cost_estimate=pl.CostEstimate(
+            flops=2 * 3 * rows * width * (2 * hidden + width),
+            bytes_accessed=50 << 20,
+            transcendentals=rows * hidden,
+        ),
+        name="middle",
+    )(mb, xb, rest, upstream, vec, bias_up, wo, wu, wd)
 
 
 def normalize(hidden, scale_row, shift_row):
@@ -556,15 +868,8 @@
     length = lax.dynamic_index_in_dim(lengths, own_seq, 0, keepdims=False)
     pair_perm = [(i, i ^ 1) for i in range(ctx)]
 
-    def exchange(array):
-        return lax.all_to_all(array, "ctx", 0, 0, tiled=True)
-
-    def over_pair(grad):
-        parts = grad.astype(BF).reshape(dp, ctx // 2, 2, -1, grad.shape[1])
-        keep = lax.dynamic_index_in_dim(parts, member, 2, keepdims=False)
-        send = lax.dynamic_index_in_dim(parts, 1 - member, 2, keepdims=False)
-        got = lax.ppermute(send, "ctx", pair_perm)
-        return (keep.astype(F32) + got.astype(F32)).astype(BF)
+    def by_owner(grad):
+        return grad.reshape(dp, ctx // 2, 2, -1, grad.shape[1])
 
     split = tokens.reshape(ctx, half, width)
     held = w_query.shape[0]
@@ -585,8 +890,7 @@
     vector_rows = full_first[:, 3 * width : 3 * width + 8].T.astype(F32)
     bias_columns = b_up.shape[0] // held
     full_bias_up = full_first[:, 3 * width + 8 : 3 * width + 8 + bias_columns].reshape(-1).astype(F32)
-    residual = exchange(split).reshape(rows, width)
-    upstream = exchange(cotangent.reshape(ctx, half, width)).reshape(rows, width)
+    left_out = (split - split.astype(BF).astype(F32)).astype(BF)
 
     slot = jnp.arange(rows, dtype=jnp.int32)
     source = slot // half
@@ -610,49 +914,32 @@
     full_up = full_up.reshape(width, -1)
     full_down = full_down.reshape(-1, width)
 
-    attention = dg(low_mixed, full_attn, NN) + vector_rows[2]
-    normed_one, standard_one, inverse_one = normalize(
-        residual + attention, vector_rows[6], vector_rows[4]
-    )
-    low_first = normed_one.astype(BF)
-    inner = dg(low_first, full_up, NN) + full_bias_up
-    active = jax.nn.gelu(inner, approximate=False).astype(BF)
-    branch = dg(active, full_down, NN) + vector_rows[3]
-    result, standard_two, inverse_two = normalize(
-        normed_one + branch, vector_rows[7], vector_rows[5]
-    )
-    output = exchange(result.reshape(ctx, half, width)).reshape(seqs, rows_dev, width)
-
-    d_gain_two = jnp.sum(upstream * standard_two, axis=0)
-    d_shift_two = jnp.sum(upstream, axis=0)
-    grad_second = normalize_back(upstream, standard_two, inverse_two, vector_rows[7])
-    low_branch = grad_second.astype(BF)
-    d_bias_down = jnp.sum(low_branch.astype(F32), axis=0)
-    d_down = dg(active, low_branch, TN)
-    d_active = dg(low_branch, full_down, NT)
-    gelu_back = jax.vjp(lambda v: jax.nn.gelu(v, approximate=False), inner)[1]
-    low_inner = gelu_back(d_active)[0].astype(BF)
-    d_bias_up = jnp.sum(low_inner.astype(F32), axis=0)
-    d_up = dg(low_first, low_inner, TN)
-    part_down = over_pair(d_down)
-    part_up = over_pair(d_up)
-    grad_first = grad_second + dg(low_inner, full_up, NT)
-    d_gain_one = jnp.sum(grad_first * standard_one, axis=0)
-    d_shift_one = jnp.sum(grad_first, axis=0)
-    grad_sum = normalize_back(grad_first, standard_one, inverse_one, vector_rows[6])
-    low_attn = grad_sum.astype(BF)
-    d_bias_attn = jnp.sum(low_attn.astype(F32), axis=0)
-    d_attn = dg(low_mixed, low_attn, TN)
-    d_mixed = dg(low_attn, full_attn, NT).astype(BF)
-
-    d_vector_rows = jnp.stack(
-        [d_bias_attn, d_bias_down, d_shift_one, d_shift_two, d_gain_one, d_gain_two]
-    )
-    extra = jnp.concatenate([d_vector_rows.T, d_bias_up.reshape(width, -1)], axis=1)
-    extra = jnp.pad(extra, ((0, 0), (0, 128 - extra.shape[1])))
-    part_attn = over_pair(jnp.concatenate([d_attn, extra], axis=1))
-    dq, dk_own, dv_own, dk_sib, dv_sib, own_up, own_down, own_attn = attention_backward(
-        queries, d_mixed, mixed, kv, kv_sib, bias, lse, [part_up, part_down, part_attn], dp, ctx
+    d_mixed, grad_sum, result, d_attn, d_up, d_down, small = middle(
+        low_mixed,
+        low_in,
+        left_out,
+        cotangent.reshape(ctx, half, width).astype(BF),
+        vector_rows,
+        full_bias_up.reshape(1, -1),
+        full_attn,
+        full_up,
+        full_down,
+        dp,
+        ctx,
+    )
+    output = result.astype(F32).reshape(seqs, rows_dev, width)
+    dq, dk_own, dv_own, dk_sib, dv_sib, own_attn, own_down, own_up, small = attention_backward(
+        queries,
+        d_mixed,
+        mixed,
+        kv,
+        kv_sib,
+        bias,
+        lse,
+        [by_owner(d_attn), by_owner(d_down), by_owner(d_up)],
+        small,
+        dp,
+        ctx,
     )
     dk_got = lax.ppermute(dk_sib, "ctx", pair_perm)
     dv_got = lax.ppermute(dv_sib, "ctx", pair_perm)
@@ -664,20 +951,23 @@
         + dg(dv, full_qkv[:, 2 * width :], NT)
     )
     sums = jnp.stack([jnp.sum(dq.astype(F32), axis=0), jnp.sum(dv.astype(F32), axis=0)])
-    sums = jnp.pad(sums.T, ((0, 0), (0, 126)))
-    part = over_pair(
-        jnp.concatenate([dg(low_in, dq, TN), dg(low_in, dk, TN), dg(low_in, dv, TN), sums], axis=1)
-    )
-    own, grad_tokens = finish_gradients(
-        part, grad_in.astype(BF).reshape(ctx, half, width), dp, ctx
+    joined = [dg(low_in, part, TN).astype(BF) for part in (dq, dk, dv)]
+    own, sums, grad_tokens = finish_gradients(
+        by_owner(jnp.concatenate(joined, axis=1)),
+        jnp.pad(sums, ((0, 6), (0, 0))),
+        grad_in.astype(BF).reshape(ctx, half, width),
+        dp,
+        ctx,
     )
     grad_tokens = grad_tokens.astype(F32).reshape(seqs, rows_dev, width)
     own_query, own_key, own_value = (own[:, i * width : (i + 1) * width] for i in range(3))
-    own_vectors = jnp.concatenate(
-        [own[:, 3 * width : 3 * width + 2], own_attn[:, width : width + 6]], axis=1
-    ).T
-    own_bias_up = own_attn[:, width + 6 : width + 6 + bias_columns].reshape(-1)
-    own_attn = own_attn[:, :width]
+    index = lax.axis_index("dp") * ctx + lax.axis_index("ctx")
+    own_vectors = lax.dynamic_slice_in_dim(
+        jnp.concatenate([sums[:2], small[:6]]), index * held, held, 1
+    )
+    own_bias_up = lax.dynamic_slice_in_dim(
+        small[6 : 6 + bias_columns].reshape(-1), index * b_up.shape[0], b_up.shape[0], 0
+    )
     return (
         output,
         grad_tokens,

time: 542 us -> 411 us (0.76)
  matrix products: 131 us -> 31.5 us
  starting transfers between devices: 16.4 us -> 1.23 us
  Pallas kernels: 321 us -> 334 us
  other arithmetic: 33.2 us -> 20.5 us
  local copies, waits for them, and re-layouts: 26.4 us -> 16.3 us
  waiting for transfers between devices: 8.44 us -> 0.01 us
    dot_general x17 -> x8, matrix products: 131 us -> 31.5 us  [dg(): return lax.dot_general(left, right, dims, preferred_element_type=F32)]
    pallas_call x0 -> x1, Pallas kernels: none -> 77.7 us  [middle(): pl.pallas_call(functools.partial(middle_kernel, dp, ctx), grid=(ctx // 2...]
    pallas_call x1, Pallas kernels: 72.8 us -> 47.6 us  [gather_first(): pl.pallas_call(functools.partial(gather_kernel, dp, ctx), in_specs=[any_s...]
    pallas_call x1, Pallas kernels: 88.1 us -> 65.4 us  [attention_forward(): pl.pallas_call(functools.partial(forward_kernel, dp, ctx), grid=(pairs, r...]
    pallas_call x1, Pallas kernels: 117 us -> 96.4 us  [attention_backward(): pl.pallas_call(functools.partial(backward_kernel, dp, ctx, ck), grid=(pai...]
    all_to_all x3 -> x0, starting transfers between devices: 14.5 us -> none  [exchange(): return lax.all_to_all(array, 'ctx', 0, 0, tiled=True)]
    all_to_all x3 -> x0, waiting for transfers between devices: 8.42 us -> none  [exchange(): return lax.all_to_all(array, 'ctx', 0, 0, tiled=True)]
    reduce_sum x6 -> x0, other arithmetic: 8.25 us -> none  [the longest x1 2.9 us: on_device(): d_gain_two = jnp.sum(upstream * standard_two, axis=0)]
  transfers between devices with their start and end apart: 10 -> 3, of which waited for: 1 -> 0; matrix products, arithmetic and copies ran while one was open for 14% -> 7% of each run, Pallas kernels for 30% -> 0%
where the time goes in v4:
time: 411 us; the launch traced here: 405 us
  Pallas kernels  334 us (81%)
  matrix products  31.5 us (8%)
  other arithmetic  20.5 us (5%)
  local copies, waits for them, and re-layouts  16.3 us (4%)
    pallas_call x1, Pallas kernels, attention_backward(): pl.pallas_call(functools.partial(backward_kernel, dp, ctx, ck), grid=(pai...  96.4 us
    pallas_call x1, Pallas kernels, middle(): pl.pallas_call(functools.partial(middle_kernel, dp, ctx), grid=(ctx // 2...  77.7 us
    pallas_call x1, Pallas kernels, attention_forward(): pl.pallas_call(functools.partial(forward_kernel, dp, ctx), grid=(pairs, r...  65.4 us
    pallas_call x1, Pallas kernels, gather_first(): pl.pallas_call(functools.partial(gather_kernel, dp, ctx), in_specs=[any_s...  47.6 us
    pallas_call x1, Pallas kernels, finish_gradients(): pl.pallas_call(functools.partial(finish_kernel, dp, ctx), in_specs=[any_s...  46.7 us
    dot_general x8, matrix products, dg(): return lax.dot_general(left, right, dims, preferred_element_type=F32)  31.5 us
  transfers between devices with their start and end apart: 3, of which 0 were waited for; matrix products, arithmetic and copies ran while one was open for 7% of the time, Pallas kernels for 0%

profile of v4, /device:TPU:1, one launch (start us, length us, event | category | flops | bytes accessed | tf_op | source)
XLA Modules:
  0.0 404.6 jit_solution(8143675265535528365)
XLA Ops:
  2.2 5.2 %subtract_convert_fusion = (bf16[8,128,768]{2,1,0:T(8,128)(2,1)}, bf16[8,128,768]{2,1,0:T(8,128)(2,1)}) fusion(f32[8,128,768]{2,1,0:T(8,128)} %bitcast.37), kind=kLoop, calls=%fused_computation.7 | loop fusion | flops 3145728 | bytes 6291456 | tf_op jit(solution)/shard_map/convert_element_type | solution.py:893
  8.1 47.6 %gather_first.1 = (bf16[8,128,768]{2,1,0:T(8,128)(2,1)}, bf16[4,8,24,2432]{3,2,1,0:T(8,128)(2,1)}, bf16[4,24,768]{2,1,0:T(8,128)(2,1)}, bf16[4,24,3072]{2,1,0:T(8,128)(2,1)}, bf16[4,96,768]{2,1,0:T(8,128)(2,1)}) custom-call(bf16[8,128,768]{2,1,0:T(8,128)(2,1)} %get-tuple-element.75.x, bf16[24,2432]{1,0:T(8,128)(2,1)} %pad_maximum_fusion.1.w, ...), custom_call_target="tpu_custom_call" | custom-call | tf_op jit(solution)/shard_map/gather_first/pallas_call | solution.py:120
  56.9 6.6 %add_convert_fusion.refs_1_.refs_3_.refs_5_ = bf16[1024,1536]{1,0:T(8,128)(2,1)} fusion(bf16[1024,768]{1,0:T(8,128)(2,1)} %bitcast.48, f32[1536]{0:T(1024)S(1)} %concatenate.17, bf16[768,2432]{1,0:T(8,128)(2,1)} %bitcast.41), kind=kOutput, calls=%fused_computation | convolution fusion | flops 2419064832 | bytes 7084032 | tf_op jit(solution)/shard_map/dot_general | solution.py:20
  63.6 1.3 convert_element_type.104
  64.9 1.0 slice_convert_fusion
  68.1 4.4 %add_convert_fusion.4.refs_0_ = bf16[1024,768]{1,0:T(8,128)(2,1)} fusion(bf16[1024,768]{1,0:T(8,128)(2,1)} %bitcast.49, f32[768]{0:T(1024)S(1)} %get-tuple-element.71, bf16[768,2432]{1,0:T(8,128)(2,1)} %bitcast.43), kind=kOutput, calls=%fused_computation.8 | convolution fusion | flops 1209532416 | bytes 4328448 | tf_op jit(solution)/shard_map/dot_general | solution.py:20
  72.8 65.4 %attend.1 = (bf16[1024,768]{1,0:T(8,128)(2,1)S(1)}, f32[1024,768]{1,0:T(8,128)}, f32[6,8,1024]{2,1,0:T(8,128)S(1)}, bf16[4,8,24,768]{3,2,1,0:T(8,128)(2,1)S(1)},...) custom-call(bf16[1024,768]{1,0:T(8,128)(2,1)} %add_convert_fusion.4.refs_0_, ...), custom_call_target="tpu_custom_call" | custom-call | flops 12884901888 | bytes 11010048 | tf_op jit(solution)/shard_map/attend/pallas_call | solution.py:438
  138.2 1.1 copy-done.4
  139.3 1.1 copy-done.5
  141.1 77.7 %middle.1 = (bf16[1024,768]{1,0:T(8,128)(2,1)}, f32[1024,768]{1,0:T(8,128)}, bf16[8,128,768]{2,1,0:T(8,128)(2,1)}, bf16[768,768]{1,0:T(8,128)(2,1)}, bf16[768,30...) custom-call(bf16[1024,768]{1,0:T(8,128)(2,1)} %copy-done.5, bf16[1024,768]{1,0:T(8,128)(2,1)} %bitcast.50, ...), custom_call_target="tpu_custom_call" | custom-call | flops 32614907904 | bytes 52428800 | tf_op jit(solution)/shard_map/middle/pallas_call | solution.py:814
  218.8 96.4 %attend_back.1 = (bf16[1024,768]{1,0:T(8,128)(2,1)}, f32[1024,768]{1,0:T(8,128)}, f32[1024,768]{1,0:T(8,128)}, bf16[1024,768]{1,0:T(8,128)(2,1)}, bf16[1024,768]...) custom-call(bf16[1024,768]{1,0:T(8,128)(2,1)} %add_convert_fusion.4.refs_0_,, ...), custom_call_target="tpu_custom_call" | custom-call | flops 32212254720 | bytes 20447232 | tf_op jit(solution)/shard_map/attend_back/pallas_call | solution.py:589
  316.3 1.9 bitcast_convert_fusion.1
  318.3 4.3 %fusion.5 = f32[1024,768]{1,0:T(8,128)} fusion(bf16[1024,768]{1,0:T(8,128)(2,1)S(1)} %copy-done.12, bf16[768,2432]{1,0:T(8,128)(2,1)} %bitcast.44), kind=kOutput, calls=%fused_computation.19 | convolution fusion | flops 1207959552 | bytes 5898240 | tf_op jit(solution)/shard_map/dot_general | solution.py:20
  324.1 3.0 convolution_convert_fusion.2
  327.1 2.0 convert_reduce_fusion
  329.1 4.5 %fusion.1 = f32[1024,768]{1,0:T(8,128)} fusion(bf16[1024,768]{1,0:T(8,128)(2,1)S(1)} %get-tuple-element.73, bf16[768,2432]{1,0:T(8,128)(2,1)} %bitcast.45), kind=kOutput, calls=%fused_computation.15 | convolution fusion | flops 1207959552 | bytes 5898240 | tf_op jit(solution)/shard_map/dot_general | solution.py:20
  333.6 1.5 convolution_convert_fusion
  335.5 3.0 convolution_convert_fusion.1
  338.5 2.1 pad_maximum_fusion
  340.5 4.3 %copy.27 = bf16[768,2304]{1,0:T(8,128)(2,1)S(1)} copy(bf16[768,2304]{0,1:T(8,128)(2,1)} %pad_maximum_fusion) | data formatting | bytes 7077888 | tf_op jit(solution)/shard_map/concatenate | solution.py:956
  344.9 4.3 %fusion.3 = f32[1024,768]{1,0:T(8,128)S(1)} fusion(bf16[768,2432]{1,0:T(8,128)(2,1)} %bitcast.46, f32[1024,768]{1,0:T(8,128)} %get-tuple-element.58, bf16[1024,768]{1,0:T(8,128)(2,1)} %collective-permute-done.1), kind=kOutput, calls=%fused_computation.17 | convolution fusion | flops 1210318848 | bytes 9043968 | tf_op jit(solution)/shard_map/dot_general | solution.py:20
  349.5 2.7 add_convert_fusion.1
  352.2 46.7 %finish_gradients.1 = (f32[24,2304]{1,0:T(8,128)S(1)}, f32[8,768]{1,0:T(8,128)S(1)}, bf16[8,128,768]{2,1,0:T(8,128)(2,1)S(1)}) custom-call(bf16[4,4,2,24,2304]{4,3,2,1,0:T(8,128)(2,1)S(1)} %bitcast.33, f32[8,768]{1,0:T(8,128)S(1)} %select_maximum_fusion.small, bf16[8,128,768]{2,1,0:T(8,128)(2,1)S(1)} %bitcast.34), custom_call_target="tpu_custom_call" | custom-call | tf_op jit(solution)/shard_map/finish_gradients/pallas_call | solution.py:345
  399.7 1.9 bitcast_convert_fusion
  (82 shorter events, 13.4 us)
Async XLA Ops:
  2.2 5.3 %copy-start.19 = (bf16[24,768]{1,0:T(8,128)(2,1)S(1)}, bf16[24,768]{1,0:T(8,128)(2,1)}, u32[]{:S(2)}) copy-start(bf16[24,768]{1,0:T(8,128)(2,1)} %param.16) | copy-start | bytes 110596
  2.2 5.3 %copy-start.20 = (bf16[24,768]{1,0:T(8,128)(2,1)S(1)}, bf16[24,768]{1,0:T(8,128)(2,1)}, u32[]{:S(2)}) copy-start(bf16[24,768]{1,0:T(8,128)(2,1)} %param.15) | copy-start | bytes 110596
  2.2 5.3 %copy-start.21 = (bf16[24,768]{1,0:T(8,128)(2,1)S(1)}, bf16[24,768]{1,0:T(8,128)(2,1)}, u32[]{:S(2)}) copy-start(bf16[24,768]{1,0:T(8,128)(2,1)} %param.14) | copy-start | bytes 110596
  56.8 6.6 %copy-start.18 = (f32[8,768]{1,0:T(8,128)}, f32[8,768]{1,0:T(8,128)S(1)}, u32[]{:S(2)}) copy-start(f32[8,768]{1,0:T(8,128)S(1)} %convert_bitcast_fusion.refs_4_) | copy-start | bytes 73732
  56.8 6.7 %copy-start.9 = (f32[4,256,768]{2,1,0:T(8,128)S(1)}, f32[4,256,768]{2,1,0:T(8,128)}, u32[]{:S(2)}) copy-start(f32[4,256,768]{2,1,0:T(8,128)} %param.12) | copy-start | bytes 9437188
  63.4 9.0 %collective-permute-start = (bf16[1024,1536]{1,0:T(8,128)(2,1)}, bf16[1024,1536]{1,0:T(8,128)(2,1)}, u32[]{:S(2)}, u32[]{:S(2)}) collective-permute-start(bf16[1024,1536]{1,0:T(8,128)(2,1)} %add_convert_fusion.refs_1_.refs_3_.refs_5_), channel_id=1, source_target_pairs={{0,1},{1,0},{2,3},{3,2},{4,5},{5,4},{6,7},{7,6},{8,9},{9,8},{10,11... | collective-permute-start | bytes 9437192 | tf_op jit(solution)/shard_map/ppermute | solution.py:908
  63.6 3.2 copy-start.24
  68.0 4.8 %copy-start.1 = (bf16[4,24,3072]{2,1,0:T(8,128)(2,1)S(1)}, bf16[4,24,3072]{2,1,0:T(8,128)(2,1)}, u32[]{:S(2)}) copy-start(bf16[4,24,3072]{2,1,0:T(8,128)(2,1)} %get-tuple-element.43.refs_7_) | copy-start | bytes 1769476
  68.1 4.8 %copy-start.2 = (bf16[4,96,768]{2,1,0:T(8,128)(2,1)S(1)}, bf16[4,96,768]{2,1,0:T(8,128)(2,1)}, u32[]{:S(2)}) copy-start(bf16[4,96,768]{2,1,0:T(8,128)(2,1)} %get-tuple-element.44.refs_8_) | copy-start | bytes 1769476
  68.1 4.8 %copy-start.3 = (bf16[4,24,768]{2,1,0:T(8,128)(2,1)S(1)}, bf16[4,24,768]{2,1,0:T(8,128)(2,1)}, u32[]{:S(2)}) copy-start(bf16[4,24,768]{2,1,0:T(8,128)(2,1)} %get-tuple-element.42.refs_6_) | copy-start | bytes 442372
  72.8 65.4 %copy-start = (bf16[2,1024,128]{2,1,0:T(8,128)(2,1)}, bf16[2,1024,128]{2,1,0:T(8,128)(2,1)S(1)}, u32[]{:S(2)}) copy-start(bf16[2,1024,128]{2,1,0:T(8,128)(2,1)S(1)} %broadcast_in_dim.20.refs_5_.refs_7_) | copy-start | bytes 1572868
  218.8 97.5 %copy-start.13 = (bf16[8,128,768]{2,1,0:T(8,128)(2,1)S(1)}, bf16[8,128,768]{2,1,0:T(8,128)(2,1)}, u32[]{:S(2)}) copy-start(bf16[8,128,768]{2,1,0:T(8,128)(2,1)} %get-tuple-element.49) | copy-start | bytes 4718596
  315.2 11.9 %collective-permute-start.2 = (bf16[1024,768]{1,0:T(8,128)(2,1)}, bf16[1024,768]{1,0:T(8,128)(2,1)}, u32[]{:S(2)}, u32[]{:S(2)}) collective-permute-start(bf16[1024,768]{1,0:T(8,128)(2,1)} %get-tuple-element.61), channel_id=1, source_target_pairs={{0,1},{1,0},{2,3},{3,2},{4,5},{5,4},{6,7},{7,6},{8,9},{9,8},{10,11... | collective-permute-start | bytes 4718600 | tf_op jit(solution)/shard_map/ppermute | solution.py:945
  316.2 18.9 %collective-permute-start.1 = (bf16[1024,768]{1,0:T(8,128)(2,1)}, bf16[1024,768]{1,0:T(8,128)(2,1)}, u32[]{:S(2)}, u32[]{:S(2)}) collective-permute-start(bf16[1024,768]{1,0:T(8,128)(2,1)} %get-tuple-element.59), channel_id=1, source_target_pairs={{0,1},{1,0},{2,3},{3,2},{4,5},{5,4},{6,7},{7,6},{8,9},{9,8},{10,11... | collective-permute-start | bytes 4718600 | tf_op jit(solution)/shard_map/ppermute | solution.py:944
  316.3 1.9 copy-start.12
  318.3 4.6 %copy-start.22 = (f32[16,768]{1,0:T(8,128)S(1)}, f32[16,768]{1,0:T(8,128)}, u32[]{:S(2)}) copy-start(f32[16,768]{1,0:T(8,128)} %get-tuple-element.67) | copy-start | bytes 147460
  324.1 3.0 copy-start.11
  329.1 4.5 %copy-start.23 = (bf16[8,128,768]{2,1,0:T(8,128)(2,1)S(1)}, bf16[8,128,768]{2,1,0:T(8,128)(2,1)}, u32[]{:S(2)}) copy-start(bf16[8,128,768]{2,1,0:T(8,128)(2,1)} %get-tuple-element.40) | copy-start | bytes 4718596
  344.9 4.3 %copy-start.7 = (f32[1024,768]{1,0:T(8,128)S(1)}, f32[1024,768]{1,0:T(8,128)}, u32[]{:S(2)}) copy-start(f32[1024,768]{1,0:T(8,128)} %get-tuple-element.62) | copy-start | bytes 9437188
  344.9 4.6 %copy-start.8 = (f32[1024,768]{1,0:T(8,128)S(1)}, f32[1024,768]{1,0:T(8,128)}, u32[]{:S(2)}) copy-start(f32[1024,768]{1,0:T(8,128)} %fusion.5) | copy-start | bytes 9437188
  399.7 1.9 copy-start.16
  399.7 2.6 copy-start.17
  399.7 3.2 copy-start.15
  399.7 4.0 copy-start.14
  (4 other events, 4.8 us)
